TPU v7x, 128 devices: a whole 4x4x4 slice. The times are simulated.
128 devices in a mesh: rep: 16 (over x, y), exp: 8 (over z, core).
Axes of the slice: x: 4, y: 4, z: 4, core: 2. Of those that a mesh axis runs over, the one named last changes fastest.
Arguments:
- hidden: bfloat16 [16384, 4096], P(('rep', 'exp')), may hold values from -6 to 6
- parents: int32 [16384], P(('rep', 'exp')), may hold values from 0 to 1023
- routes: int32 [16384, 8], P(('rep', 'exp')), may hold values from 0 to 127, all different within a row; in each aligned block of 128 rows (0 to 127, 128 to 255, ...) at most 10 rows name the same one
- gates: float32 [16384, 8], P(('rep', 'exp')), may hold values from 0.05 to 1
- counts: int32 [128], P(('rep', 'exp')), may hold values from 64 to 128, as said below
- norm_gain: float32 [4096], replicated, may hold values from 0.1 to 1.9
- w_gate: bfloat16 [128, 4096, 768], P(('rep', 'exp')), may hold values from -0.09375 to 0.09375
- w_up: bfloat16 [128, 4096, 768], P(('rep', 'exp')), may hold values from -0.09375 to 0.09375
- w_down: bfloat16 [128, 768, 4096], P(('rep', 'exp')), may hold values from -0.21875 to 0.21875
Outputs:
- mixed: bfloat16 [16384, 4096], P(('rep', 'exp'))
Inputs may be any that keep to these rules, and one draw needn't show every extreme that they name: `routes`: in the rows of one device no expert is named more than 10 times. `counts`: some device has all of its rows live.
All inputs are finite; a program needn't handle non-finite values.
Results may differ from a plain program's by a relative error of at most 0.0071.
Values may be sent and summed in bfloat16 or wider, within the bound.
A program may use at most 128 MiB of HBM per device.

v0:
```python
import jax
import jax.numpy as jnp
from jax import lax
from jax.sharding import PartitionSpec as P


def run_expert(arrived, w_gate, w_up, w_down):
    gate_val = jnp.dot(arrived, w_gate[0], preferred_element_type=jnp.float32)
    up_val = jnp.dot(arrived, w_up[0], preferred_element_type=jnp.float32)
    act = (jax.nn.silu(gate_val) * up_val).astype(jnp.bfloat16)
    return jnp.dot(act, w_down[0], preferred_element_type=jnp.float32).astype(jnp.bfloat16)


def shards(hidden, parents, routes, gates, counts, norm_gain, w_gate, w_up, w_down):
    rows = hidden.shape[0]
    width = hidden.shape[1]
    top = routes.shape[1]
    n_rep = lax.axis_size("rep")
    n_exp = lax.axis_size("exp")
    n_dev = n_rep * n_exp
    cap = rows * top // n_dev + 2
    group = lax.all_gather(hidden, "exp", axis=0, tiled=True)
    picked = jnp.take(group, parents, axis=0).astype(jnp.float32)
    scale = lax.rsqrt(jnp.mean(picked * picked, axis=1, keepdims=True) + 1e-06)
    normed = (picked * scale * norm_gain).astype(jnp.bfloat16)
    live = jnp.arange(rows, dtype=jnp.int32) < counts[0]
    weights = gates / jnp.sum(gates, axis=1, keepdims=True) * live[:, None].astype(jnp.float32)
    flat = routes.reshape(-1)
    live_slot = jnp.repeat(live, top)
    onehot = (
        (flat[:, None] == jnp.arange(n_dev, dtype=jnp.int32)[None, :]) & live_slot[:, None]
    ).astype(jnp.int32)
    before = jnp.cumsum(onehot, axis=0) - onehot
    rank = jnp.sum(before * onehot, axis=1)
    position = jnp.where(live_slot, flat * cap + rank, n_dev * cap)
    row_of_slot = jnp.arange(rows * top, dtype=jnp.int32) // top
    source = jnp.zeros((n_dev * cap,), jnp.int32).at[position].set(row_of_slot, mode="drop")
    filled = jnp.zeros((n_dev * cap,), jnp.bool_).at[position].set(True, mode="drop")
    outgoing = jnp.where(
        filled[:, None], jnp.take(normed, source, axis=0), jnp.zeros((), jnp.bfloat16)
    )
    arrived = lax.all_to_all(outgoing, ("rep", "exp"), split_axis=0, concat_axis=0, tiled=True)
    results = run_expert(arrived, w_gate, w_up, w_down)
    returned = lax.all_to_all(results, ("rep", "exp"), split_axis=0, concat_axis=0, tiled=True)
    safe = jnp.minimum(position, n_dev * cap - 1)
    collected = jnp.take(returned, safe, axis=0).reshape(rows, top, width)
    mixed = jnp.zeros((rows, width), jnp.float32)
    for slot in range(top):
        mixed = mixed + weights[:, slot : slot + 1] * collected[:, slot].astype(jnp.float32)
    return mixed.astype(jnp.bfloat16)


def solution(mesh):
    placed = (
        P(("rep", "exp"), None),
        P(("rep", "exp")),
        P(("rep", "exp"), None),
        P(("rep", "exp"), None),
        P(("rep", "exp")),
        P(),
        P(("rep", "exp"), None, None),
        P(("rep", "exp"), None, None),
        P(("rep", "exp"), None, None),
    )
    return jax.shard_map(
        shards, mesh=mesh, in_specs=placed, out_specs=P(("rep", "exp"), None), check_vma=False
    )
```

profile of v0, /device:TPU:50, one launch (start us, length us, event | category | flops | bytes accessed | tf_op | source)
XLA Modules:
  0.0 686.2 jit_solution(13560979731594647370)
XLA Ops:
  6.5 0.7 all-gather.2.cloned.1.call-update
  8.0 0.1 reshape.171
  8.1 0.1 reshape.173
  8.2 0.8 copy.18
  9.2 0.7 broadcast_multiply_fusion
  9.9 0.1 copy.25
  10.2 0.3 fusion.24
  10.6 0.1 copy.22
  10.8 0.5 fusion.23
  11.3 4.3 scatter_custom_fusion.1
  15.6 0.2 broadcast_in_dim.91
  15.8 4.6 scatter_custom_fusion
  20.5 0.2 broadcast_in_dim.88
  20.7 39.2 %all-gather.2.cloned.1.call-done = bf16[1024,4096]{1,0:T(8,128)(2,1)} async-done(((bf16[128,4096]{1,0:T(8,128)(2,1)}), bf16[1024,4096]{1,0:T(8,128)(2,1)}) %all-gather.2.cloned.1.call-update) | async-done | bytes 8388624 | tf_op jit(solution)/shard_map/all_gather | solution.py:22
  59.9 6.7 gather_fusion
  66.6 0.4 fusion.11
  67.0 0.4 fusion.13
  67.4 8.4 %gather_fusion.1 = bf16[1280,4096]{1,0:T(8,128)(2,1)} fusion(bf16[128,4096]{1,0:T(8,128)(2,1)S(1)} %fusion.13, s32[2048]{0:T(1024)S(1)} %pad_clamp_fusion), kind=kCustom, calls=%fused_computation.1 | custom fusion | bytes 20976640 | tf_op jit(solution)/shard_map/jit(_take)/gather | solution.py:40
  75.8 15.2 %gather.18 = bf16[128,10,4096]{2,1,0:T(8,128)(2,1)} reshape(bf16[1280,4096]{1,0:T(8,128)(2,1)} %gather_fusion.1) | data formatting | bytes 20971520 | tf_op jit(solution)/shard_map/jit(_take)/gather | solution.py:40
  91.0 8.8 %select_select_fusion = bf16[128,10,4096]{2,1,0:T(8,128)(2,1)S(1)} fusion(bf16[128,10,4096]{2,1,0:T(8,128)(2,1)} %gather.18, pred[128,10]{1,0:T(8,128)(4,1)S(1)} %broadcast_in_dim.91, pred[128,10]{1,0:T(8,128)(4,1)S(1)} %broadcast_in_dim.88), kind=kLoop, calls=%fused_computation.5 | loop fusion | flops 10485760 | bytes 20974080 | tf_op jit(solution)/shard_map/jit(_where)/select_n | solution.py:39
  99.8 200.7 %all_to_all.21 = bf16[128,10,4096]{2,1,0:T(8,128)(2,1)} all-to-all(bf16[128,10,4096]{2,1,0:T(8,128)(2,1)S(1)} %select_select_fusion), channel_id=1, replica_groups=mesh['rep'=16,'exp'=8] {'rep','exp'}, dimensions={0} | all-to-all | bytes 20971520 | tf_op jit(solution)/shard_map/all_to_all | solution.py:42
  300.5 16.7 %all_to_all.15 = bf16[1280,4096]{1,0:T(8,128)(2,1)} reshape(bf16[128,10,4096]{2,1,0:T(8,128)(2,1)} %all_to_all.21) | data formatting | bytes 20971520 | tf_op jit(solution)/shard_map/all_to_all | solution.py:42
  317.2 12.3 %fusion.3 = f32[1280,768]{1,0:T(8,128)S(1)} fusion(bf16[1280,4096]{1,0:T(8,128)(2,1)} %all_to_all.15, bf16[1,4096,768]{2,1,0:T(8,128)(2,1)} %param.15), kind=kOutput, calls=%fused_computation.11 | convolution fusion | flops 8053063680 | bytes 20709376 | tf_op jit(solution)/shard_map/dot_general | solution.py:8
  329.5 9.0 %fusion.8 = bf16[1280,768]{1,0:T(8,128)(2,1)S(1)} fusion(bf16[1280,4096]{1,0:T(8,128)(2,1)S(1)} %copy-done, bf16[1,4096,768]{2,1,0:T(8,128)(2,1)S(1)} %bitcast.99, f32[1280,768]{1,0:T(8,128)S(1)} %fusion.3), kind=kOutput, calls=%fused_computation.14 | convolution fusion | flops 8058961920 | bytes 22675456 | tf_op jit(solution)/shard_map/dot_general | solution.py:9
  338.5 13.7 %convolution_convert_fusion = bf16[1280,4096]{1,0:T(8,128)(2,1)} fusion(bf16[1280,768]{1,0:T(8,128)(2,1)S(1)} %fusion.8, bf16[1,768,4096]{2,1,0:T(8,128)(2,1)} %param.17), kind=kOutput, calls=%fused_computation.6 | convolution fusion | flops 8058306560 | bytes 18743296 | tf_op jit(solution)/shard_map/dot_general | solution.py:11
  352.2 15.2 %all_to_all.16 = bf16[128,10,4096]{2,1,0:T(8,128)(2,1)} reshape(bf16[1280,4096]{1,0:T(8,128)(2,1)} %convolution_convert_fusion) | data formatting | bytes 20971520 | tf_op jit(solution)/shard_map/all_to_all | solution.py:44
  367.4 11.2 %all-to-all-start.1 = ((bf16[128,10,4096]{2,1,0:T(8,128)(2,1)}), bf16[128,10,4096]{2,1,0:T(8,128)(2,1)}, u32[]{:S(2)}, u32[]{:S(2)}) async-start(bf16[128,10,4096]{2,1,0:T(8,128)(2,1)} %all_to_all.16), calls=%async_computation.1 | async-start | bytes 33554432 | tf_op jit(solution)/shard_map/all_to_all | solution.py:44
  378.8 241.6 %all-to-all-done.1 = bf16[128,10,4096]{2,1,0:T(8,128)(2,1)} async-done(((bf16[128,10,4096]{2,1,0:T(8,128)(2,1)}), bf16[128,10,4096]{2,1,0:T(8,128)(2,1)}, u32[]{:S(2)}, u32[]{:S(2)}) %all-to-all-start.1) | async-done | bytes 10485792 | tf_op jit(solution)/shard_map/all_to_all | solution.py:44
  620.4 16.5 %all_to_all.18 = bf16[1280,4096]{1,0:T(8,128)(2,1)} reshape(bf16[128,10,4096]{2,1,0:T(8,128)(2,1)} %all-to-all-done.1) | data formatting | bytes 20971520 | tf_op jit(solution)/shard_map/all_to_all | solution.py:44
  637.0 20.6 %gather_fusion.2 = bf16[1024,4096]{1,0:T(8,128)(2,1)} fusion(bf16[1280,4096]{1,0:T(8,128)(2,1)} %all_to_all.18, s32[1024]{0:T(1024)S(1)} %broadcast_clamp_fusion), kind=kCustom, calls=%fused_computation.2 | custom fusion | bytes 16781312 | tf_op jit(solution)/shard_map/jit(_take)/gather | solution.py:46
  657.5 16.3 %copy_select_fusion = bf16[128,8,4096]{2,0,1:T(8,128)(2,1)} fusion(bf16[128,8,4096]{2,1,0:T(8,128)(2,1)} %bitcast.93, pred[128,8]{0,1:T(8,128)(4,1)S(1)} %compare_and_fusion.1), kind=kLoop, calls=%fused_computation.7 | loop fusion | flops 4194304 | bytes 16778240 | tf_op jit(solution)/shard_map/jit(_take)/select_n | solution.py:46
  673.9 5.3 fusion.15
  (45 shorter events, 0.9 us)
Async XLA Ops:
  6.5 14.1 %copy-start.4 = (s32[128]{0:T(128)S(1)}, s32[128]{0:T(128)}, u32[]{:S(2)}) copy-start(s32[128]{0:T(128)} %param.10) | copy-start | bytes 1540
  6.5 53.4 %all-gather.2.cloned.1.call-start = ((), (), s32[]{:S(2)}) async-start(), calls=%async_computation.2 | async-start | bytes 9437184 | tf_op jit(solution)/shard_map/all_gather | solution.py:22
  20.7 46.3 %copy-start.2 = (f32[4096]{0:T(1024)S(1)}, f32[4096]{0:T(1024)}, u32[]{:S(2)}) copy-start(f32[4096]{0:T(1024)} %param.14) | copy-start | bytes 49156
  300.5 29.0 %slice-start = ((s8[6291456]{0:T(1024)(128)(4,1)}), s8[2097152]{0:T(1024)(128)(4,1)S(1)}, s32[]{:S(2)}) async-start(s8[6291456]{0:T(1024)(128)(4,1)} %bitcast.98), calls=%async_computation.3 | async-start | bytes 4194304
  317.2 12.3 %copy-start = (bf16[1280,4096]{1,0:T(8,128)(2,1)S(1)}, bf16[1280,4096]{1,0:T(8,128)(2,1)}, u32[]{:S(2)}) copy-start(bf16[1280,4096]{1,0:T(8,128)(2,1)} %all_to_all.15) | copy-start | bytes 31457284
  317.2 12.3 %slice-start.1 = ((s8[6291456]{0:T(1024)(128)(4,1)}), s8[4194304]{0:T(1024)(128)(4,1)S(1)}, s32[]{:S(2)}) async-start(s8[6291456]{0:T(1024)(128)(4,1)} %bitcast.98), calls=%async_computation.4 | async-start | bytes 8388608
  367.3 11.4 %copy-start.3 = (f32[128,8]{0,1:T(8,128)S(1)}, f32[128,8]{0,1:T(8,128)}, u32[]{:S(2)}) copy-start(f32[128,8]{0,1:T(8,128)} %param.12) | copy-start | bytes 12292
  367.3 11.4 %copy-start.1 = (s32[128,8]{0,1:T(8,128)S(1)}, s32[128,8]{0,1:T(8,128)}, u32[]{:S(2)}) copy-start(s32[128,8]{0,1:T(8,128)} %param.11) | copy-start | bytes 12292
  367.4 253.1 %all-to-all-start.1 = ((bf16[128,10,4096]{2,1,0:T(8,128)(2,1)}), bf16[128,10,4096]{2,1,0:T(8,128)(2,1)}, u32[]{:S(2)}, u32[]{:S(2)}) async-start(bf16[128,10,4096]{2,1,0:T(8,128)(2,1)} %all_to_all.16), calls=%async_computation.1 | async-start | bytes 33554432 | tf_op jit(solution)/shard_map/all_to_all | solution.py:44
Sparse Core Ops, SparseCore 0:
  9.1 50.7 all-gather.1
where the time goes:
time: 693 us; the launch traced here: 686 us
  waiting for transfers between devices  282 us (41%)
  blocking collectives  201 us (29%)
  local copies, waits for them, and re-layouts  110 us (16%)
  matrix products  34.9 us (5%)
  other arithmetic  33 us (5%)
  between operations  14.6 us (2%)
  starting transfers between devices  11.2 us (2%)
    all_to_all x1, waiting for transfers between devices, shards(): lax.all_to_all(results, ('rep', 'exp'), split_axis=0, concat_axis=0, tile...  242 us
    all_to_all x1, blocking collectives, shards(): lax.all_to_all(outgoing, ('rep', 'exp'), split_axis=0, concat_axis=0, til...  201 us
    all_gather x1, waiting for transfers between devices, shards(): group = lax.all_gather(hidden, 'exp', axis=0, tiled=True)  39.2 us
    all_to_all x2, local copies, waits for them, and re-layouts, shards(): lax.all_to_all(results, ('rep', 'exp'), split_axis=0, concat_axis=0, tile...  31.7 us
    gather x2, local copies, waits for them, and re-layouts, shards(): jnp.take(normed, source, axis=0)  23.6 us
    gather x1, local copies, waits for them, and re-layouts, shards(): collected = jnp.take(returned, safe, axis=0).reshape(rows, top, width)  20.6 us
    all_to_all x1, local copies, waits for them, and re-layouts, shards(): lax.all_to_all(outgoing, ('rep', 'exp'), split_axis=0, concat_axis=0, til...  16.7 us
    select_n x2, other arithmetic, shards(): collected = jnp.take(returned, safe, axis=0).reshape(rows, top, width)  16.4 us
  transfers between devices with their start and end apart: 2, of which 2 were waited for; matrix products, arithmetic and copies ran while one was open for 2% of the time, Pallas kernels for 0%

commit v1 on v0

--- a/solution.py
+++ b/solution.py
@@ -1,7 +1,59 @@
 import jax
 import jax.numpy as jnp
 from jax import lax
+from jax.experimental import pallas as pl
+from jax.experimental.pallas import tpu as pltpu
 from jax.sharding import PartitionSpec as P
+import functools
+
+MESH = pl.DeviceIdType.MESH
+
+
+def exchange_kernel(n_rep, n_exp, x_ref, o_ref, send_sem, recv_sem, local_sem):
+    n = n_rep * n_exp
+    me = lax.axis_index("rep") * n_exp + lax.axis_index("exp")
+    barrier = pltpu.get_barrier_semaphore()
+
+    def greet(s, carry):
+        d = lax.rem(me + s, n)
+        pl.semaphore_signal(barrier, inc=1, device_id=(d // n_exp, d % n_exp), device_id_type=MESH)
+        return carry
+
+    lax.fori_loop(1, n, greet, 0)
+    pl.semaphore_wait(barrier, n - 1)
+    own = pltpu.make_async_copy(x_ref.at[me], o_ref.at[me], local_sem)
+    own.start()
+
+    def send(s, carry):
+        d = lax.rem(me + s, n)
+        pltpu.make_async_remote_copy(
+            src_ref=x_ref.at[d], dst_ref=o_ref.at[me], send_sem=send_sem, recv_sem=recv_sem,
+            device_id=(d // n_exp, d % n_exp), device_id_type=MESH,
+        ).start()
+        return carry
+
+    lax.fori_loop(1, n, send, 0)
+    own.wait()
+    whole = pltpu.make_async_remote_copy(
+        src_ref=x_ref.at[pl.ds(0, n - 1)], dst_ref=o_ref.at[pl.ds(0, n - 1)], send_sem=send_sem,
+        recv_sem=recv_sem, device_id=(0, 0), device_id_type=MESH,
+    )
+    whole.wait_send()
+    whole.wait_recv()
+
+
+def exchange(x, ident):
+    n_rep = lax.axis_size("rep")
+    n_exp = lax.axis_size("exp")
+    return pl.pallas_call(
+        functools.partial(exchange_kernel, n_rep, n_exp),
+        out_shape=jax.ShapeDtypeStruct(x.shape, x.dtype),
+        in_specs=[pl.BlockSpec(memory_space=pl.ANY)],
+        out_specs=pl.BlockSpec(memory_space=pl.ANY),
+        scratch_shapes=[pltpu.SemaphoreType.DMA, pltpu.SemaphoreType.DMA, pltpu.SemaphoreType.DMA],
+        compiler_params=pltpu.CompilerParams(collective_id=ident, has_side_effects=True),
+        name=f"exchange{ident}",
+    )(x)
 
 
 def run_expert(arrived, w_gate, w_up, w_down):
@@ -39,9 +91,9 @@
     outgoing = jnp.where(
         filled[:, None], jnp.take(normed, source, axis=0), jnp.zeros((), jnp.bfloat16)
     )
-    arrived = lax.all_to_all(outgoing, ("rep", "exp"), split_axis=0, concat_axis=0, tiled=True)
+    arrived = exchange(outgoing.reshape(n_dev, cap, width), 0).reshape(n_dev * cap, width)
     results = run_expert(arrived, w_gate, w_up, w_down)
-    returned = lax.all_to_all(results, ("rep", "exp"), split_axis=0, concat_axis=0, tiled=True)
+    returned = exchange(results.reshape(n_dev, cap, width), 1).reshape(n_dev * cap, width)
     safe = jnp.minimum(position, n_dev * cap - 1)
     collected = jnp.take(returned, safe, axis=0).reshape(rows, top, width)
     mixed = jnp.zeros((rows, width), jnp.float32)

time: 693 us -> 1310 us (1.89)
  the two profiles are of different devices: /device:TPU:50 before, /device:TPU:125 now
where the time goes in v1:
time: 1310 us
  Pallas kernels  1070 us (82%)
  local copies, waits for them, and re-layouts  111 us (8%)
  other arithmetic  39.1 us (3%)
  waiting for transfers between devices  36.8 us (3%)
  matrix products  34.9 us (3%)
  between operations  14.7 us (1%)
    pallas_call x2, Pallas kernels, exchange(): pl.pallas_call(functools.partial(exchange_kernel, n_rep, n_exp), out_shap...  1070 us
    all_gather x1, waiting for transfers between devices, shards(): group = lax.all_gather(hidden, 'exp', axis=0, tiled=True)  36 us
  transfers between devices with their start and end apart: 1, of which 1 were waited for; matrix products, arithmetic and copies ran while one was open for 1% of the time, Pallas kernels for 0%

profile of v1, /device:TPU:125, one launch (start us, length us, event | category | flops | bytes accessed | tf_op | source)
XLA Modules:
  0.0 1306.1 jit_solution(3812034187588169246)
XLA Ops:
  6.5 0.7 all-gather.2.cloned.1.call-update
  8.0 0.1 reshape.177
  8.1 0.1 reshape.179
  8.2 0.8 copy.18
  9.2 0.7 broadcast_multiply_fusion
  9.9 0.1 copy.25
  10.2 0.3 fusion.24
  10.8 0.5 fusion.23
  11.4 4.3 scatter_custom_fusion.1
  15.7 0.2 broadcast_in_dim.91
  15.9 4.8 scatter_custom_fusion
  20.7 0.2 broadcast_in_dim.88
  21.1 0.6 slice_bitcast_fusion.16
  21.6 0.6 compare_and_fusion.1
  22.2 36.0 %all-gather.2.cloned.1.call-done = bf16[1024,4096]{1,0:T(8,128)(2,1)} async-done(((bf16[128,4096]{1,0:T(8,128)(2,1)}), bf16[1024,4096]{1,0:T(8,128)(2,1)}) %all-gather.2.cloned.1.call-update) | async-done | bytes 8388624 | tf_op jit(solution)/shard_map/all_gather | solution.py:74
  58.3 6.7 gather_fusion
  64.9 0.4 fusion.11
  65.4 0.4 fusion.13
  65.8 8.3 gather_fusion.1
  74.1 15.2 %gather.18 = bf16[128,10,4096]{2,1,0:T(8,128)(2,1)} reshape(bf16[1280,4096]{1,0:T(8,128)(2,1)} %gather_fusion.1) | data formatting | bytes 20971520 | tf_op jit(solution)/shard_map/jit(_take)/gather | solution.py:92
  89.3 14.4 %select_select_fusion.x_ref = bf16[128,10,4096]{2,1,0:T(8,128)(2,1)} fusion(bf16[128,10,4096]{2,1,0:T(8,128)(2,1)} %gather.18, pred[128,10]{1,0:T(8,128)(4,1)S(1)} %broadcast_in_dim.91, pred[128,10]{1,0:T(8,128)(4,1)S(1)} %broadcast_in_dim.88), kind=kLoop, calls=%fused_computation.5 | loop fusion | flops 10485760 | bytes 20974080 | tf_op jit(solution)/shard_map/jit(_where)/select_n | solution.py:91
  103.7 549.3 %exchange0.1 = bf16[128,10,4096]{2,1,0:T(8,128)(2,1)} custom-call(bf16[128,10,4096]{2,1,0:T(8,128)(2,1)} %select_select_fusion.x_ref), custom_call_target="tpu_custom_call" | custom-call | tf_op jit(solution)/shard_map/exchange0/pallas_call | solution.py:48
  653.0 16.7 %reshape.180 = bf16[1280,4096]{1,0:T(8,128)(2,1)} reshape(bf16[128,10,4096]{2,1,0:T(8,128)(2,1)} %exchange0.1) | data formatting | bytes 20971520 | tf_op jit(solution)/shard_map/reshape | solution.py:94
  669.7 12.4 fusion.3
  682.2 9.0 fusion.8
  691.2 13.5 %convolution_convert_fusion = bf16[1280,4096]{1,0:T(8,128)(2,1)} fusion(bf16[1280,768]{1,0:T(8,128)(2,1)S(1)} %fusion.8, bf16[1,768,4096]{2,1,0:T(8,128)(2,1)} %param.17), kind=kOutput, calls=%fused_computation.6 | convolution fusion | flops 8058306560 | bytes 18743296 | tf_op jit(solution)/shard_map/dot_general | solution.py:63
  704.7 15.5 %reshape.181.x_ref = bf16[128,10,4096]{2,1,0:T(8,128)(2,1)} reshape(bf16[1280,4096]{1,0:T(8,128)(2,1)} %convolution_convert_fusion) | data formatting | bytes 20971520 | tf_op jit(solution)/shard_map/reshape | solution.py:96
  720.2 519.9 %exchange1.1 = bf16[128,10,4096]{2,1,0:T(8,128)(2,1)} custom-call(bf16[128,10,4096]{2,1,0:T(8,128)(2,1)} %reshape.181.x_ref), custom_call_target="tpu_custom_call" | custom-call | tf_op jit(solution)/shard_map/exchange1/pallas_call | solution.py:48
  1240.1 16.5 %reshape.182 = bf16[1280,4096]{1,0:T(8,128)(2,1)} reshape(bf16[128,10,4096]{2,1,0:T(8,128)(2,1)} %exchange1.1) | data formatting | bytes 20971520 | tf_op jit(solution)/shard_map/reshape | solution.py:96
  1256.6 20.6 %gather_fusion.2 = bf16[1024,4096]{1,0:T(8,128)(2,1)} fusion(bf16[1280,4096]{1,0:T(8,128)(2,1)} %reshape.182, s32[1024]{0:T(1024)S(1)} %broadcast_clamp_fusion), kind=kCustom, calls=%fused_computation.2 | custom fusion | bytes 16781312 | tf_op jit(solution)/shard_map/jit(_take)/gather | solution.py:98
  1277.4 16.4 %copy_select_fusion = bf16[128,8,4096]{2,0,1:T(8,128)(2,1)} fusion(bf16[128,8,4096]{2,1,0:T(8,128)(2,1)} %bitcast.93, pred[128,8]{0,1:T(8,128)(4,1)S(1)} %copy-done.4), kind=kLoop, calls=%fused_computation.7 | loop fusion | flops 4194304 | bytes 16778240 | tf_op jit(solution)/shard_map/jit(_take)/select_n | solution.py:98
  1293.8 5.3 fusion.15
  (62 shorter events, 1.0 us)
Async XLA Ops:
  6.5 15.1 %copy-start.1 = (s32[128,8]{0,1:T(8,128)S(1)}, s32[128,8]{0,1:T(8,128)}, u32[]{:S(2)}) copy-start(s32[128,8]{0,1:T(8,128)} %param.11) | copy-start | bytes 12292
  6.5 14.4 %copy-start.3 = (f32[128,8]{0,1:T(8,128)S(1)}, f32[128,8]{0,1:T(8,128)}, u32[]{:S(2)}) copy-start(f32[128,8]{0,1:T(8,128)} %param.12) | copy-start | bytes 12292
  6.5 14.4 %copy-start.13 = (s32[128]{0:T(128)S(1)}, s32[128]{0:T(128)}, u32[]{:S(2)}) copy-start(s32[128]{0:T(128)} %param.10) | copy-start | bytes 1540
  6.5 51.7 %all-gather.2.cloned.1.call-start = ((), (), s32[]{:S(2)}) async-start(), calls=%async_computation | async-start | bytes 9437184 | tf_op jit(solution)/shard_map/all_gather | solution.py:74
  22.2 43.2 %copy-start.2 = (f32[4096]{0:T(1024)S(1)}, f32[4096]{0:T(1024)}, u32[]{:S(2)}) copy-start(f32[4096]{0:T(1024)} %param.14) | copy-start | bytes 49156
  653.0 29.1 %slice-start = ((s8[6291456]{0:T(1024)(128)(4,1)}), s8[2097152]{0:T(1024)(128)(4,1)S(1)}, s32[]{:S(2)}) async-start(s8[6291456]{0:T(1024)(128)(4,1)} %bitcast.98), calls=%async_computation.1 | async-start | bytes 4194304
  669.7 12.5 copy-start
  669.7 12.5 slice-start.1
  1256.6 20.7 %copy-start.4 = (pred[128,8]{0,1:T(8,128)(4,1)S(1)}, pred[128,8]{0,1:T(8,128)(4,1)}, u32[]{:S(2)}) copy-start(pred[128,8]{0,1:T(8,128)(4,1)} %compare_and_fusion.1) | copy-start | bytes 3076
  1277.3 16.4 %copy-start.5 = (f32[128]{0:T(128)S(1)}, f32[128]{0:T(128)}, u32[]{:S(2)}) copy-start(f32[128]{0:T(128)} %get-tuple-element.7) | copy-start | bytes 1540
  1277.3 16.4 %copy-start.6 = (f32[128]{0:T(128)S(1)}, f32[128]{0:T(128)}, u32[]{:S(2)}) copy-start(f32[128]{0:T(128)} %get-tuple-element.8) | copy-start | bytes 1540
  1277.3 16.4 %copy-start.7 = (f32[128]{0:T(128)S(1)}, f32[128]{0:T(128)}, u32[]{:S(2)}) copy-start(f32[128]{0:T(128)} %get-tuple-element.9) | copy-start | bytes 1540
  1277.3 16.4 %copy-start.8 = (f32[128]{0:T(128)S(1)}, f32[128]{0:T(128)}, u32[]{:S(2)}) copy-start(f32[128]{0:T(128)} %get-tuple-element.10) | copy-start | bytes 1540
  1277.3 16.4 %copy-start.9 = (f32[128]{0:T(128)S(1)}, f32[128]{0:T(128)}, u32[]{:S(2)}) copy-start(f32[128]{0:T(128)} %get-tuple-element.11) | copy-start | bytes 1540
  1277.4 16.4 %copy-start.10 = (f32[128]{0:T(128)S(1)}, f32[128]{0:T(128)}, u32[]{:S(2)}) copy-start(f32[128]{0:T(128)} %get-tuple-element.12) | copy-start | bytes 1540
  1277.4 16.4 %copy-start.11 = (f32[128]{0:T(128)S(1)}, f32[128]{0:T(128)}, u32[]{:S(2)}) copy-start(f32[128]{0:T(128)} %get-tuple-element.13) | copy-start | bytes 1540
  1277.4 16.4 %copy-start.12 = (f32[128]{0:T(128)S(1)}, f32[128]{0:T(128)}, u32[]{:S(2)}) copy-start(f32[128]{0:T(128)} %get-tuple-element.14) | copy-start | bytes 1540
Sparse Core Ops, SparseCore 0:
  9.1 49.1 all-gather.1

commit v2 on v0

v2 whole, which is shorter than its diff:
```python
import jax
import jax.numpy as jnp
from jax import lax
from jax.sharding import PartitionSpec as P


def run_expert(arrived, w_gate, w_up, w_down):
    gate_val = jnp.dot(arrived, w_gate[0], preferred_element_type=jnp.float32)
    up_val = jnp.dot(arrived, w_up[0], preferred_element_type=jnp.float32)
    act = (jax.nn.silu(gate_val) * up_val).astype(jnp.bfloat16)
    return jnp.dot(act, w_down[0], preferred_element_type=jnp.float32).astype(jnp.bfloat16)


def shards(hidden, parents, routes, gates, counts, norm_gain, w_gate, w_up, w_down):
    rows = hidden.shape[0]
    width = hidden.shape[1]
    top = routes.shape[1]
    n_rep = lax.axis_size("rep")
    n_exp = lax.axis_size("exp")
    n_dev = n_rep * n_exp
    cap = rows * top // n_dev + 2
    column = lax.axis_index("exp")
    micro = rows * n_exp
    per_expert = cap * n_exp
    slots = n_rep * per_expert

    live = jnp.arange(rows, dtype=jnp.int32) < counts[0]
    weights = gates / jnp.sum(gates, axis=1, keepdims=True) * live[:, None].astype(jnp.float32)
    flat = routes.reshape(-1)
    live_slot = jnp.repeat(live, top)
    onehot = (
        (flat[:, None] == jnp.arange(n_dev, dtype=jnp.int32)[None, :]) & live_slot[:, None]
    ).astype(jnp.int32)
    before = jnp.cumsum(onehot, axis=0) - onehot
    rank = jnp.sum(before * onehot, axis=1)
    code = jnp.where(live_slot, flat, -1)
    ints = jnp.concatenate(
        [code.reshape(rows, top), rank.reshape(rows, top), parents[:, None]], axis=1
    )

    group = lax.all_gather(hidden, "exp", axis=0, tiled=True)
    ints_all = lax.all_gather(ints, "exp", axis=0, tiled=True)
    w_all = lax.all_gather(weights, "exp", axis=0, tiled=True)

    code_all = ints_all[:, :top]
    rank_all = ints_all[:, top : 2 * top]
    parent_all = ints_all[:, 2 * top]
    mine = (code_all >= 0) & (code_all % n_exp == column)
    owner = (jnp.arange(micro, dtype=jnp.int32) // rows)[:, None]
    dest = (code_all // n_exp) * per_expert + owner * cap + rank_all
    dest = jnp.where(mine, dest, slots).reshape(-1)
    row_id = jnp.broadcast_to(jnp.arange(micro, dtype=jnp.int32)[:, None], (micro, top)).reshape(-1)
    src_row = jnp.zeros((slots,), jnp.int32).at[dest].set(row_id, mode="drop")
    filled = jnp.zeros((slots,), jnp.bool_).at[dest].set(True, mode="drop")
    slot_w = jnp.zeros((slots,), jnp.float32).at[dest].set(w_all.reshape(-1), mode="drop")

    picked = jnp.take(group, jnp.take(parent_all, src_row), axis=0).astype(jnp.float32)
    scale = lax.rsqrt(jnp.mean(picked * picked, axis=1, keepdims=True) + 1e-06)
    normed = (picked * scale * norm_gain).astype(jnp.bfloat16)
    outgoing = jnp.where(filled[:, None], normed, jnp.zeros((), jnp.bfloat16))

    arrived = lax.all_to_all(outgoing, "rep", split_axis=0, concat_axis=0, tiled=True)
    results = run_expert(arrived, w_gate, w_up, w_down)
    returned = lax.all_to_all(results, "rep", split_axis=0, concat_axis=0, tiled=True)

    contrib = slot_w[:, None] * returned.astype(jnp.float32)
    target = jnp.where(filled, src_row, micro)
    partial = jnp.zeros((micro, width), jnp.float32).at[target].add(contrib, mode="drop")
    mixed = lax.psum_scatter(partial.astype(jnp.bfloat16), "exp", scatter_dimension=0, tiled=True)
    return mixed


def solution(mesh):
    placed = (
        P(("rep", "exp"), None),
        P(("rep", "exp")),
        P(("rep", "exp"), None),
        P(("rep", "exp"), None),
        P(("rep", "exp")),
        P(),
        P(("rep", "exp"), None, None),
        P(("rep", "exp"), None, None),
        P(("rep", "exp"), None, None),
    )
    return jax.shard_map(
        shards, mesh=mesh, in_specs=placed, out_specs=P(("rep", "exp"), None), check_vma=False
    )
```

time: 693 us -> 597 us (0.86)
  waiting for transfers between devices: 282 us -> 185 us
  blocking collectives: 201 us -> 149 us
  other arithmetic: 33 us -> 70.3 us
  local copies, waits for them, and re-layouts: 110 us -> 127 us
    all_to_all x1, waiting for transfers between devices: 242 us -> 89.5 us  [shards(): lax.all_to_all(results, 'rep', split_axis=0, concat_axis=0, tiled=True)]
    reduce_scatter x0 -> x1, waiting for transfers between devices: none -> 94.7 us  [shards(): lax.psum_scatter(partial.astype(jnp.bfloat16), 'exp', scatter_dimension=0...]
    scatter x2 -> x3, local copies, waits for them, and re-layouts: 8.95 us -> 95.9 us  [the longest x1 34.6 us: shards(): filled = jnp.zeros((slots,), jnp.bool_).at[dest].set(True, mode='drop')]
    all_to_all x1, blocking collectives: 201 us -> 123 us  [shards(): lax.all_to_all(outgoing, 'rep', split_axis=0, concat_axis=0, tiled=True)]
    all_to_all x3 -> x0, local copies, waits for them, and re-layouts: 48.4 us -> none  [the longest x2 31.7 us: shards(): lax.all_to_all(results, ('rep', 'exp'), split_axis=0, concat_axis=0, tile...]
    scatter-add x0 -> x1, other arithmetic: none -> 42.9 us  [shards(): jnp.zeros((micro, width), jnp.float32).at[target].add(contrib, mode='drop')]
    all_gather x1, waiting for transfers between devices: 39.2 us -> 0.02 us  [shards(): group = lax.all_gather(hidden, 'exp', axis=0, tiled=True)]
    all_gather x0 -> x2, blocking collectives: none -> 26.4 us  [the longest x1 13.6 us: shards(): ints_all = lax.all_gather(ints, 'exp', axis=0, tiled=True)]
  transfers between devices with their start and end apart: 2 -> 3, of which waited for: 2 -> 2; matrix products, arithmetic and copies ran while one was open for 2% -> 18% of each run, Pallas kernels for 0% -> 0%
where the time goes in v2:
time: 597 us; the launch traced here: 587 us
  waiting for transfers between devices  185 us (31%)
  blocking collectives  149 us (25%)
  local copies, waits for them, and re-layouts  127 us (21%)
  other arithmetic  70.3 us (12%)
  matrix products  32.8 us (5%)
  between operations  14.6 us (2%)
  starting transfers between devices  8.33 us (1%)
    all_to_all x1, blocking collectives, shards(): lax.all_to_all(outgoing, 'rep', split_axis=0, concat_axis=0, tiled=True)  123 us
    reduce_scatter x1, waiting for transfers between devices, shards(): lax.psum_scatter(partial.astype(jnp.bfloat16), 'exp', scatter_dimension=0...  94.7 us
    all_to_all x1, waiting for transfers between devices, shards(): lax.all_to_all(results, 'rep', split_axis=0, concat_axis=0, tiled=True)  89.5 us
    scatter-add x1, other arithmetic, shards(): jnp.zeros((micro, width), jnp.float32).at[target].add(contrib, mode='drop')  42.9 us
    scatter x1, local copies, waits for them, and re-layouts, shards(): filled = jnp.zeros((slots,), jnp.bool_).at[dest].set(True, mode='drop')  34.6 us
    scatter x1, local copies, waits for them, and re-layouts, shards(): src_row = jnp.zeros((slots,), jnp.int32).at[dest].set(row_id, mode='drop')  30.9 us
    scatter x1, local copies, waits for them, and re-layouts, shards(): jnp.zeros((slots,), jnp.float32).at[dest]  30.4 us
    gather x1, local copies, waits for them, and re-layouts, shards(): jnp.take(group, jnp.take(parent_all, src_row), axis=0).astype(jnp.float32)  23.2 us
  transfers between devices with their start and end apart: 3, of which 2 were waited for; matrix products, arithmetic and copies ran while one was open for 18% of the time, Pallas kernels for 0%

profile of v2, /device:TPU:50, one launch (start us, length us, event | category | flops | bytes accessed | tf_op | source)
XLA Modules:
  0.0 587.2 jit_solution(2126128571061677138)
XLA Ops:
  6.5 0.7 all-gather.2.cloned.1.call-update
  7.3 0.8 copy.28
  9.0 0.1 and.55
  9.1 0.1 copy.31
  9.2 0.3 fusion.17
  9.7 0.1 copy.32
  9.8 0.5 fusion.16
  10.4 0.7 broadcast_select_fusion
  11.1 0.7 pad_add_fusion
  11.8 13.6 %all_gather.9 = s32[1024,17]{0,1:T(8,128)S(1)} all-gather(s32[128,17]{0,1:T(8,128)S(1)} %pad_add_fusion), channel_id=1, replica_groups=mesh['rep'=16,'exp'=8] {'exp'}, dimensions={0}, use_global_device_ids=true | all-gather | bytes 78336 | tf_op jit(solution)/shard_map/all_gather | solution.py:42
  25.5 0.2 copy.34
  25.7 0.3 reshape.150
  26.1 34.6 %scatter_custom_fusion = pred[1280]{0:T(1024)(128)(4,1)S(1)} fusion(s32[8192]{0:T(1024)S(1)} %bitcast.48, pred[8192]{0:T(1024)(128)(4,1)S(1)} %broadcast.149, pred[]{:T(512)} %constant.90.clone.1), kind=kCustom, calls=%fused_computation.72 | custom fusion | bytes 1281 | tf_op jit(solution)/shard_map/scatter | solution.py:54
  60.8 0.3 reshape.182
  61.0 30.9 %scatter_custom_fusion.1 = s32[1280]{0:T(1024)S(1)} fusion(s32[8192]{0:T(1024)S(1)} %bitcast.49, s32[8192]{0:T(1024)S(1)} %reshape.182, s32[]{:T(128)} %constant.93.clone.1), kind=kCustom, calls=%fused_computation.69 | custom fusion | bytes 5124 | tf_op jit(solution)/shard_map/scatter | solution.py:53
  92.0 5.0 gather_fusion
  97.1 23.2 %gather_fusion.1 = bf16[1280,4096]{1,0:T(8,128)(2,1)} fusion(bf16[1024,4096]{1,0:T(8,128)(2,1)} %all-gather.2.cloned.1.call-done, s32[2048]{0:T(1024)S(1)} %pad_clamp_fusion), kind=kCustom, calls=%fused_computation.1 | custom fusion | bytes 20976640 | tf_op jit(solution)/shard_map/jit(_take)/gather | solution.py:57
  120.3 6.9 %multiply_reduce_fusion = f32[1280]{0:T(1024)S(1)} fusion(bf16[1280,4096]{1,0:T(8,128)(2,1)} %gather_fusion.1, pred[1280]{0:T(1024)(128)(4,1)S(1)} %get-tuple-element.5), kind=kLoop, calls=%fused_computation.9 | loop fusion | flops 20970240 | bytes 10492160 | tf_op jit(solution)/shard_map/reduce_sum | solution.py:58
  127.3 9.0 %fusion.1 = bf16[16,80,4096]{2,1,0:T(8,128)(2,1)S(1)} fusion(f32[4096]{0:T(1024)S(1)} %copy-done, f32[16,80]{1,0:T(8,128)S(1)} %rsqrt.12, bf16[16,80,4096]{2,1,0:T(8,128)(2,1)} %bitcast.44, pred[16,80]{1,0:T(8,128)(4,1)S(1)} %broadcast_in_dim.109, pred[16,80]{1,0:T(8,128)(4,1)S(1)} %broadcast_in_dim.105), kind=kLoop, calls=%fused_computation.11 | loop fusion | flops 31457280 | bytes 20995584 | tf_op jit(solution)/shard_map/jit(_where)/select_n | solution.py:60
  136.4 122.8 %all_to_all.18 = bf16[16,80,4096]{2,1,0:T(8,128)(2,1)S(1)} all-to-all(bf16[16,80,4096]{2,1,0:T(8,128)(2,1)S(1)} %fusion.1), channel_id=1, replica_groups=mesh['rep'=16,'exp'=8] {'rep'}, dimensions={0} | all-to-all | bytes 20971520 | tf_op jit(solution)/shard_map/all_to_all | solution.py:62
  259.1 11.8 %fusion.7 = f32[1280,768]{1,0:T(8,128)} fusion(bf16[1280,4096]{1,0:T(8,128)(2,1)S(1)} %bitcast.46, bf16[1,4096,768]{2,1,0:T(8,128)(2,1)} %param.15), kind=kOutput, calls=%fused_computation.17 | convolution fusion | flops 8053063680 | bytes 20709376 | tf_op jit(solution)/shard_map/dot_general | solution.py:8
  271.0 10.3 %fusion.12 = bf16[1280,768]{1,0:T(8,128)(2,1)S(1)} fusion(bf16[1280,4096]{1,0:T(8,128)(2,1)S(1)} %bitcast.47, bf16[1,4096,768]{2,1,0:T(8,128)(2,1)S(1)} %bitcast.53, f32[1280,768]{1,0:T(8,128)} %fusion.7), kind=kOutput, calls=%fused_computation.20 | convolution fusion | flops 8058961920 | bytes 22675456 | tf_op jit(solution)/shard_map/dot_general | solution.py:9
  281.3 10.7 %convolution_convert_fusion = bf16[1280,4096]{1,0:T(8,128)(2,1)} fusion(bf16[1280,768]{1,0:T(8,128)(2,1)S(1)} %fusion.12, bf16[1,768,4096]{2,1,0:T(8,128)(2,1)S(1)} %bitcast.55), kind=kOutput, calls=%fused_computation.10 | convolution fusion | flops 8058306560 | bytes 18743296 | tf_op jit(solution)/shard_map/dot_general | solution.py:11
  292.0 8.3 %all-to-all-start.1 = ((bf16[16,80,4096]{2,1,0:T(8,128)(2,1)}), bf16[16,80,4096]{2,1,0:T(8,128)(2,1)}, u32[]{:S(2)}, u32[]{:S(2)}) async-start(bf16[16,80,4096]{2,1,0:T(8,128)(2,1)} %bitcast.45), calls=%async_computation.1 | async-start | bytes 20971520 | tf_op jit(solution)/shard_map/all_to_all | solution.py:64
  300.3 12.8 %all_gather.10 = f32[1024,8]{0,1:T(8,128)S(1)} all-gather(f32[128,8]{0,1:T(8,128)S(1)} %divide_multiply_fusion), channel_id=1, replica_groups=mesh['rep'=16,'exp'=8] {'exp'}, dimensions={0}, use_global_device_ids=true | all-gather | bytes 36864 | tf_op jit(solution)/shard_map/all_gather | solution.py:43
  313.1 0.2 copy.35
  313.3 0.3 reshape.190
  313.6 30.4 %scatter_custom_fusion.2 = f32[1280]{0:T(1024)S(1)} fusion(s32[8192]{0:T(1024)S(1)} %bitcast.50, f32[8192]{0:T(1024)S(1)} %reshape.190, f32[]{:T(128)} %constant.89.clone.1), kind=kCustom, calls=%fused_computation.67 | custom fusion | bytes 5124 | tf_op jit(solution)/shard_map/scatter | solution.py:55
  344.0 89.5 %all-to-all-done.1 = bf16[16,80,4096]{2,1,0:T(8,128)(2,1)} async-done(((bf16[16,80,4096]{2,1,0:T(8,128)(2,1)}), bf16[16,80,4096]{2,1,0:T(8,128)(2,1)}, u32[]{:S(2)}, u32[]{:S(2)}) %all-to-all-start.1) | async-done | bytes 10485792 | tf_op jit(solution)/shard_map/all_to_all | solution.py:64
  433.5 42.9 %scatter_custom_fusion.3 = f32[1024,4096]{1,0:T(8,128)} fusion(s32[1280]{0:T(1024)S(1)} %get-tuple-element.8, bf16[1280,4096]{1,0:T(8,128)(2,1)} %bitcast.16, f32[1280]{0:T(1024)S(1)} %scatter_custom_fusion.2, f32[]{:T(128)} %constant.89.clone.1), kind=kCustom, calls=%fused_computation.7 | custom fusion | flops 15728640 | bytes 27271172 | tf_op jit(solution)/shard_map/scatter-add | solution.py:68
  476.4 9.0 %convert_element_type.50 = bf16[1024,4096]{1,0:T(8,128)(2,1)} convert(f32[1024,4096]{1,0:T(8,128)} %scatter_custom_fusion.3) | non-fusion elementwise | flops 4194304 | bytes 25165824 | tf_op jit(solution)/shard_map/convert_element_type | solution.py:69
  485.5 94.7 %reduce-scatter.2.cloned.1.call-done = bf16[128,4096]{1,0:T(8,128)(2,1)} async-done(((bf16[1024,4096]{1,0:T(8,128)(2,1)}), bf16[128,4096]{1,0:T(8,128)(2,1)}) %reduce-scatter.2.cloned.1.call-update) | async-done | bytes 1048592 | tf_op jit(solution)/shard_map/reduce_scatter | solution.py:69
  (47 shorter events, 1.1 us)
Async XLA Ops:
  6.5 90.6 %all-gather.2.cloned.1.call-start = ((), (), s32[]{:S(2)}) async-start(), calls=%async_computation.3 | async-start | bytes 9437184 | tf_op jit(solution)/shard_map/all_gather | solution.py:41
  120.3 7.0 %copy-start = (f32[4096]{0:T(1024)S(1)}, f32[4096]{0:T(1024)}, u32[]{:S(2)}) copy-start(f32[4096]{0:T(1024)} %param.14) | copy-start | bytes 49156
  136.3 134.6 %slice-start = ((s8[6291456]{0:T(1024)(128)(4,1)}), s8[4194304]{0:T(1024)(128)(4,1)S(1)}, s32[]{:S(2)}) async-start(s8[6291456]{0:T(1024)(128)(4,1)} %bitcast.52), calls=%async_computation.5 | async-start | bytes 8388608
  136.4 144.9 %slice-start.2 = ((s8[6291456]{0:T(1024)(128)(4,1)}), s8[4194304]{0:T(1024)(128)(4,1)S(1)}, s32[]{:S(2)}) async-start(s8[6291456]{0:T(1024)(128)(4,1)} %bitcast.54), calls=%async_computation.7 | async-start | bytes 8388608
  259.1 11.8 %slice-start.1 = ((s8[6291456]{0:T(1024)(128)(4,1)}), s8[2097152]{0:T(1024)(128)(4,1)S(1)}, s32[]{:S(2)}) async-start(s8[6291456]{0:T(1024)(128)(4,1)} %bitcast.52), calls=%async_computation.6 | async-start | bytes 4194304
  259.1 22.1 %slice-start.3 = ((s8[6291456]{0:T(1024)(128)(4,1)}), s8[2097152]{0:T(1024)(128)(4,1)S(1)}, s32[]{:S(2)}) async-start(s8[6291456]{0:T(1024)(128)(4,1)} %bitcast.54), calls=%async_computation.8 | async-start | bytes 4194304
  292.0 8.3 %copy-start.1 = (f32[128,8]{0,1:T(8,128)S(1)}, f32[128,8]{0,1:T(8,128)}, u32[]{:S(2)}) copy-start(f32[128,8]{0,1:T(8,128)} %param.12) | copy-start | bytes 12292
  292.0 141.6 %all-to-all-start.1 = ((bf16[16,80,4096]{2,1,0:T(8,128)(2,1)}), bf16[16,80,4096]{2,1,0:T(8,128)(2,1)}, u32[]{:S(2)}, u32[]{:S(2)}) async-start(bf16[16,80,4096]{2,1,0:T(8,128)(2,1)} %bitcast.45), calls=%async_computation.1 | async-start | bytes 20971520 | tf_op jit(solution)/shard_map/all_to_all | solution.py:64
  300.2 279.9 %reduce-scatter.2.cloned.1.call-start = ((), (), s32[]{:S(2)}) async-start(), calls=%async_computation.4 | async-start | bytes 9437184 | tf_op jit(solution)/shard_map/reduce_scatter | solution.py:69
Sparse Core Ops, SparseCore 0:
  9.1 50.7 all-gather.1
  485.6 94.5 reduce-scatter.1

commit v3 on v2

--- a/solution.py
+++ b/solution.py
@@ -33,28 +33,33 @@
     ).astype(jnp.int32)
     before = jnp.cumsum(onehot, axis=0) - onehot
     rank = jnp.sum(before * onehot, axis=1)
-    code = jnp.where(live_slot, flat, -1)
-    ints = jnp.concatenate(
-        [code.reshape(rows, top), rank.reshape(rows, top), parents[:, None]], axis=1
+    position = jnp.where(live_slot, flat * cap + rank, n_dev * cap)
+    slot_row = jnp.arange(rows * top, dtype=jnp.int32) // top
+    match = position[:, None] == jnp.arange(n_dev * cap, dtype=jnp.int32)[None, :]
+    filled_here = jnp.any(match, axis=0)
+    row_here = jnp.sum(jnp.where(match, slot_row[:, None], 0), axis=0)
+    parent_here = jnp.sum(jnp.where(match, jnp.take(parents, slot_row)[:, None], 0), axis=0)
+    w_here = jnp.sum(jnp.where(match, weights.reshape(-1)[:, None], 0.0), axis=0)
+    table = jnp.stack(
+        [
+            jnp.where(filled_here, row_here, -1).astype(jnp.float32),
+            parent_here.astype(jnp.float32),
+            w_here,
+        ],
+        axis=1,
     )
 
     group = lax.all_gather(hidden, "exp", axis=0, tiled=True)
-    ints_all = lax.all_gather(ints, "exp", axis=0, tiled=True)
-    w_all = lax.all_gather(weights, "exp", axis=0, tiled=True)
+    table_all = lax.all_gather(table, "exp", axis=0, tiled=False)
+    table_all = table_all.reshape(n_exp, n_rep, n_exp, cap, 3)
+    table_col = lax.dynamic_index_in_dim(table_all, column, axis=2, keepdims=False)
+    table_col = jnp.transpose(table_col, (1, 0, 2, 3))
+    row_tbl = table_col[..., 0].astype(jnp.int32)
+    src_row = table_col[..., 1].astype(jnp.int32).reshape(-1)
+    w_tbl = table_col[..., 2]
+    filled = (row_tbl >= 0).reshape(-1)
 
-    code_all = ints_all[:, :top]
-    rank_all = ints_all[:, top : 2 * top]
-    parent_all = ints_all[:, 2 * top]
-    mine = (code_all >= 0) & (code_all % n_exp == column)
-    owner = (jnp.arange(micro, dtype=jnp.int32) // rows)[:, None]
-    dest = (code_all // n_exp) * per_expert + owner * cap + rank_all
-    dest = jnp.where(mine, dest, slots).reshape(-1)
-    row_id = jnp.broadcast_to(jnp.arange(micro, dtype=jnp.int32)[:, None], (micro, top)).reshape(-1)
-    src_row = jnp.zeros((slots,), jnp.int32).at[dest].set(row_id, mode="drop")
-    filled = jnp.zeros((slots,), jnp.bool_).at[dest].set(True, mode="drop")
-    slot_w = jnp.zeros((slots,), jnp.float32).at[dest].set(w_all.reshape(-1), mode="drop")
-
-    picked = jnp.take(group, jnp.take(parent_all, src_row), axis=0).astype(jnp.float32)
+    picked = jnp.take(group, src_row, axis=0).astype(jnp.float32)
     scale = lax.rsqrt(jnp.mean(picked * picked, axis=1, keepdims=True) + 1e-06)
     normed = (picked * scale * norm_gain).astype(jnp.bfloat16)
     outgoing = jnp.where(filled[:, None], normed, jnp.zeros((), jnp.bfloat16))
@@ -63,9 +68,16 @@
     results = run_expert(arrived, w_gate, w_up, w_down)
     returned = lax.all_to_all(results, "rep", split_axis=0, concat_axis=0, tiled=True)
 
-    contrib = slot_w[:, None] * returned.astype(jnp.float32)
-    target = jnp.where(filled, src_row, micro)
-    partial = jnp.zeros((micro, width), jnp.float32).at[target].add(contrib, mode="drop")
+    returned = returned.reshape(n_rep, n_exp, cap, width)
+    pick = row_tbl[None] == jnp.arange(rows, dtype=jnp.int32)[:, None, None, None]
+    mix = jnp.transpose(jnp.where(pick, w_tbl[None], 0.0), (2, 0, 1, 3))
+    mix_hi = mix.astype(jnp.bfloat16)
+    mix_lo = (mix - mix_hi.astype(jnp.float32)).astype(jnp.bfloat16)
+    partial = jnp.einsum("drec,edcw->drw", mix_hi, returned, preferred_element_type=jnp.float32)
+    partial = partial + jnp.einsum(
+        "drec,edcw->drw", mix_lo, returned, preferred_element_type=jnp.float32
+    )
+    partial = partial.reshape(micro, width)
     mixed = lax.psum_scatter(partial.astype(jnp.bfloat16), "exp", scatter_dimension=0, tiled=True)
     return mixed
 

time: 597 us -> 543 us (0.910); the launches traced: 587 us -> 539 us
  local copies, waits for them, and re-layouts: 127 us -> 47.9 us
  waiting for transfers between devices: 185 us -> 252 us
  other arithmetic: 70.3 us -> 21.1 us
  matrix products: 32.8 us -> 58.6 us
  blocking collectives: 149 us -> 137 us
    scatter x3 -> x0, local copies, waits for them, and re-layouts: 95.9 us -> none  [the longest x1 34.6 us: shards(): filled = jnp.zeros((slots,), jnp.bool_).at[dest].set(True, mode='drop')]
    all_to_all x1, waiting for transfers between devices: 89.5 us -> 134 us  [shards(): lax.all_to_all(results, 'rep', split_axis=0, concat_axis=0, tiled=True)]
    scatter-add x1 -> x0, other arithmetic: 42.9 us -> none  [shards(): jnp.zeros((micro, width), jnp.float32).at[target].add(contrib, mode='drop')]
    dot_general x0 -> x2, matrix products: none -> 25.8 us  [the longest x1 13.7 us: shards(): jnp.einsum('drec,edcw->drw', mix_lo, returned, preferred_element_type=jnp...]
    all_gather x1, waiting for transfers between devices: 0.02 us -> 22.3 us  [shards(): group = lax.all_gather(hidden, 'exp', axis=0, tiled=True)]
    all_to_all x0 -> x1, local copies, waits for them, and re-layouts: none -> 13.7 us  [shards(): lax.all_to_all(results, 'rep', split_axis=0, concat_axis=0, tiled=True)]
    all_gather x2 -> x1, blocking collectives: 26.4 us -> 14.1 us  [shards(): table_all = lax.all_gather(table, 'exp', axis=0, tiled=False)]
    convert_element_type x2, other arithmetic: 9.01 us -> 0.01 us  [the longest x1 0.01 us: shards(): jnp.where(filled_here, row_here, -1).astype(jnp.float32)]
  transfers between devices with their start and end apart: 3 -> 3, of which waited for: 2 -> 3; matrix products, arithmetic and copies ran while one was open for 18% -> 3% of each run, Pallas kernels for 0% -> 0%
where the time goes in v3:
time: 543 us; the launch traced here: 539 us
  waiting for transfers between devices  252 us (46%)
  blocking collectives  137 us (25%)
  matrix products  58.6 us (11%)
  local copies, waits for them, and re-layouts  47.9 us (9%)
  other arithmetic  21.1 us (4%)
  between operations  14.4 us (3%)
  starting transfers between devices  8.47 us (2%)
    all_to_all x1, waiting for transfers between devices, shards(): lax.all_to_all(results, 'rep', split_axis=0, concat_axis=0, tiled=True)  134 us
    all_to_all x1, blocking collectives, shards(): lax.all_to_all(outgoing, 'rep', split_axis=0, concat_axis=0, tiled=True)  122 us
    reduce_scatter x1, waiting for transfers between devices, shards(): lax.psum_scatter(partial.astype(jnp.bfloat16), 'exp', scatter_dimension=0...  95.3 us
    gather x1, local copies, waits for them, and re-layouts, shards(): picked = jnp.take(group, src_row, axis=0).astype(jnp.float32)  23.2 us
    all_gather x1, waiting for transfers between devices, shards(): group = lax.all_gather(hidden, 'exp', axis=0, tiled=True)  22.3 us
    all_gather x1, blocking collectives, shards(): table_all = lax.all_gather(table, 'exp', axis=0, tiled=False)  14.1 us
    dot_general x1, matrix products, shards(): jnp.einsum('drec,edcw->drw', mix_lo, returned, preferred_element_type=jnp...  13.7 us
    all_to_all x1, local copies, waits for them, and re-layouts, shards(): lax.all_to_all(results, 'rep', split_axis=0, concat_axis=0, tiled=True)  13.7 us
  transfers between devices with their start and end apart: 3, of which 3 were waited for; matrix products, arithmetic and copies ran while one was open for 3% of the time, Pallas kernels for 0%

profile of v3, /device:TPU:50, one launch (start us, length us, event | category | flops | bytes accessed | tf_op | source)
XLA Modules:
  0.0 539.4 jit_solution(7561383748799319188)
XLA Ops:
  6.5 0.7 all-gather.3.cloned.1.call-update
  7.3 0.8 copy.36
  9.1 0.7 reduce_sum.57
  9.8 0.7 divide_multiply_fusion
  10.8 0.3 fusion.17
  11.4 0.5 fusion.16
  11.9 0.7 select_reduce_fusion
  12.6 6.6 %gather_fusion = s32[1024]{0:T(1024)S(1)} fusion(s32[128]{0:T(128)S(1)} %copy-done, s32[1024]{0:T(1024)S(1)} %broadcast_clamp_fusion), kind=kCustom, calls=%fused_computation | custom fusion | bytes 12288 | tf_op jit(solution)/shard_map/jit(_take)/gather | solution.py:41
  19.2 0.8 fusion.7
  20.0 1.2 select_reduce_fusion.2
  21.3 14.1 %all-gather = f32[10240,3]{0,1:T(4,128)S(1)} all-gather(f32[1280,3]{0,1:T(4,128)S(1)} %pad_maximum_fusion), channel_id=2, replica_groups=mesh['rep'=16,'exp'=8] {'exp'}, dimensions={0}, use_global_device_ids=true | all-gather | bytes 138240 | tf_op jit(solution)/shard_map/all_gather | solution.py:53
  35.4 1.6 reshape.234
  37.0 0.2 constant_dynamic-slice_fusion
  37.2 0.2 copy.41
  37.5 0.1 convert_element_type.122
  37.7 0.1 convert_element_type.124
  37.9 0.1 copy.44
  38.2 22.3 %all-gather.3.cloned.1.call-done = bf16[1024,4096]{1,0:T(8,128)(2,1)} async-done(((bf16[128,4096]{1,0:T(8,128)(2,1)}), bf16[1024,4096]{1,0:T(8,128)(2,1)}) %all-gather.3.cloned.1.call-update) | async-done | bytes 8388624 | tf_op jit(solution)/shard_map/all_gather | solution.py:52
  60.6 23.2 %gather_fusion.1 = bf16[1280,4096]{1,0:T(8,128)(2,1)} fusion(bf16[1024,4096]{1,0:T(8,128)(2,1)} %all-gather.3.cloned.1.call-done, s32[2048]{0:T(1024)S(1)} %pad_clamp_fusion), kind=kCustom, calls=%fused_computation.1 | custom fusion | bytes 20976640 | tf_op jit(solution)/shard_map/jit(_take)/gather | solution.py:62
  83.8 6.9 %multiply_reduce_fusion = f32[1280]{0:T(1024)S(1)} fusion(bf16[1280,4096]{1,0:T(8,128)(2,1)} %gather_fusion.1, pred[1280]{0:T(1024)(128)(4,1)S(1)} %compare_and_fusion), kind=kLoop, calls=%fused_computation.3 | loop fusion | flops 20970240 | bytes 10492160 | tf_op jit(solution)/shard_map/reduce_sum | solution.py:63
  90.8 9.1 %fusion.1 = bf16[16,80,4096]{2,1,0:T(8,128)(2,1)S(1)} fusion(f32[4096]{0:T(1024)S(1)} %copy-done.2, f32[16,80]{1,0:T(8,128)S(1)} %rsqrt.12, bf16[16,80,4096]{2,1,0:T(8,128)(2,1)} %bitcast.76, pred[16,80]{1,0:T(8,128)(4,1)S(1)} %compare_and_fusion.1, pred[16,80]{1,0:T(8,128)(4,1)S(1)} %ge.45), kind=kLoop, calls=%fused_computation.7 | loop fusion | flops 31457280 | bytes 20995584 | tf_op jit(solution)/shard_map/jit(_where)/select_n | solution.py:65
  99.9 122.5 %all_to_all.18 = bf16[16,80,4096]{2,1,0:T(8,128)(2,1)S(1)} all-to-all(bf16[16,80,4096]{2,1,0:T(8,128)(2,1)S(1)} %fusion.1), channel_id=1, replica_groups=mesh['rep'=16,'exp'=8] {'rep'}, dimensions={0} | all-to-all | bytes 20971520 | tf_op jit(solution)/shard_map/all_to_all | solution.py:67
  222.3 11.9 %fusion.5 = f32[1280,768]{1,0:T(8,128)} fusion(bf16[1280,4096]{1,0:T(8,128)(2,1)S(1)} %bitcast.81, bf16[1,4096,768]{2,1,0:T(8,128)(2,1)} %param.15), kind=kOutput, calls=%fused_computation.11 | convolution fusion | flops 8053063680 | bytes 20709376 | tf_op jit(solution)/shard_map/dot_general | solution.py:8
  234.2 10.3 %fusion.11 = bf16[1280,768]{1,0:T(8,128)(2,1)S(1)} fusion(bf16[1280,4096]{1,0:T(8,128)(2,1)S(1)} %bitcast.82, bf16[1,4096,768]{2,1,0:T(8,128)(2,1)S(1)} %bitcast.87, f32[1280,768]{1,0:T(8,128)} %fusion.5), kind=kOutput, calls=%fused_computation.19 | convolution fusion | flops 8058961920 | bytes 22675456 | tf_op jit(solution)/shard_map/dot_general | solution.py:9
  244.6 10.6 %convolution_convert_fusion = bf16[1280,4096]{1,0:T(8,128)(2,1)} fusion(bf16[1280,768]{1,0:T(8,128)(2,1)S(1)} %fusion.11, bf16[1,768,4096]{2,1,0:T(8,128)(2,1)S(1)} %bitcast.89), kind=kOutput, calls=%fused_computation.6 | convolution fusion | flops 8058306560 | bytes 18743296 | tf_op jit(solution)/shard_map/dot_general | solution.py:11
  255.1 8.2 %all-to-all-start.1 = ((bf16[16,80,4096]{2,1,0:T(8,128)(2,1)}), bf16[16,80,4096]{2,1,0:T(8,128)(2,1)}, u32[]{:S(2)}, u32[]{:S(2)}) async-start(bf16[16,80,4096]{2,1,0:T(8,128)(2,1)} %bitcast.80), calls=%async_computation.1 | async-start | bytes 20971520 | tf_op jit(solution)/shard_map/all_to_all | solution.py:69
  263.3 0.3 reduce-scatter.2.cloned.1.call-start
  263.6 134.0 %all-to-all-done.1 = bf16[16,80,4096]{2,1,0:T(8,128)(2,1)} async-done(((bf16[16,80,4096]{2,1,0:T(8,128)(2,1)}), bf16[16,80,4096]{2,1,0:T(8,128)(2,1)}, u32[]{:S(2)}, u32[]{:S(2)}) %all-to-all-start.1) | async-done | bytes 10485792 | tf_op jit(solution)/shard_map/all_to_all | solution.py:69
  397.6 13.7 %copy.48 = bf16[16,80,4096]{2,0,1:T(8,128)(2,1)} copy(bf16[16,80,4096]{2,1,0:T(8,128)(2,1)} %all-to-all-done.1) | data formatting | bytes 20971520 | tf_op jit(solution)/shard_map/all_to_all | solution.py:69
  411.3 12.1 %fusion.22 = f32[8,128,4096,1]{2,1,3,0:T(8,128)} fusion(bf16[16,8,10,4096]{3,0,2,1:T(8,128)(2,1)} %bitcast.77, f32[8,16,10]{1,2,0:T(8,128)S(1)} %copy.43, s32[8,16,10]{1,2,0:T(8,128)S(1)} %copy.42), kind=kOutput, calls=%fused_computation.33 | convolution fusion | flops 1342504960 | bytes 27273216 | tf_op jit(solution)/shard_map/drec,edcw->drw/dot_general | solution.py:76
  423.5 13.7 %fusion = bf16[8,128,4096]{2,1,0:T(8,128)(2,1)} fusion(f32[8,128,4096,1]{2,1,3,0:T(8,128)} %fusion.22, bf16[16,8,10,4096]{3,0,2,1:T(8,128)(2,1)} %bitcast.78, f32[8,16,10]{1,2,0:T(8,128)S(1)} %copy.43, s32[8,16,10]{1,2,0:T(8,128)S(1)} %copy.42), kind=kOutput, calls=%fused_computation.5 | convolution fusion | flops 1351548928 | bytes 35661824 | tf_op jit(solution)/shard_map/drec,edcw->drw/dot_general | solution.py:77
  437.2 95.3 %reduce-scatter.2.cloned.1.call-done = bf16[128,4096]{1,0:T(8,128)(2,1)} async-done(((bf16[1024,4096]{1,0:T(8,128)(2,1)}), bf16[128,4096]{1,0:T(8,128)(2,1)}) %reduce-scatter.2.cloned.1.call-update) | async-done | bytes 1048592 | tf_op jit(solution)/shard_map/reduce_scatter | solution.py:81
  (56 shorter events, 1.5 us)
Async XLA Ops:
  6.5 6.1 %copy-start = (s32[128]{0:T(128)S(1)}, s32[128]{0:T(128)}, u32[]{:S(2)}) copy-start(s32[128]{0:T(128)} %param.10) | copy-start | bytes 1540
  6.5 54.0 %all-gather.3.cloned.1.call-start = ((), (), s32[]{:S(2)}) async-start(), calls=%async_computation.3 | async-start | bytes 9437184 | tf_op jit(solution)/shard_map/all_gather | solution.py:52
  83.8 7.0 %copy-start.2 = (f32[4096]{0:T(1024)S(1)}, f32[4096]{0:T(1024)}, u32[]{:S(2)}) copy-start(f32[4096]{0:T(1024)} %param.14) | copy-start | bytes 49156
  99.8 134.3 %slice-start = ((s8[6291456]{0:T(1024)(128)(4,1)}), s8[4194304]{0:T(1024)(128)(4,1)S(1)}, s32[]{:S(2)}) async-start(s8[6291456]{0:T(1024)(128)(4,1)} %bitcast.86), calls=%async_computation.5 | async-start | bytes 8388608
  99.9 144.7 %slice-start.2 = ((s8[6291456]{0:T(1024)(128)(4,1)}), s8[4194304]{0:T(1024)(128)(4,1)S(1)}, s32[]{:S(2)}) async-start(s8[6291456]{0:T(1024)(128)(4,1)} %bitcast.88), calls=%async_computation.7 | async-start | bytes 8388608
  222.3 11.9 %slice-start.1 = ((s8[6291456]{0:T(1024)(128)(4,1)}), s8[2097152]{0:T(1024)(128)(4,1)S(1)}, s32[]{:S(2)}) async-start(s8[6291456]{0:T(1024)(128)(4,1)} %bitcast.86), calls=%async_computation.6 | async-start | bytes 4194304
  222.3 22.2 %slice-start.3 = ((s8[6291456]{0:T(1024)(128)(4,1)}), s8[2097152]{0:T(1024)(128)(4,1)S(1)}, s32[]{:S(2)}) async-start(s8[6291456]{0:T(1024)(128)(4,1)} %bitcast.88), calls=%async_computation.8 | async-start | bytes 4194304
  255.1 142.5 %all-to-all-start.1 = ((bf16[16,80,4096]{2,1,0:T(8,128)(2,1)}), bf16[16,80,4096]{2,1,0:T(8,128)(2,1)}, u32[]{:S(2)}, u32[]{:S(2)}) async-start(bf16[16,80,4096]{2,1,0:T(8,128)(2,1)} %bitcast.80), calls=%async_computation.1 | async-start | bytes 20971520 | tf_op jit(solution)/shard_map/all_to_all | solution.py:69
  263.3 269.3 %reduce-scatter.2.cloned.1.call-start = ((), (), s32[]{:S(2)}) async-start(), calls=%async_computation.4 | async-start | bytes 9437184 | tf_op jit(solution)/shard_map/reduce_scatter | solution.py:81
  423.5 109.1 %copy-start.1 = (s32[128]{0:T(128)S(1)}, s32[128]{0:T(128)}, u32[]{:S(2)}) copy-start(s32[128]{0:T(128)} %param.10) | copy-start | bytes 1540
Sparse Core Ops, SparseCore 0:
  9.1 51.4 all-gather.2
  437.3 95.1 reduce-scatter.1

commit v4 on v3

--- a/solution.py
+++ b/solution.py
@@ -38,7 +38,7 @@
     match = position[:, None] == jnp.arange(n_dev * cap, dtype=jnp.int32)[None, :]
     filled_here = jnp.any(match, axis=0)
     row_here = jnp.sum(jnp.where(match, slot_row[:, None], 0), axis=0)
-    parent_here = jnp.sum(jnp.where(match, jnp.take(parents, slot_row)[:, None], 0), axis=0)
+    parent_here = jnp.sum(jnp.where(match, jnp.repeat(parents, top)[:, None], 0), axis=0)
     w_here = jnp.sum(jnp.where(match, weights.reshape(-1)[:, None], 0.0), axis=0)
     table = jnp.stack(
         [
@@ -67,10 +67,10 @@
     arrived = lax.all_to_all(outgoing, "rep", split_axis=0, concat_axis=0, tiled=True)
     results = run_expert(arrived, w_gate, w_up, w_down)
     returned = lax.all_to_all(results, "rep", split_axis=0, concat_axis=0, tiled=True)
-
     returned = returned.reshape(n_rep, n_exp, cap, width)
-    pick = row_tbl[None] == jnp.arange(rows, dtype=jnp.int32)[:, None, None, None]
-    mix = jnp.transpose(jnp.where(pick, w_tbl[None], 0.0), (2, 0, 1, 3))
+    after = (returned[0, 0, 0, 0] * 0).astype(jnp.int32)
+    pick = (row_tbl + after)[None] == jnp.arange(rows, dtype=jnp.int32)[:, None, None, None]
+    mix = jnp.transpose(jnp.where(pick, (w_tbl + after.astype(jnp.float32))[None], 0.0), (2, 0, 1, 3))
     mix_hi = mix.astype(jnp.bfloat16)
     mix_lo = (mix - mix_hi.astype(jnp.float32)).astype(jnp.bfloat16)
     partial = jnp.einsum("drec,edcw->drw", mix_hi, returned, preferred_element_type=jnp.float32)

time: 543 us -> 477 us (0.88)
  waiting for transfers between devices: 252 us -> 79.5 us
  blocking collectives: 137 us -> 257 us
  starting transfers between devices: 8.47 us -> 0.04 us
    all_to_all x1 -> x0, waiting for transfers between devices: 134 us -> none  [shards(): lax.all_to_all(results, 'rep', split_axis=0, concat_axis=0, tiled=True)]
    all_to_all x0 -> x1, blocking collectives: none -> 121 us  [shards(): lax.all_to_all(results, 'rep', split_axis=0, concat_axis=0, tiled=True)]
    reduce_scatter x1, waiting for transfers between devices: 95.3 us -> 51.1 us  [shards(): lax.psum_scatter(partial.astype(jnp.bfloat16), 'exp', scatter_dimension=0...]
    all_to_all x1 -> x0, starting transfers between devices: 8.17 us -> none  [shards(): lax.all_to_all(results, 'rep', split_axis=0, concat_axis=0, tiled=True)]
    gather x1 -> x0, local copies, waits for them, and re-layouts: 6.57 us -> none  [shards(): jnp.take(parents, slot_row)[:, None]]
  transfers between devices with their start and end apart: 3 -> 2, of which waited for: 3 -> 2; matrix products, arithmetic and copies ran while one was open for 3% -> 2% of each run, Pallas kernels for 0% -> 0%
where the time goes in v4:
time: 477 us; the launch traced here: 473 us
  blocking collectives  257 us (54%)
  waiting for transfers between devices  79.5 us (17%)
  matrix products  56.9 us (12%)
  local copies, waits for them, and re-layouts  43.4 us (9%)
  other arithmetic  21 us (4%)
  between operations  15.1 us (3%)
    all_to_all x1, blocking collectives, shards(): lax.all_to_all(outgoing, 'rep', split_axis=0, concat_axis=0, tiled=True)  122 us
    all_to_all x1, blocking collectives, shards(): lax.all_to_all(results, 'rep', split_axis=0, concat_axis=0, tiled=True)  121 us
    reduce_scatter x1, waiting for transfers between devices, shards(): lax.psum_scatter(partial.astype(jnp.bfloat16), 'exp', scatter_dimension=0...  51.1 us
    all_gather x1, waiting for transfers between devices, shards(): group = lax.all_gather(hidden, 'exp', axis=0, tiled=True)  27.7 us
    gather x1, local copies, waits for them, and re-layouts, shards(): picked = jnp.take(group, src_row, axis=0).astype(jnp.float32)  23.2 us
    all_gather x1, blocking collectives, shards(): table_all = lax.all_gather(table, 'exp', axis=0, tiled=False)  14 us
    dot_general x1, matrix products, shards(): jnp.einsum('drec,edcw->drw', mix_lo, returned, preferred_element_type=jnp...  13.7 us
    all_to_all x1, local copies, waits for them, and re-layouts, shards(): lax.all_to_all(results, 'rep', split_axis=0, concat_axis=0, tiled=True)  13.7 us
  transfers between devices with their start and end apart: 2, of which 2 were waited for; matrix products, arithmetic and copies ran while one was open for 2% of the time, Pallas kernels for 0%

profile of v4, /device:TPU:50, one launch (start us, length us, event | category | flops | bytes accessed | tf_op | source)
XLA Modules:
  0.0 473.2 jit_solution(8589164267291266154)
XLA Ops:
  6.5 0.7 all-gather.3.cloned.1.call-update
  7.3 0.8 copy.36
  9.1 0.7 reduce_sum.57
  9.8 0.7 divide_multiply_fusion
  10.8 0.7 broadcast_in_dim.110
  11.7 0.3 fusion.17
  12.2 0.5 fusion.16
  12.8 0.7 select_reduce_fusion
  13.5 0.8 fusion.7
  14.2 1.2 select_reduce_fusion.2
  15.6 14.0 %all-gather = f32[10240,3]{0,1:T(4,128)S(1)} all-gather(f32[1280,3]{0,1:T(4,128)S(1)} %pad_maximum_fusion), channel_id=2, replica_groups=mesh['rep'=16,'exp'=8] {'exp'}, dimensions={0}, use_global_device_ids=true | all-gather | bytes 138240 | tf_op jit(solution)/shard_map/all_gather | solution.py:53
  29.6 1.6 reshape.203
  31.2 0.2 constant_dynamic-slice_fusion
  31.4 0.2 copy.41
  31.6 0.1 copy.43
  31.7 0.1 convert_element_type.127
  31.9 0.1 convert_element_type.129
  32.1 0.1 copy.42
  32.4 27.7 %all-gather.3.cloned.1.call-done = bf16[1024,4096]{1,0:T(8,128)(2,1)} async-done(((bf16[128,4096]{1,0:T(8,128)(2,1)}), bf16[1024,4096]{1,0:T(8,128)(2,1)}) %all-gather.3.cloned.1.call-update) | async-done | bytes 8388624 | tf_op jit(solution)/shard_map/all_gather | solution.py:52
  60.1 23.2 %gather_fusion = bf16[1280,4096]{1,0:T(8,128)(2,1)} fusion(bf16[1024,4096]{1,0:T(8,128)(2,1)} %all-gather.3.cloned.1.call-done, s32[2048]{0:T(1024)S(1)} %pad_clamp_fusion), kind=kCustom, calls=%fused_computation | custom fusion | bytes 20976640 | tf_op jit(solution)/shard_map/jit(_take)/gather | solution.py:62
  83.4 6.9 %multiply_reduce_fusion = f32[1280]{0:T(1024)S(1)} fusion(bf16[1280,4096]{1,0:T(8,128)(2,1)} %gather_fusion, pred[1280]{0:T(1024)(128)(4,1)S(1)} %compare_and_fusion), kind=kLoop, calls=%fused_computation.2 | loop fusion | flops 20970240 | bytes 10492160 | tf_op jit(solution)/shard_map/reduce_sum | solution.py:63
  90.3 9.0 %fusion.1 = bf16[16,80,4096]{2,1,0:T(8,128)(2,1)S(1)} fusion(f32[4096]{0:T(1024)S(1)} %copy-done, f32[16,80]{1,0:T(8,128)S(1)} %rsqrt.12, bf16[16,80,4096]{2,1,0:T(8,128)(2,1)} %bitcast.77, pred[16,80]{1,0:T(8,128)(4,1)S(1)} %compare_and_fusion.1, pred[16,80]{1,0:T(8,128)(4,1)S(1)} %ge.31), kind=kLoop, calls=%fused_computation.6 | loop fusion | flops 31457280 | bytes 20995584 | tf_op jit(solution)/shard_map/jit(_where)/select_n | solution.py:65
  99.4 122.5 %all_to_all.18 = bf16[16,80,4096]{2,1,0:T(8,128)(2,1)S(1)} all-to-all(bf16[16,80,4096]{2,1,0:T(8,128)(2,1)S(1)} %fusion.1), channel_id=1, replica_groups=mesh['rep'=16,'exp'=8] {'rep'}, dimensions={0} | all-to-all | bytes 20971520 | tf_op jit(solution)/shard_map/all_to_all | solution.py:67
  221.9 11.8 %fusion.5 = f32[1280,768]{1,0:T(8,128)} fusion(bf16[1280,4096]{1,0:T(8,128)(2,1)S(1)} %bitcast.82, bf16[1,4096,768]{2,1,0:T(8,128)(2,1)} %param.15), kind=kOutput, calls=%fused_computation.10 | convolution fusion | flops 8053063680 | bytes 20709376 | tf_op jit(solution)/shard_map/dot_general | solution.py:8
  233.7 10.3 %fusion.11 = bf16[1280,768]{1,0:T(8,128)(2,1)S(1)} fusion(bf16[1280,4096]{1,0:T(8,128)(2,1)S(1)} %bitcast.83, bf16[1,4096,768]{2,1,0:T(8,128)(2,1)S(1)} %bitcast.90, f32[1280,768]{1,0:T(8,128)} %fusion.5), kind=kOutput, calls=%fused_computation.18 | convolution fusion | flops 8058961920 | bytes 22675456 | tf_op jit(solution)/shard_map/dot_general | solution.py:9
  244.0 8.9 %convolution_convert_fusion = bf16[1280,4096]{1,0:T(8,128)(2,1)S(1)} fusion(bf16[1280,768]{1,0:T(8,128)(2,1)S(1)} %fusion.11, bf16[1,768,4096]{2,1,0:T(8,128)(2,1)S(1)} %bitcast.92), kind=kOutput, calls=%fused_computation.5 | convolution fusion | flops 8058306560 | bytes 18743296 | tf_op jit(solution)/shard_map/dot_general | solution.py:11
  252.9 120.9 %all_to_all.19 = bf16[16,80,4096]{2,1,0:T(8,128)(2,1)} all-to-all(bf16[16,80,4096]{2,1,0:T(8,128)(2,1)S(1)} %bitcast.84), channel_id=1, replica_groups=mesh['rep'=16,'exp'=8] {'rep'}, dimensions={0} | all-to-all | bytes 20971520 | tf_op jit(solution)/shard_map/all_to_all | solution.py:69
  373.8 13.7 %copy.46 = bf16[16,80,4096]{2,0,1:T(8,128)(2,1)} copy(bf16[16,80,4096]{2,1,0:T(8,128)(2,1)} %all_to_all.19) | data formatting | bytes 20971520 | tf_op jit(solution)/shard_map/all_to_all | solution.py:69
  387.5 1.2 slice.30
  389.4 12.2 %fusion.22 = f32[8,128,4096,1]{2,1,3,0:T(8,128)} fusion(bf16[16,8,10,4096]{3,0,2,1:T(8,128)(2,1)} %bitcast.79, f32[8,16,10]{1,2,0:T(8,128)S(1)} %copy.48, s32[8,16,10]{1,2,0:T(8,128)S(1)} %copy.47), kind=kOutput, calls=%fused_computation.32 | convolution fusion | flops 1342504960 | bytes 27273216 | tf_op jit(solution)/shard_map/drec,edcw->drw/dot_general | solution.py:76
  401.5 13.7 %fusion = bf16[8,128,4096]{2,1,0:T(8,128)(2,1)} fusion(f32[8,128,4096,1]{2,1,3,0:T(8,128)} %fusion.22, bf16[16,8,10,4096]{3,0,2,1:T(8,128)(2,1)} %bitcast.80, f32[8,16,10]{1,2,0:T(8,128)S(1)} %copy.48, s32[8,16,10]{1,2,0:T(8,128)S(1)} %copy.47), kind=kOutput, calls=%fused_computation.4 | convolution fusion | flops 1351548928 | bytes 35661824 | tf_op jit(solution)/shard_map/drec,edcw->drw/dot_general | solution.py:77
  415.3 51.1 %reduce-scatter.2.cloned.1.call-done = bf16[128,4096]{1,0:T(8,128)(2,1)} async-done(((bf16[1024,4096]{1,0:T(8,128)(2,1)}), bf16[128,4096]{1,0:T(8,128)(2,1)}) %reduce-scatter.2.cloned.1.call-update) | async-done | bytes 1048592 | tf_op jit(solution)/shard_map/reduce_scatter | solution.py:81
  (53 shorter events, 1.5 us)
Async XLA Ops:
  6.5 53.6 %all-gather.3.cloned.1.call-start = ((), (), s32[]{:S(2)}) async-start(), calls=%async_computation.3 | async-start | bytes 9437184 | tf_op jit(solution)/shard_map/all_gather | solution.py:52
  7.3 459.1 %reduce-scatter.2.cloned.1.call-start = ((), (), s32[]{:S(2)}) async-start(), calls=%async_computation.4 | async-start | bytes 9437184 | tf_op jit(solution)/shard_map/reduce_scatter | solution.py:81
  83.4 7.0 %copy-start = (f32[4096]{0:T(1024)S(1)}, f32[4096]{0:T(1024)}, u32[]{:S(2)}) copy-start(f32[4096]{0:T(1024)} %param.14) | copy-start | bytes 49156
  99.4 134.3 %slice-start = ((s8[6291456]{0:T(1024)(128)(4,1)}), s8[4194304]{0:T(1024)(128)(4,1)S(1)}, s32[]{:S(2)}) async-start(s8[6291456]{0:T(1024)(128)(4,1)} %bitcast.89), calls=%async_computation.5 | async-start | bytes 8388608
  99.4 144.6 %slice-start.2 = ((s8[6291456]{0:T(1024)(128)(4,1)}), s8[4194304]{0:T(1024)(128)(4,1)S(1)}, s32[]{:S(2)}) async-start(s8[6291456]{0:T(1024)(128)(4,1)} %bitcast.91), calls=%async_computation.7 | async-start | bytes 8388608
  221.8 11.8 %slice-start.1 = ((s8[6291456]{0:T(1024)(128)(4,1)}), s8[2097152]{0:T(1024)(128)(4,1)S(1)}, s32[]{:S(2)}) async-start(s8[6291456]{0:T(1024)(128)(4,1)} %bitcast.89), calls=%async_computation.6 | async-start | bytes 4194304
  221.9 22.1 %slice-start.3 = ((s8[6291456]{0:T(1024)(128)(4,1)}), s8[2097152]{0:T(1024)(128)(4,1)S(1)}, s32[]{:S(2)}) async-start(s8[6291456]{0:T(1024)(128)(4,1)} %bitcast.91), calls=%async_computation.8 | async-start | bytes 4194304
Sparse Core Ops, SparseCore 0:
  9.1 51.0 all-gather.2
  415.4 50.9 reduce-scatter.1

commit v5 on v4

--- a/solution.py
+++ b/solution.py
@@ -42,14 +42,17 @@
     w_here = jnp.sum(jnp.where(match, weights.reshape(-1)[:, None], 0.0), axis=0)
     table = jnp.stack(
         [
-            jnp.where(filled_here, row_here, -1).astype(jnp.float32),
+            jnp.where(filled_here, column * rows + row_here, -1).astype(jnp.float32),
             parent_here.astype(jnp.float32),
             w_here,
         ],
         axis=1,
     )
 
-    group = lax.all_gather(hidden, "exp", axis=0, tiled=True)
+    own = hidden.astype(jnp.float32)
+    own_scale = lax.rsqrt(jnp.mean(own * own, axis=1, keepdims=True) + 1e-06)
+    normed = (own * own_scale * norm_gain).astype(jnp.bfloat16)
+    group = lax.all_gather(normed, "exp", axis=0, tiled=True)
     table_all = lax.all_gather(table, "exp", axis=0, tiled=False)
     table_all = table_all.reshape(n_exp, n_rep, n_exp, cap, 3)
     table_col = lax.dynamic_index_in_dim(table_all, column, axis=2, keepdims=False)
@@ -59,25 +62,20 @@
     w_tbl = table_col[..., 2]
     filled = (row_tbl >= 0).reshape(-1)
 
-    picked = jnp.take(group, src_row, axis=0).astype(jnp.float32)
-    scale = lax.rsqrt(jnp.mean(picked * picked, axis=1, keepdims=True) + 1e-06)
-    normed = (picked * scale * norm_gain).astype(jnp.bfloat16)
-    outgoing = jnp.where(filled[:, None], normed, jnp.zeros((), jnp.bfloat16))
+    picked = jnp.take(group, src_row, axis=0)
+    outgoing = jnp.where(filled[:, None], picked, jnp.zeros((), jnp.bfloat16))
 
     arrived = lax.all_to_all(outgoing, "rep", split_axis=0, concat_axis=0, tiled=True)
     results = run_expert(arrived, w_gate, w_up, w_down)
     returned = lax.all_to_all(results, "rep", split_axis=0, concat_axis=0, tiled=True)
     returned = returned.reshape(n_rep, n_exp, cap, width)
-    after = (returned[0, 0, 0, 0] * 0).astype(jnp.int32)
-    pick = (row_tbl + after)[None] == jnp.arange(rows, dtype=jnp.int32)[:, None, None, None]
-    mix = jnp.transpose(jnp.where(pick, (w_tbl + after.astype(jnp.float32))[None], 0.0), (2, 0, 1, 3))
-    mix_hi = mix.astype(jnp.bfloat16)
-    mix_lo = (mix - mix_hi.astype(jnp.float32)).astype(jnp.bfloat16)
-    partial = jnp.einsum("drec,edcw->drw", mix_hi, returned, preferred_element_type=jnp.float32)
-    partial = partial + jnp.einsum(
-        "drec,edcw->drw", mix_lo, returned, preferred_element_type=jnp.float32
-    )
-    partial = partial.reshape(micro, width)
+    after = returned[0, 0, 0, 0].astype(jnp.float32) * 0
+    table_post = table_col + after
+    key = table_post[..., 0].astype(jnp.int32).reshape(-1)
+    w_key = table_post[..., 2].reshape(-1)
+    pick = jnp.arange(micro, dtype=jnp.int32)[:, None] == key[None, :]
+    mix = jnp.where(pick, w_key[None, :], 0.0).astype(jnp.bfloat16)
+    partial = jnp.dot(mix, returned.reshape(slots, width), preferred_element_type=jnp.float32)
     mixed = lax.psum_scatter(partial.astype(jnp.bfloat16), "exp", scatter_dimension=0, tiled=True)
     return mixed
 

time: 477 us -> 460 us (0.964)
  matrix products: 56.9 us -> 47.9 us
  other arithmetic: 21 us -> 15.3 us
    dot_general x2 -> x1, matrix products: 25.9 us -> 16.9 us  [shards(): jnp.dot(mix, returned.reshape(slots, width), preferred_element_type=jnp.f...]
    reduce_sum x1, other arithmetic: 6.86 us -> 1.52 us  [shards(): own_scale = lax.rsqrt(jnp.mean(own * own, axis=1, keepdims=True) + 1e-06)]
where the time goes in v5:
time: 460 us; the launch traced here: 457 us
  blocking collectives  257 us (56%)
  waiting for transfers between devices  77.5 us (17%)
  matrix products  47.9 us (10%)
  local copies, waits for them, and re-layouts  43.6 us (9%)
  other arithmetic  15.3 us (3%)
  between operations  15 us (3%)
    all_to_all x1, blocking collectives, shards(): lax.all_to_all(outgoing, 'rep', split_axis=0, concat_axis=0, tiled=True)  122 us
    all_to_all x1, blocking collectives, shards(): lax.all_to_all(results, 'rep', split_axis=0, concat_axis=0, tiled=True)  121 us
    reduce_scatter x1, waiting for transfers between devices, shards(): lax.psum_scatter(partial.astype(jnp.bfloat16), 'exp', scatter_dimension=0...  51.1 us
    all_gather x1, waiting for transfers between devices, shards(): group = lax.all_gather(normed, 'exp', axis=0, tiled=True)  26.4 us
    gather x1, local copies, waits for them, and re-layouts, shards(): picked = jnp.take(group, src_row, axis=0)  23.2 us
    dot_general x1, matrix products, shards(): jnp.dot(mix, returned.reshape(slots, width), preferred_element_type=jnp.f...  16.9 us
    all_gather x1, blocking collectives, shards(): table_all = lax.all_gather(table, 'exp', axis=0, tiled=False)  13.9 us
    all_to_all x1, local copies, waits for them, and re-layouts, shards(): lax.all_to_all(results, 'rep', split_axis=0, concat_axis=0, tiled=True)  13.5 us
  transfers between devices with their start and end apart: 2, of which 2 were waited for; matrix products, arithmetic and copies ran while one was open for 2% of the time, Pallas kernels for 0%

profile of v5, /device:TPU:50, one launch (start us, length us, event | category | flops | bytes accessed | tf_op | source)
XLA Modules:
  0.0 456.5 jit_solution(4574132553321854317)
XLA Ops:
  6.5 1.5 fusion.15
  8.1 2.5 fusion.17
  10.7 0.8 copy.41
  12.5 0.7 reduce_sum.57
  13.2 0.7 divide_multiply_fusion
  14.2 0.7 broadcast_in_dim.102
  15.1 0.3 fusion.20
  15.6 0.5 fusion.19
  16.1 0.7 select_reduce_fusion
  16.8 0.8 fusion.5
  17.6 1.2 select_reduce_fusion.2
  18.9 13.9 %all-gather = f32[10240,3]{0,1:T(4,128)S(1)} all-gather(f32[1280,3]{0,1:T(4,128)S(1)} %pad_maximum_fusion), channel_id=2, replica_groups=mesh['rep'=16,'exp'=8] {'exp'}, dimensions={0}, use_global_device_ids=true | all-gather | bytes 138240 | tf_op jit(solution)/shard_map/all_gather | solution.py:56
  32.8 1.6 reshape.179
  34.4 0.2 constant_dynamic-slice_fusion
  34.6 0.2 copy.46
  35.0 0.1 convert_element_type.113
  35.2 0.1 copy.47
  35.5 26.4 %all-gather.3.cloned.1.call-done = bf16[1024,4096]{1,0:T(8,128)(2,1)} async-done(((bf16[128,4096]{1,0:T(8,128)(2,1)}), bf16[1024,4096]{1,0:T(8,128)(2,1)}) %all-gather.3.cloned.1.call-update) | async-done | bytes 8388624 | tf_op jit(solution)/shard_map/all_gather | solution.py:55
  61.9 23.2 %gather_fusion = bf16[1280,4096]{1,0:T(8,128)(2,1)} fusion(bf16[1024,4096]{1,0:T(8,128)(2,1)} %all-gather.3.cloned.1.call-done, s32[2048]{0:T(1024)S(1)} %pad_clamp_fusion), kind=kCustom, calls=%fused_computation | custom fusion | bytes 20976640 | tf_op jit(solution)/shard_map/jit(_take)/gather | solution.py:65
  85.1 6.1 %select_select_fusion = bf16[16,80,4096]{2,1,0:T(8,128)(2,1)S(1)} fusion(bf16[16,80,4096]{2,1,0:T(8,128)(2,1)} %bitcast.65, pred[16,80]{1,0:T(8,128)(4,1)S(1)} %compare_and_fusion, pred[16,80]{1,0:T(8,128)(4,1)S(1)} %ge.29), kind=kLoop, calls=%fused_computation.2 | loop fusion | flops 10485760 | bytes 20974080 | tf_op jit(solution)/shard_map/jit(_where)/select_n | solution.py:66
  91.3 122.5 %all_to_all.21 = bf16[16,80,4096]{2,1,0:T(8,128)(2,1)S(1)} all-to-all(bf16[16,80,4096]{2,1,0:T(8,128)(2,1)S(1)} %select_select_fusion), channel_id=1, replica_groups=mesh['rep'=16,'exp'=8] {'rep'}, dimensions={0} | all-to-all | bytes 20971520 | tf_op jit(solution)/shard_map/all_to_all | solution.py:68
  213.8 11.8 %fusion.3 = f32[1280,768]{1,0:T(8,128)} fusion(bf16[1280,4096]{1,0:T(8,128)(2,1)S(1)} %bitcast.66, bf16[1,4096,768]{2,1,0:T(8,128)(2,1)} %param.15), kind=kOutput, calls=%fused_computation.7 | convolution fusion | flops 8053063680 | bytes 20709376 | tf_op jit(solution)/shard_map/dot_general | solution.py:8
  225.6 10.3 %fusion.9 = bf16[1280,768]{1,0:T(8,128)(2,1)S(1)} fusion(bf16[1280,4096]{1,0:T(8,128)(2,1)S(1)} %bitcast.67, bf16[1,4096,768]{2,1,0:T(8,128)(2,1)S(1)} %bitcast.73, f32[1280,768]{1,0:T(8,128)} %fusion.3), kind=kOutput, calls=%fused_computation.17 | convolution fusion | flops 8058961920 | bytes 22675456 | tf_op jit(solution)/shard_map/dot_general | solution.py:9
  235.9 8.9 %convolution_convert_fusion = bf16[1280,4096]{1,0:T(8,128)(2,1)S(1)} fusion(bf16[1280,768]{1,0:T(8,128)(2,1)S(1)} %fusion.9, bf16[1,768,4096]{2,1,0:T(8,128)(2,1)S(1)} %bitcast.75), kind=kOutput, calls=%fused_computation.1 | convolution fusion | flops 8058306560 | bytes 18743296 | tf_op jit(solution)/shard_map/dot_general | solution.py:11
  244.8 120.9 %all_to_all.22 = bf16[16,80,4096]{2,1,0:T(8,128)(2,1)} all-to-all(bf16[16,80,4096]{2,1,0:T(8,128)(2,1)S(1)} %bitcast.68), channel_id=1, replica_groups=mesh['rep'=16,'exp'=8] {'rep'}, dimensions={0} | all-to-all | bytes 20971520 | tf_op jit(solution)/shard_map/all_to_all | solution.py:70
  365.7 13.5 %copy.50 = bf16[16,80,4096]{2,0,1:T(8,128)(2,1)} copy(bf16[16,80,4096]{2,1,0:T(8,128)(2,1)} %all_to_all.22) | data formatting | bytes 20971520 | tf_op jit(solution)/shard_map/all_to_all | solution.py:70
  379.2 1.2 slice.34
  381.1 0.1 copy.52
  381.2 0.1 broadcast_in_dim.112
  381.5 0.1 convert_element_type.118
  381.6 16.9 %convolution_convert_fusion.1 = bf16[1024,4096]{1,0:T(8,128)(2,1)} fusion(bf16[1280,4096]{1,0:T(8,128)(2,1)} %bitcast.64, bf16[1280]{0:T(1024)(128)(2,1)S(1)} %broadcast_in_dim.112, s32[1280]{0:T(1024)S(1)} %convert_element_type.118), kind=kOutput, calls=%fused_computation.3 | convolution fusion | flops 10744233984 | bytes 18882048 | tf_op jit(solution)/shard_map/dot_general | solution.py:78
  398.6 51.1 %reduce-scatter.2.cloned.1.call-done = bf16[128,4096]{1,0:T(8,128)(2,1)} async-done(((bf16[1024,4096]{1,0:T(8,128)(2,1)}), bf16[128,4096]{1,0:T(8,128)(2,1)}) %reduce-scatter.2.cloned.1.call-update) | async-done | bytes 1048592 | tf_op jit(solution)/shard_map/reduce_scatter | solution.py:79
  (51 shorter events, 1.7 us)
Async XLA Ops:
  6.5 55.4 %all-gather.3.cloned.1.call-start = ((), (), s32[]{:S(2)}) async-start(), calls=%async_computation.3 | async-start | bytes 9437184 | tf_op jit(solution)/shard_map/all_gather | solution.py:55
  10.6 439.1 %reduce-scatter.2.cloned.1.call-start = ((), (), s32[]{:S(2)}) async-start(), calls=%async_computation.4 | async-start | bytes 9437184 | tf_op jit(solution)/shard_map/reduce_scatter | solution.py:79
  91.3 134.3 %slice-start = ((s8[6291456]{0:T(1024)(128)(4,1)}), s8[4194304]{0:T(1024)(128)(4,1)S(1)}, s32[]{:S(2)}) async-start(s8[6291456]{0:T(1024)(128)(4,1)} %bitcast.72), calls=%async_computation.5 | async-start | bytes 8388608
  91.3 144.6 %slice-start.2 = ((s8[6291456]{0:T(1024)(128)(4,1)}), s8[4194304]{0:T(1024)(128)(4,1)S(1)}, s32[]{:S(2)}) async-start(s8[6291456]{0:T(1024)(128)(4,1)} %bitcast.74), calls=%async_computation.7 | async-start | bytes 8388608
  213.8 11.8 %slice-start.1 = ((s8[6291456]{0:T(1024)(128)(4,1)}), s8[2097152]{0:T(1024)(128)(4,1)S(1)}, s32[]{:S(2)}) async-start(s8[6291456]{0:T(1024)(128)(4,1)} %bitcast.72), calls=%async_computation.6 | async-start | bytes 4194304
  213.8 22.1 %slice-start.3 = ((s8[6291456]{0:T(1024)(128)(4,1)}), s8[2097152]{0:T(1024)(128)(4,1)S(1)}, s32[]{:S(2)}) async-start(s8[6291456]{0:T(1024)(128)(4,1)} %bitcast.74), calls=%async_computation.8 | async-start | bytes 4194304
Sparse Core Ops, SparseCore 0:
  10.7 51.1 all-gather.2
  398.7 50.9 reduce-scatter.1

commit v6 on v5

--- a/solution.py
+++ b/solution.py
@@ -53,10 +53,8 @@
     own_scale = lax.rsqrt(jnp.mean(own * own, axis=1, keepdims=True) + 1e-06)
     normed = (own * own_scale * norm_gain).astype(jnp.bfloat16)
     group = lax.all_gather(normed, "exp", axis=0, tiled=True)
-    table_all = lax.all_gather(table, "exp", axis=0, tiled=False)
-    table_all = table_all.reshape(n_exp, n_rep, n_exp, cap, 3)
+    table_all = lax.all_gather(table.reshape(n_rep, n_exp, cap, 3), "exp", axis=1, tiled=False)
     table_col = lax.dynamic_index_in_dim(table_all, column, axis=2, keepdims=False)
-    table_col = jnp.transpose(table_col, (1, 0, 2, 3))
     row_tbl = table_col[..., 0].astype(jnp.int32)
     src_row = table_col[..., 1].astype(jnp.int32).reshape(-1)
     w_tbl = table_col[..., 2]
@@ -68,14 +66,13 @@
     arrived = lax.all_to_all(outgoing, "rep", split_axis=0, concat_axis=0, tiled=True)
     results = run_expert(arrived, w_gate, w_up, w_down)
     returned = lax.all_to_all(results, "rep", split_axis=0, concat_axis=0, tiled=True)
-    returned = returned.reshape(n_rep, n_exp, cap, width)
-    after = returned[0, 0, 0, 0].astype(jnp.float32) * 0
+    after = returned[0, 0].astype(jnp.float32) * 0
     table_post = table_col + after
     key = table_post[..., 0].astype(jnp.int32).reshape(-1)
     w_key = table_post[..., 2].reshape(-1)
     pick = jnp.arange(micro, dtype=jnp.int32)[:, None] == key[None, :]
     mix = jnp.where(pick, w_key[None, :], 0.0).astype(jnp.bfloat16)
-    partial = jnp.dot(mix, returned.reshape(slots, width), preferred_element_type=jnp.float32)
+    partial = jnp.dot(mix, returned, preferred_element_type=jnp.float32)
     mixed = lax.psum_scatter(partial.astype(jnp.bfloat16), "exp", scatter_dimension=0, tiled=True)
     return mixed
 

time: 460 us -> 453 us (0.985)
  local copies, waits for them, and re-layouts: 43.6 us -> 32 us
    all_to_all x1 -> x0, local copies, waits for them, and re-layouts: 13.5 us -> none  [shards(): lax.all_to_all(results, 'rep', split_axis=0, concat_axis=0, tiled=True)]
where the time goes in v6:
time: 453 us; the launch traced here: 449 us
  blocking collectives  260 us (57%)
  waiting for transfers between devices  79 us (17%)
  matrix products  47.9 us (11%)
  local copies, waits for them, and re-layouts  32 us (7%)
  other arithmetic  15.3 us (3%)
  between operations  15 us (3%)
    all_to_all x1, blocking collectives, shards(): lax.all_to_all(outgoing, 'rep', split_axis=0, concat_axis=0, tiled=True)  122 us
    all_to_all x1, blocking collectives, shards(): lax.all_to_all(results, 'rep', split_axis=0, concat_axis=0, tiled=True)  121 us
    reduce_scatter x1, waiting for transfers between devices, shards(): lax.psum_scatter(partial.astype(jnp.bfloat16), 'exp', scatter_dimension=0...  51.9 us
    all_gather x1, waiting for transfers between devices, shards(): group = lax.all_gather(normed, 'exp', axis=0, tiled=True)  27.1 us
    gather x1, local copies, waits for them, and re-layouts, shards(): picked = jnp.take(group, src_row, axis=0)  23.2 us
    dot_general x1, matrix products, shards(): partial = jnp.dot(mix, returned, preferred_element_type=jnp.float32)  16.9 us
    all_gather x1, blocking collectives, shards(): lax.all_gather(table.reshape(n_rep, n_exp, cap, 3), 'exp', axis=1, tiled=...  16.6 us
    dot_general x1, matrix products, run_expert(): gate_val = jnp.dot(arrived, w_gate[0], preferred_element_type=jnp.float32)  11.8 us
  transfers between devices with their start and end apart: 2, of which 2 were waited for; matrix products, arithmetic and copies ran while one was open for 2% of the time, Pallas kernels for 0%

profile of v6, /device:TPU:50, one launch (start us, length us, event | category | flops | bytes accessed | tf_op | source)
XLA Modules:
  0.0 449.1 jit_solution(5560486016694757373)
XLA Ops:
  6.5 1.5 fusion.15
  8.1 2.5 fusion.17
  10.7 0.8 copy.38
  12.5 0.7 reduce_sum.57
  13.2 0.7 divide_multiply_fusion
  14.2 0.7 broadcast_in_dim.102
  15.1 0.3 fusion.20
  15.6 0.5 fusion.19
  16.2 1.2 select_reduce_fusion.2
  17.5 0.8 fusion.5
  18.5 0.7 select_reduce_fusion
  19.3 0.2 copy.43
  19.5 16.6 %all_gather.6 = f32[16,8,8,10,3]{0,2,4,3,1:T(8,128)S(1)} all-gather(f32[16,1,8,10,3]{0,2,4,3,1:T(8,128)S(1)} %copy.43), channel_id=1, replica_groups=mesh['rep'=16,'exp'=8] {'exp'}, dimensions={1}, use_global_device_ids=true | all-gather | bytes 138240 | tf_op jit(solution)/shard_map/all_gather | solution.py:56
  36.2 0.1 copy.46
  36.4 0.1 convert_element_type.115
  36.6 0.1 copy.45
  36.9 27.1 %all-gather.2.cloned.1.call-done = bf16[1024,4096]{1,0:T(8,128)(2,1)} async-done(((bf16[128,4096]{1,0:T(8,128)(2,1)}), bf16[1024,4096]{1,0:T(8,128)(2,1)}) %all-gather.2.cloned.1.call-update) | async-done | bytes 8388624 | tf_op jit(solution)/shard_map/all_gather | solution.py:55
  64.0 23.2 %gather_fusion = bf16[1280,4096]{1,0:T(8,128)(2,1)} fusion(bf16[1024,4096]{1,0:T(8,128)(2,1)} %all-gather.2.cloned.1.call-done, s32[2048]{0:T(1024)S(1)} %pad_clamp_fusion), kind=kCustom, calls=%fused_computation | custom fusion | bytes 20976640 | tf_op jit(solution)/shard_map/jit(_take)/gather | solution.py:63
  87.2 6.1 %select_select_fusion = bf16[16,80,4096]{2,1,0:T(8,128)(2,1)S(1)} fusion(bf16[16,80,4096]{2,1,0:T(8,128)(2,1)} %bitcast.62, pred[16,80]{1,0:T(8,128)(4,1)S(1)} %compare_and_fusion, pred[16,80]{1,0:T(8,128)(4,1)S(1)} %ge.29), kind=kLoop, calls=%fused_computation.2 | loop fusion | flops 10485760 | bytes 20974080 | tf_op jit(solution)/shard_map/jit(_where)/select_n | solution.py:64
  93.4 122.5 %all_to_all.21 = bf16[16,80,4096]{2,1,0:T(8,128)(2,1)S(1)} all-to-all(bf16[16,80,4096]{2,1,0:T(8,128)(2,1)S(1)} %select_select_fusion), channel_id=1, replica_groups=mesh['rep'=16,'exp'=8] {'rep'}, dimensions={0} | all-to-all | bytes 20971520 | tf_op jit(solution)/shard_map/all_to_all | solution.py:66
  215.9 11.8 %fusion.3 = f32[1280,768]{1,0:T(8,128)} fusion(bf16[1280,4096]{1,0:T(8,128)(2,1)S(1)} %bitcast.65, bf16[1,4096,768]{2,1,0:T(8,128)(2,1)} %param.15), kind=kOutput, calls=%fused_computation.7 | convolution fusion | flops 8053063680 | bytes 20709376 | tf_op jit(solution)/shard_map/dot_general | solution.py:8
  227.7 10.3 %fusion.9 = bf16[1280,768]{1,0:T(8,128)(2,1)S(1)} fusion(bf16[1280,4096]{1,0:T(8,128)(2,1)S(1)} %bitcast.66, bf16[1,4096,768]{2,1,0:T(8,128)(2,1)S(1)} %bitcast.71, f32[1280,768]{1,0:T(8,128)} %fusion.3), kind=kOutput, calls=%fused_computation.17 | convolution fusion | flops 8058961920 | bytes 22675456 | tf_op jit(solution)/shard_map/dot_general | solution.py:9
  238.0 8.9 %convolution_convert_fusion = bf16[1280,4096]{1,0:T(8,128)(2,1)S(1)} fusion(bf16[1280,768]{1,0:T(8,128)(2,1)S(1)} %fusion.9, bf16[1,768,4096]{2,1,0:T(8,128)(2,1)S(1)} %bitcast.73), kind=kOutput, calls=%fused_computation.1 | convolution fusion | flops 8058306560 | bytes 18743296 | tf_op jit(solution)/shard_map/dot_general | solution.py:11
  246.9 120.8 %all_to_all.22 = bf16[16,80,4096]{2,1,0:T(8,128)(2,1)S(1)} all-to-all(bf16[16,80,4096]{2,1,0:T(8,128)(2,1)S(1)} %bitcast.67), channel_id=1, replica_groups=mesh['rep'=16,'exp'=8] {'rep'}, dimensions={0} | all-to-all | bytes 20971520 | tf_op jit(solution)/shard_map/all_to_all | solution.py:68
  367.7 4.0 copy-done
  371.7 0.5 slice.34
  372.9 0.1 copy.49
  373.0 0.1 broadcast_in_dim.112
  373.2 0.1 copy.48
  373.3 0.1 convert_element_type.120
  373.4 16.9 %convolution_convert_fusion.1 = bf16[1024,4096]{1,0:T(8,128)(2,1)} fusion(bf16[1280,4096]{1,0:T(8,128)(2,1)} %bitcast.64, bf16[1280]{0:T(1024)(128)(2,1)S(1)} %broadcast_in_dim.112, s32[1280]{0:T(1024)S(1)} %convert_element_type.120), kind=kOutput, calls=%fused_computation.3 | convolution fusion | flops 10744233984 | bytes 18882048 | tf_op jit(solution)/shard_map/dot_general | solution.py:75
  390.4 51.9 %reduce-scatter.2.cloned.1.call-done = bf16[128,4096]{1,0:T(8,128)(2,1)} async-done(((bf16[1024,4096]{1,0:T(8,128)(2,1)}), bf16[128,4096]{1,0:T(8,128)(2,1)}) %reduce-scatter.2.cloned.1.call-update) | async-done | bytes 1048592 | tf_op jit(solution)/shard_map/reduce_scatter | solution.py:76
  (52 shorter events, 1.9 us)
Async XLA Ops:
  6.5 57.5 %all-gather.2.cloned.1.call-start = ((), (), s32[]{:S(2)}) async-start(), calls=%async_computation.3 | async-start | bytes 9437184 | tf_op jit(solution)/shard_map/all_gather | solution.py:55
  10.6 431.7 %reduce-scatter.2.cloned.1.call-start = ((), (), s32[]{:S(2)}) async-start(), calls=%async_computation.4 | async-start | bytes 9437184 | tf_op jit(solution)/shard_map/reduce_scatter | solution.py:76
  93.4 134.3 %slice-start = ((s8[6291456]{0:T(1024)(128)(4,1)}), s8[4194304]{0:T(1024)(128)(4,1)S(1)}, s32[]{:S(2)}) async-start(s8[6291456]{0:T(1024)(128)(4,1)} %bitcast.70), calls=%async_computation.5 | async-start | bytes 8388608
  93.4 144.6 %slice-start.2 = ((s8[6291456]{0:T(1024)(128)(4,1)}), s8[4194304]{0:T(1024)(128)(4,1)S(1)}, s32[]{:S(2)}) async-start(s8[6291456]{0:T(1024)(128)(4,1)} %bitcast.72), calls=%async_computation.7 | async-start | bytes 8388608
  215.9 11.8 %slice-start.1 = ((s8[6291456]{0:T(1024)(128)(4,1)}), s8[2097152]{0:T(1024)(128)(4,1)S(1)}, s32[]{:S(2)}) async-start(s8[6291456]{0:T(1024)(128)(4,1)} %bitcast.70), calls=%async_computation.6 | async-start | bytes 4194304
  215.9 22.1 %slice-start.3 = ((s8[6291456]{0:T(1024)(128)(4,1)}), s8[2097152]{0:T(1024)(128)(4,1)S(1)}, s32[]{:S(2)}) async-start(s8[6291456]{0:T(1024)(128)(4,1)} %bitcast.72), calls=%async_computation.8 | async-start | bytes 4194304
  367.7 4.0 copy-start
Sparse Core Ops, SparseCore 0:
  10.7 53.2 all-gather.1
  390.5 51.7 reduce-scatter.1

commit v7 on v6

--- a/solution.py
+++ b/solution.py
@@ -52,29 +52,41 @@
     own = hidden.astype(jnp.float32)
     own_scale = lax.rsqrt(jnp.mean(own * own, axis=1, keepdims=True) + 1e-06)
     normed = (own * own_scale * norm_gain).astype(jnp.bfloat16)
-    group = lax.all_gather(normed, "exp", axis=0, tiled=True)
     table_all = lax.all_gather(table.reshape(n_rep, n_exp, cap, 3), "exp", axis=1, tiled=False)
     table_col = lax.dynamic_index_in_dim(table_all, column, axis=2, keepdims=False)
-    row_tbl = table_col[..., 0].astype(jnp.int32)
     src_row = table_col[..., 1].astype(jnp.int32).reshape(-1)
-    w_tbl = table_col[..., 2]
-    filled = (row_tbl >= 0).reshape(-1)
 
-    picked = jnp.take(group, src_row, axis=0)
-    outgoing = jnp.where(filled[:, None], picked, jnp.zeros((), jnp.bfloat16))
-
-    arrived = lax.all_to_all(outgoing, "rep", split_axis=0, concat_axis=0, tiled=True)
-    results = run_expert(arrived, w_gate, w_up, w_down)
-    returned = lax.all_to_all(results, "rep", split_axis=0, concat_axis=0, tiled=True)
-    after = returned[0, 0].astype(jnp.float32) * 0
-    table_post = table_col + after
-    key = table_post[..., 0].astype(jnp.int32).reshape(-1)
-    w_key = table_post[..., 2].reshape(-1)
-    pick = jnp.arange(micro, dtype=jnp.int32)[:, None] == key[None, :]
-    mix = jnp.where(pick, w_key[None, :], 0.0).astype(jnp.bfloat16)
-    partial = jnp.dot(mix, returned, preferred_element_type=jnp.float32)
-    mixed = lax.psum_scatter(partial.astype(jnp.bfloat16), "exp", scatter_dimension=0, tiled=True)
-    return mixed
+    half = width // 2
+    sent = []
+    order = 0
+    for part in range(2):
+        group = lax.all_gather(normed[:, part * half : (part + 1) * half], "exp", axis=0, tiled=True)
+        picked = jnp.take(group, src_row + order, axis=0)
+        sent.append(lax.all_to_all(picked, "rep", split_axis=0, concat_axis=0, tiled=True))
+        order = (sent[-1][0, 0] * 0).astype(jnp.int32)
+    gate_val = jnp.dot(sent[0], w_gate[0, :half], preferred_element_type=jnp.float32)
+    gate_val = gate_val + jnp.dot(sent[1], w_gate[0, half:], preferred_element_type=jnp.float32)
+    up_val = jnp.dot(sent[0], w_up[0, :half], preferred_element_type=jnp.float32)
+    up_val = up_val + jnp.dot(sent[1], w_up[0, half:], preferred_element_type=jnp.float32)
+    act = (jax.nn.silu(gate_val) * up_val).astype(jnp.bfloat16)
+    mixed = []
+    hold = 0.0
+    for part in range(2):
+        results = jnp.dot(act, w_down[0, :, part * half : (part + 1) * half], preferred_element_type=jnp.float32)
+        results = (results + hold).astype(jnp.bfloat16)
+        returned = lax.all_to_all(results, "rep", split_axis=0, concat_axis=0, tiled=True)
+        after = returned[0, 0].astype(jnp.float32) * 0
+        table_post = table_col + after
+        key = table_post[..., 0].astype(jnp.int32).reshape(-1)
+        w_key = table_post[..., 2].reshape(-1)
+        pick = jnp.arange(micro, dtype=jnp.int32)[:, None] == key[None, :]
+        mix = jnp.where(pick, w_key[None, :], 0.0).astype(jnp.bfloat16)
+        partial = jnp.dot(mix, returned, preferred_element_type=jnp.float32)
+        hold = partial[0, 0] * 0
+        mixed.append(
+            lax.psum_scatter(partial.astype(jnp.bfloat16), "exp", scatter_dimension=0, tiled=True)
+        )
+    return jnp.concatenate(mixed, axis=1)
 
 
 def solution(mesh):

time: 453 us -> 468 us (1.033)
  blocking collectives: 260 us -> 216 us
  matrix products: 47.9 us -> 66.4 us
  waiting for transfers between devices: 79 us -> 96.2 us
  local copies, waits for them, and re-layouts: 32 us -> 41.2 us
  starting transfers between devices: 0.04 us -> 8.05 us
    all_to_all x1, blocking collectives: 122 us -> 66 us  [shards(): lax.all_to_all(picked, 'rep', split_axis=0, concat_axis=0, tiled=True)]
    all_to_all x0 -> x1, waiting for transfers between devices: none -> 48.3 us  [shards(): lax.all_to_all(picked, 'rep', split_axis=0, concat_axis=0, tiled=True)]
    reduce_scatter x1 -> x2, waiting for transfers between devices: 51.9 us -> 35.9 us  [shards(): lax.psum_scatter(partial.astype(jnp.bfloat16), 'exp', scatter_dimension=0...]
    all_gather x1 -> x2, waiting for transfers between devices: 27.1 us -> 11.3 us  [shards(): lax.all_gather(normed[:, part * half:(part + 1) * half], 'exp', axis=0, t...]
    dot_general x3 -> x6, matrix products: 31 us -> 45.9 us  [the longest x2 10.9 us: shards(): jnp.dot(act, w_down[0, :, part * half:(part + 1) * half], preferred_eleme...]
    all_to_all x1 -> x2, blocking collectives: 121 us -> 134 us  [shards(): lax.all_to_all(results, 'rep', split_axis=0, concat_axis=0, tiled=True)]
    all_to_all x0 -> x1, starting transfers between devices: none -> 7.93 us  [shards(): lax.all_to_all(picked, 'rep', split_axis=0, concat_axis=0, tiled=True)]
    gather x1 -> x2, local copies, waits for them, and re-layouts: 23.2 us -> 27.1 us  [shards(): picked = jnp.take(group, src_row + order, axis=0)]
  transfers between devices with their start and end apart: 2 -> 5, of which waited for: 2 -> 3; matrix products, arithmetic and copies ran while one was open for 2% -> 13% of each run, Pallas kernels for 0% -> 0%
where the time goes in v7:
time: 468 us; the launch traced here: 463 us
  blocking collectives  216 us (46%)
  waiting for transfers between devices  96.2 us (21%)
  matrix products  66.4 us (14%)
  local copies, waits for them, and re-layouts  41.2 us (9%)
  other arithmetic  17.6 us (4%)
  between operations  16.8 us (4%)
  starting transfers between devices  8.05 us (2%)
    all_to_all x2, blocking collectives, shards(): lax.all_to_all(results, 'rep', split_axis=0, concat_axis=0, tiled=True)  134 us
    all_to_all x1, blocking collectives, shards(): lax.all_to_all(picked, 'rep', split_axis=0, concat_axis=0, tiled=True)  66 us
    all_to_all x1, waiting for transfers between devices, shards(): lax.all_to_all(picked, 'rep', split_axis=0, concat_axis=0, tiled=True)  48.3 us
    reduce_scatter x2, waiting for transfers between devices, shards(): lax.psum_scatter(partial.astype(jnp.bfloat16), 'exp', scatter_dimension=0...  35.9 us
    gather x2, local copies, waits for them, and re-layouts, shards(): picked = jnp.take(group, src_row + order, axis=0)  27.1 us
    dot_general x2, matrix products, shards(): partial = jnp.dot(mix, returned, preferred_element_type=jnp.float32)  20.5 us
    all_gather x1, blocking collectives, shards(): lax.all_gather(table.reshape(n_rep, n_exp, cap, 3), 'exp', axis=1, tiled=...  16.5 us
    all_gather x2, waiting for transfers between devices, shards(): lax.all_gather(normed[:, part * half:(part + 1) * half], 'exp', axis=0, t...  11.3 us
  transfers between devices with their start and end apart: 5, of which 3 were waited for; matrix products, arithmetic and copies ran while one was open for 13% of the time, Pallas kernels for 0%

profile of v7, /device:TPU:50, one launch (start us, length us, event | category | flops | bytes accessed | tf_op | source)
XLA Modules:
  0.0 462.7 jit_solution(8396986245719532596)
XLA Ops:
  6.5 1.6 fusion.23
  8.1 1.6 fusion.25
  9.7 1.1 fusion.41
  10.8 0.7 all-gather.5.cloned.1.call-update
  14.1 0.8 fusion
  14.9 0.7 select_reduce_fusion
  15.9 1.2 select_reduce_fusion.2
  17.7 16.5 %all_gather.9 = f32[16,8,8,10,3]{0,2,4,3,1:T(8,128)S(1)} all-gather(f32[16,1,8,10,3]{0,2,4,3,1:T(8,128)S(1)} %copy.43), channel_id=1, replica_groups=mesh['rep'=16,'exp'=8] {'exp'}, dimensions={1}, use_global_device_ids=true | all-gather | bytes 138240 | tf_op jit(solution)/shard_map/all_gather | solution.py:55
  34.6 11.2 %all-gather.3.cloned.1.call-done = bf16[1024,2048]{1,0:T(8,128)(2,1)} async-done(((bf16[128,2048]{1,0:T(8,128)(2,1)}), bf16[1024,2048]{1,0:T(8,128)(2,1)}) %all-gather.3.cloned.1.call-update) | async-done | bytes 4194320 | tf_op jit(solution)/shard_map/all_gather | solution.py:63
  45.9 13.6 %gather_fusion = bf16[1280,2048]{1,0:T(8,128)(2,1)} fusion(bf16[1024,2048]{1,0:T(8,128)(2,1)} %all-gather.3.cloned.1.call-done, s32[2048]{0:T(1024)S(1)} %pad_clamp_fusion.1), kind=kCustom, calls=%fused_computation.clone | custom fusion | bytes 10490880 | tf_op jit(solution)/shard_map/jit(_take)/gather | solution.py:64
  59.4 3.1 broadcast_select_fusion.1
  62.5 66.0 %all_to_all.48 = bf16[16,80,2048]{2,1,0:T(8,128)(2,1)S(1)} all-to-all(bf16[16,80,2048]{2,1,0:T(8,128)(2,1)S(1)} %bitcast.82), channel_id=1, replica_groups=mesh['rep'=16,'exp'=8] {'rep'}, dimensions={0} | all-to-all | bytes 10485760 | tf_op jit(solution)/shard_map/all_to_all | solution.py:65
  128.5 2.3 copy-done
  132.1 13.6 %gather_fusion.1 = bf16[1280,2048]{1,0:T(8,128)(2,1)} fusion(bf16[1024,2048]{1,0:T(8,128)(2,1)} %all-gather.5.cloned.1.call-done, s32[2048]{0:T(1024)S(1)} %pad_clamp_fusion), kind=kCustom, calls=%fused_computation.1.clone | custom fusion | bytes 10490880 | tf_op jit(solution)/shard_map/jit(_take)/gather | solution.py:64
  145.7 5.4 %broadcast_select_fusion = bf16[1280,2048]{1,0:T(8,128)(2,1)} fusion(bf16[1280,2048]{1,0:T(8,128)(2,1)} %gather_fusion.1, pred[1280]{0:T(1024)(128)(4,1)S(1)} %get-tuple-element.8), kind=kLoop, calls=%fused_computation.13 | loop fusion | flops 2621440 | bytes 10487040 | tf_op jit(solution)/shard_map/jit(_take)/select_n | solution.py:64
  151.1 7.9 %all-to-all-start.1 = ((bf16[16,80,2048]{2,1,0:T(8,128)(2,1)}), bf16[16,80,2048]{2,1,0:T(8,128)(2,1)}, u32[]{:S(2)}, u32[]{:S(2)}) async-start(bf16[16,80,2048]{2,1,0:T(8,128)(2,1)} %bitcast.81), calls=%async_computation.1 | async-start | bytes 10485760 | tf_op jit(solution)/shard_map/all_to_all | solution.py:65
  159.0 9.6 %fusion.4 = f32[1280,768]{1,0:T(8,128)} fusion(bf16[1280,2048]{1,0:T(8,128)(2,1)} %bitcast.84, bf16[1,4096,768]{2,1,0:T(8,128)(2,1)} %param.18), kind=kOutput, calls=%fused_computation.20 | convolution fusion | flops 4026531840 | bytes 12320768 | tf_op jit(solution)/shard_map/dot_general | solution.py:69
  168.6 9.6 %fusion.8 = f32[1280,768]{1,0:T(8,128)} fusion(bf16[1280,2048]{1,0:T(8,128)(2,1)} %bitcast.85, bf16[1,4096,768]{2,1,0:T(8,128)(2,1)} %param.17), kind=kOutput, calls=%fused_computation.24 | convolution fusion | flops 4026531840 | bytes 12320768 | tf_op jit(solution)/shard_map/dot_general | solution.py:67
  178.3 48.3 %all-to-all-done.1 = bf16[16,80,2048]{2,1,0:T(8,128)(2,1)} async-done(((bf16[16,80,2048]{2,1,0:T(8,128)(2,1)}), bf16[16,80,2048]{2,1,0:T(8,128)(2,1)}, u32[]{:S(2)}, u32[]{:S(2)}) %all-to-all-start.1) | async-done | bytes 5242912 | tf_op jit(solution)/shard_map/all_to_all | solution.py:65
  226.5 7.5 %fusion.6 = f32[1280,768]{1,0:T(8,128)S(1)} fusion(bf16[1280,2048]{1,0:T(8,128)(2,1)} %bitcast.11, bf16[1,4096,768]{2,1,0:T(8,128)(2,1)} %param.17), kind=kOutput, calls=%fused_computation.22 | convolution fusion | flops 4026531840 | bytes 12320768 | tf_op jit(solution)/shard_map/dot_general | solution.py:68
  234.0 8.4 %multiply_convert_fusion = bf16[1280,768]{1,0:T(8,128)(2,1)S(1)} fusion(f32[1280,768]{1,0:T(8,128)S(1)} %copy-done.6, f32[1280,768]{1,0:T(8,128)S(1)} %copy-done.7, f32[1280,768]{1,0:T(8,128)S(1)} %fusion.6, bf16[1280,2048]{1,0:T(8,128)(2,1)} %bitcast.11, bf16[1,4096,768]{2,1,0:T(8,128)(2,1)} %param.18), kind=kOutput, calls=%fused_computation.15 | convolution fusion | flops 4034396160 | bytes 22151168 | tf_op jit(solution)/shard_map/dot_general | solution.py:70
  242.5 4.5 convolution_convert_fusion
  247.0 68.8 %all_to_all.49 = bf16[16,80,2048]{2,1,0:T(8,128)(2,1)S(1)} all-to-all(bf16[16,80,2048]{2,1,0:T(8,128)(2,1)S(1)} %bitcast.91), channel_id=1, replica_groups=mesh['rep'=16,'exp'=8] {'rep'}, dimensions={0} | all-to-all | bytes 10485760 | tf_op jit(solution)/shard_map/all_to_all | solution.py:77
  315.8 2.4 copy-done.1
  319.9 10.9 %fusion.42 = (bf16[1024,2048]{1,0:T(8,128)(2,1)}, f32[1024,2048]{1,0:T(8,128)}) fusion(bf16[1280,2048]{1,0:T(8,128)(2,1)} %bitcast.87, bf16[1280]{0:T(1024)(128)(2,1)S(1)} %broadcast_in_dim.104, s32[1280]{0:T(1024)S(1)} %convert_element_type.128), kind=kOutput, calls=%fused_computation.90 | convolution fusion | flops 5373427712 | bytes 17833472 | tf_op jit(solution)/shard_map/dot_general | solution.py:84
  330.9 1.2 slice.89
  332.7 6.4 %add_convert_fusion = bf16[1280,2048]{1,0:T(8,128)(2,1)S(1)} fusion(bf16[1280,768]{1,0:T(8,128)(2,1)S(1)} %multiply_convert_fusion, f32[]{:T(128)} %bitcast.20, bf16[1,768,4096]{2,1,0:T(8,128)(2,1)} %param.19), kind=kOutput, calls=%fused_computation.2 | convolution fusion | flops 4031774720 | bytes 10355200 | tf_op jit(solution)/shard_map/dot_general | solution.py:75
  339.1 65.1 %all_to_all.50 = bf16[16,80,2048]{2,1,0:T(8,128)(2,1)S(1)} all-to-all(bf16[16,80,2048]{2,1,0:T(8,128)(2,1)S(1)} %bitcast.90), channel_id=1, replica_groups=mesh['rep'=16,'exp'=8] {'rep'}, dimensions={0} | all-to-all | bytes 10485760 | tf_op jit(solution)/shard_map/all_to_all | solution.py:77
  404.1 2.3 copy-done.2
  408.2 9.7 %convolution_convert_fusion.1 = bf16[1024,2048]{1,0:T(8,128)(2,1)} fusion(bf16[1280,2048]{1,0:T(8,128)(2,1)} %bitcast.89, bf16[1280]{0:T(1024)(128)(2,1)S(1)} %broadcast_in_dim.106, s32[1280]{0:T(1024)S(1)} %convert_element_type.134), kind=kOutput, calls=%fused_computation.16 | convolution fusion | flops 5373427712 | bytes 9444864 | tf_op jit(solution)/shard_map/dot_general | solution.py:84
  417.9 35.9 %reduce-scatter.5.cloned.1.call-done = bf16[128,2048]{1,0:T(8,128)(2,1)} async-done(((bf16[1024,2048]{1,0:T(8,128)(2,1)}), bf16[128,2048]{1,0:T(8,128)(2,1)}) %reduce-scatter.5.cloned.1.call-update) | async-done | bytes 524304 | tf_op jit(solution)/shard_map/reduce_scatter | solution.py:87
  453.9 2.3 pad_maximum_fusion
  (86 shorter events, 6.1 us)
Async XLA Ops:
  6.5 5.0 %copy-start.4 = (s32[128,8]{0,1:T(8,128)S(1)}, s32[128,8]{0,1:T(8,128)}, u32[]{:S(2)}) copy-start(s32[128,8]{0,1:T(8,128)} %param.13) | copy-start | bytes 12292
  6.5 6.0 %copy-start.3 = (f32[128,8]{0,1:T(8,128)S(1)}, f32[128,8]{0,1:T(8,128)}, u32[]{:S(2)}) copy-start(f32[128,8]{0,1:T(8,128)} %param.14) | copy-start | bytes 12292
  6.5 9.2 %copy-start.5 = (s32[128]{0:T(128)S(1)}, s32[128]{0:T(128)}, u32[]{:S(2)}) copy-start(s32[128]{0:T(128)} %param.12) | copy-start | bytes 1540
  6.5 39.3 %all-gather.3.cloned.1.call-start = ((), (), s32[]{:S(2)}) async-start(), calls=%async_computation.6 | async-start | bytes 4718592 | tf_op jit(solution)/shard_map/all_gather | solution.py:63
  10.8 121.3 %all-gather.5.cloned.1.call-start = ((), (), s32[]{:S(2)}) async-start(), calls=%async_computation.7 | async-start | bytes 4718592 | tf_op jit(solution)/shard_map/all_gather | solution.py:63
  128.5 2.3 copy-start
  151.1 75.5 %all-to-all-start.1 = ((bf16[16,80,2048]{2,1,0:T(8,128)(2,1)}), bf16[16,80,2048]{2,1,0:T(8,128)(2,1)}, u32[]{:S(2)}, u32[]{:S(2)}) async-start(bf16[16,80,2048]{2,1,0:T(8,128)(2,1)} %bitcast.81), calls=%async_computation.1 | async-start | bytes 10485760 | tf_op jit(solution)/shard_map/all_to_all | solution.py:65
  159.0 258.9 %reduce-scatter.3.cloned.1.call-start = ((), (), s32[]{:S(2)}) async-start(), calls=%async_computation.8 | async-start | bytes 4718592 | tf_op jit(solution)/shard_map/reduce_scatter | solution.py:87
  226.5 7.5 %copy-start.6 = (f32[1280,768]{1,0:T(8,128)S(1)}, f32[1280,768]{1,0:T(8,128)}, u32[]{:S(2)}) copy-start(f32[1280,768]{1,0:T(8,128)} %fusion.4) | copy-start | bytes 11796484
  226.5 7.5 %copy-start.7 = (f32[1280,768]{1,0:T(8,128)S(1)}, f32[1280,768]{1,0:T(8,128)}, u32[]{:S(2)}) copy-start(f32[1280,768]{1,0:T(8,128)} %fusion.8) | copy-start | bytes 11796484
  226.5 15.9 %slice-start = ((s8[6291456]{0:T(1024)(128)(4,1)}), s8[4194304]{0:T(1024)(128)(4,1)S(1)}, s32[]{:S(2)}) async-start(s8[6291456]{0:T(1024)(128)(4,1)} %bitcast.93), calls=%async_computation.10 | async-start | bytes 8388608
  234.0 8.4 %slice-start.1 = ((s8[6291456]{0:T(1024)(128)(4,1)}), s8[2097152]{0:T(1024)(128)(4,1)S(1)}, s32[]{:S(2)}) async-start(s8[6291456]{0:T(1024)(128)(4,1)} %bitcast.93), calls=%async_computation.11 | async-start | bytes 4194304
  315.8 2.4 copy-start.1
  330.8 123.0 %reduce-scatter.5.cloned.1.call-start = ((), (), s32[]{:S(2)}) async-start(), calls=%async_computation.9 | async-start | bytes 4718592 | tf_op jit(solution)/shard_map/reduce_scatter | solution.py:87
  404.1 2.3 copy-start.2
Sparse Core Ops, SparseCore 0:
  10.9 34.9 all-gather.2
  47.6 32.4 all-gather.4
  330.9 35.8 reduce-scatter.2
  418.0 35.7 reduce-scatter.4

commit v8 on v6

--- a/solution.py
+++ b/solution.py
@@ -60,8 +60,9 @@
     w_tbl = table_col[..., 2]
     filled = (row_tbl >= 0).reshape(-1)
 
-    picked = jnp.take(group, src_row, axis=0)
-    outgoing = jnp.where(filled[:, None], picked, jnp.zeros((), jnp.bfloat16))
+    src_key = jnp.where(filled, src_row, -1)
+    choose = (src_key[:, None] == jnp.arange(micro, dtype=jnp.int32)[None, :]).astype(jnp.bfloat16)
+    outgoing = jnp.dot(choose, group, preferred_element_type=jnp.float32).astype(jnp.bfloat16)
 
     arrived = lax.all_to_all(outgoing, "rep", split_axis=0, concat_axis=0, tiled=True)
     results = run_expert(arrived, w_gate, w_up, w_down)

time: 453 us -> 441 us (0.974)
  local copies, waits for them, and re-layouts: 32 us -> 8.45 us
  matrix products: 47.9 us -> 65.2 us
  other arithmetic: 15.3 us -> 9.11 us
    gather x1 -> x0, local copies, waits for them, and re-layouts: 23.2 us -> none  [shards(): picked = jnp.take(group, src_row, axis=0)]
    dot_general x0 -> x1, matrix products: none -> 15.2 us  [shards(): jnp.dot(choose, group, preferred_element_type=jnp.float32)]
    select_n x2 -> x1, other arithmetic: 6.16 us -> 0.01 us  [shards(): src_key = jnp.where(filled, src_row, -1)]
where the time goes in v8:
time: 441 us; the launch traced here: 437 us
  blocking collectives  260 us (59%)
  waiting for transfers between devices  79.4 us (18%)
  matrix products  65.2 us (15%)
  between operations  15 us (3%)
  other arithmetic  9.11 us (2%)
  local copies, waits for them, and re-layouts  8.45 us (2%)
    all_to_all x1, blocking collectives, shards(): lax.all_to_all(outgoing, 'rep', split_axis=0, concat_axis=0, tiled=True)  122 us
    all_to_all x1, blocking collectives, shards(): lax.all_to_all(results, 'rep', split_axis=0, concat_axis=0, tiled=True)  121 us
    reduce_scatter x1, waiting for transfers between devices, shards(): lax.psum_scatter(partial.astype(jnp.bfloat16), 'exp', scatter_dimension=0...  51.9 us
    all_gather x1, waiting for transfers between devices, shards(): group = lax.all_gather(normed, 'exp', axis=0, tiled=True)  27.5 us
    dot_general x1, matrix products, shards(): partial = jnp.dot(mix, returned, preferred_element_type=jnp.float32)  16.9 us
    all_gather x1, blocking collectives, shards(): lax.all_gather(table.reshape(n_rep, n_exp, cap, 3), 'exp', axis=1, tiled=...  16.6 us
    dot_general x1, matrix products, shards(): jnp.dot(choose, group, preferred_element_type=jnp.float32)  15.2 us
    dot_general x1, matrix products, run_expert(): gate_val = jnp.dot(arrived, w_gate[0], preferred_element_type=jnp.float32)  12.4 us
  transfers between devices with their start and end apart: 2, of which 2 were waited for; matrix products, arithmetic and copies ran while one was open for 2% of the time, Pallas kernels for 0%

profile of v8, /device:TPU:50, one launch (start us, length us, event | category | flops | bytes accessed | tf_op | source)
XLA Modules:
  0.0 437.2 jit_solution(6877020377310681667)
XLA Ops:
  6.5 1.5 fusion.16
  8.1 2.5 fusion.18
  10.7 0.8 copy.34
  12.5 0.7 reduce_sum.57
  13.2 0.7 divide_multiply_fusion
  14.2 0.7 broadcast_in_dim.85
  15.1 0.3 fusion.21
  15.6 0.5 fusion.20
  16.2 1.2 select_reduce_fusion.2
  17.4 0.1 convert_element_type.102
  17.5 0.8 fusion.5
  18.3 0.1 convert_element_type.100
  18.5 0.7 select_reduce_fusion
  19.3 0.2 copy.39
  19.5 16.6 %all_gather.6 = f32[16,8,8,10,3]{0,2,4,3,1:T(8,128)S(1)} all-gather(f32[16,1,8,10,3]{0,2,4,3,1:T(8,128)S(1)} %copy.39), channel_id=1, replica_groups=mesh['rep'=16,'exp'=8] {'exp'}, dimensions={1}, use_global_device_ids=true | all-gather | bytes 138240 | tf_op jit(solution)/shard_map/all_gather | solution.py:56
  36.2 0.1 copy.41
  36.4 0.1 select_n.67
  36.5 27.5 %all-gather.2.cloned.1.call-done = bf16[1024,4096]{1,0:T(8,128)(2,1)} async-done(((bf16[128,4096]{1,0:T(8,128)(2,1)}), bf16[1024,4096]{1,0:T(8,128)(2,1)}) %all-gather.2.cloned.1.call-update) | async-done | bytes 8388624 | tf_op jit(solution)/shard_map/all_gather | solution.py:55
  64.0 15.2 %convolution_convert_fusion.1 = bf16[1280,4096]{1,0:T(8,128)(2,1)S(1)} fusion(bf16[1024,4096]{1,0:T(8,128)(2,1)} %all-gather.2.cloned.1.call-done, s32[1280]{0:T(1024)S(1)} %select_n.67), kind=kOutput, calls=%fused_computation.1 | convolution fusion | flops 10743971840 | bytes 18879488 | tf_op jit(solution)/shard_map/dot_general | solution.py:65
  79.2 122.3 %all_to_all.24 = bf16[16,80,4096]{2,1,0:T(8,128)(2,1)S(1)} all-to-all(bf16[16,80,4096]{2,1,0:T(8,128)(2,1)S(1)} %bitcast.57), channel_id=1, replica_groups=mesh['rep'=16,'exp'=8] {'rep'}, dimensions={0} | all-to-all | bytes 20971520 | tf_op jit(solution)/shard_map/all_to_all | solution.py:67
  201.5 12.4 %fusion.3 = f32[1280,768]{1,0:T(8,128)S(1)} fusion(bf16[1280,4096]{1,0:T(8,128)(2,1)S(1)} %bitcast.58, bf16[1,4096,768]{2,1,0:T(8,128)(2,1)} %param.15), kind=kOutput, calls=%fused_computation.6 | convolution fusion | flops 8053063680 | bytes 20709376 | tf_op jit(solution)/shard_map/dot_general | solution.py:8
  214.0 9.0 %fusion.9 = bf16[1280,768]{1,0:T(8,128)(2,1)S(1)} fusion(bf16[1280,4096]{1,0:T(8,128)(2,1)S(1)} %bitcast.59, bf16[1,4096,768]{2,1,0:T(8,128)(2,1)S(1)} %bitcast.63, f32[1280,768]{1,0:T(8,128)S(1)} %fusion.3), kind=kOutput, calls=%fused_computation.17 | convolution fusion | flops 8058961920 | bytes 22675456 | tf_op jit(solution)/shard_map/dot_general | solution.py:9
  223.0 11.7 %convolution_convert_fusion = bf16[1280,4096]{1,0:T(8,128)(2,1)S(1)} fusion(bf16[1280,768]{1,0:T(8,128)(2,1)S(1)} %fusion.9, bf16[1,768,4096]{2,1,0:T(8,128)(2,1)} %param.17), kind=kOutput, calls=%fused_computation | convolution fusion | flops 8058306560 | bytes 18743296 | tf_op jit(solution)/shard_map/dot_general | solution.py:11
  234.7 121.0 %all_to_all.25 = bf16[16,80,4096]{2,1,0:T(8,128)(2,1)S(1)} all-to-all(bf16[16,80,4096]{2,1,0:T(8,128)(2,1)S(1)} %bitcast.60), channel_id=1, replica_groups=mesh['rep'=16,'exp'=8] {'rep'}, dimensions={0} | all-to-all | bytes 20971520 | tf_op jit(solution)/shard_map/all_to_all | solution.py:69
  355.7 4.0 copy-done
  359.7 0.5 slice.32
  360.9 0.1 copy.43
  361.1 0.1 broadcast_in_dim.92
  361.2 0.1 copy.42
  361.4 0.1 convert_element_type.113
  361.5 16.9 %convolution_convert_fusion.2 = bf16[1024,4096]{1,0:T(8,128)(2,1)} fusion(bf16[1280,4096]{1,0:T(8,128)(2,1)} %bitcast.56, bf16[1280]{0:T(1024)(128)(2,1)S(1)} %broadcast_in_dim.92, s32[1280]{0:T(1024)S(1)} %convert_element_type.113), kind=kOutput, calls=%fused_computation.2 | convolution fusion | flops 10744233984 | bytes 18882048 | tf_op jit(solution)/shard_map/dot_general | solution.py:76
  378.4 51.9 %reduce-scatter.2.cloned.1.call-done = bf16[128,4096]{1,0:T(8,128)(2,1)} async-done(((bf16[1024,4096]{1,0:T(8,128)(2,1)}), bf16[128,4096]{1,0:T(8,128)(2,1)}) %reduce-scatter.2.cloned.1.call-update) | async-done | bytes 1048592 | tf_op jit(solution)/shard_map/reduce_scatter | solution.py:77
  (39 shorter events, 1.4 us)
Async XLA Ops:
  6.5 57.5 %all-gather.2.cloned.1.call-start = ((), (), s32[]{:S(2)}) async-start(), calls=%async_computation.3 | async-start | bytes 9437184 | tf_op jit(solution)/shard_map/all_gather | solution.py:55
  10.6 419.7 %reduce-scatter.2.cloned.1.call-start = ((), (), s32[]{:S(2)}) async-start(), calls=%async_computation.4 | async-start | bytes 9437184 | tf_op jit(solution)/shard_map/reduce_scatter | solution.py:77
  79.2 134.8 %slice-start = ((s8[6291456]{0:T(1024)(128)(4,1)}), s8[2097152]{0:T(1024)(128)(4,1)S(1)}, s32[]{:S(2)}) async-start(s8[6291456]{0:T(1024)(128)(4,1)} %bitcast.62), calls=%async_computation.5 | async-start | bytes 4194304
  201.5 12.5 %slice-start.1 = ((s8[6291456]{0:T(1024)(128)(4,1)}), s8[4194304]{0:T(1024)(128)(4,1)S(1)}, s32[]{:S(2)}) async-start(s8[6291456]{0:T(1024)(128)(4,1)} %bitcast.62), calls=%async_computation.6 | async-start | bytes 8388608
  355.7 4.0 copy-start
Sparse Core Ops, SparseCore 0:
  10.7 53.2 all-gather.1
  378.5 51.7 reduce-scatter.1

commit v9 on v8

--- a/solution.py
+++ b/solution.py
@@ -62,17 +62,17 @@
 
     src_key = jnp.where(filled, src_row, -1)
     choose = (src_key[:, None] == jnp.arange(micro, dtype=jnp.int32)[None, :]).astype(jnp.bfloat16)
-    outgoing = jnp.dot(choose, group, preferred_element_type=jnp.float32).astype(jnp.bfloat16)
+    key = table_col[..., 0].astype(jnp.int32).reshape(-1)
+    w_key = table_col[..., 2].reshape(-1)
+    pick = jnp.arange(micro, dtype=jnp.int32)[:, None] == key[None, :]
+    mix = jnp.where(pick, w_key[None, :], 0.0).astype(jnp.bfloat16)
+    outgoing = jnp.dot(choose, group, preferred_element_type=jnp.float32) + jnp.sum(mix) * 0
+    outgoing = outgoing.astype(jnp.bfloat16)
 
     arrived = lax.all_to_all(outgoing, "rep", split_axis=0, concat_axis=0, tiled=True)
     results = run_expert(arrived, w_gate, w_up, w_down)
+    results = results + jnp.sum(mix) * 0
     returned = lax.all_to_all(results, "rep", split_axis=0, concat_axis=0, tiled=True)
-    after = returned[0, 0].astype(jnp.float32) * 0
-    table_post = table_col + after
-    key = table_post[..., 0].astype(jnp.int32).reshape(-1)
-    w_key = table_post[..., 2].reshape(-1)
-    pick = jnp.arange(micro, dtype=jnp.int32)[:, None] == key[None, :]
-    mix = jnp.where(pick, w_key[None, :], 0.0).astype(jnp.bfloat16)
     partial = jnp.dot(mix, returned, preferred_element_type=jnp.float32)
     mixed = lax.psum_scatter(partial.astype(jnp.bfloat16), "exp", scatter_dimension=0, tiled=True)
     return mixed

time: 441 us -> 431 us (0.977)
  local copies, waits for them, and re-layouts: 8.45 us -> 3.95 us
  transfers between devices with their start and end apart: 2 -> 2, of which waited for: 2 -> 2; matrix products, arithmetic and copies ran while one was open for 2% -> 3% of each run, Pallas kernels for 0% -> 0%
where the time goes in v9:
time: 431 us; the launch traced here: 428 us
  blocking collectives  260 us (60%)
  waiting for transfers between devices  76.4 us (18%)
  matrix products  61.3 us (14%)
  between operations  14.9 us (3%)
  other arithmetic  11 us (3%)
    all_to_all x1, blocking collectives, shards(): lax.all_to_all(outgoing, 'rep', split_axis=0, concat_axis=0, tiled=True)  122 us
    all_to_all x1, blocking collectives, shards(): lax.all_to_all(results, 'rep', split_axis=0, concat_axis=0, tiled=True)  121 us
    reduce_scatter x1, waiting for transfers between devices, shards(): lax.psum_scatter(partial.astype(jnp.bfloat16), 'exp', scatter_dimension=0...  52 us
    all_gather x1, waiting for transfers between devices, shards(): group = lax.all_gather(normed, 'exp', axis=0, tiled=True)  24.4 us
    all_gather x1, blocking collectives, shards(): lax.all_gather(table.reshape(n_rep, n_exp, cap, 3), 'exp', axis=1, tiled=...  16.6 us
    dot_general x1, matrix products, shards(): jnp.dot(choose, group, preferred_element_type=jnp.float32)  15.2 us
    dot_general x1, matrix products, shards(): partial = jnp.dot(mix, returned, preferred_element_type=jnp.float32)  13 us
    dot_general x1, matrix products, run_expert(): gate_val = jnp.dot(arrived, w_gate[0], preferred_element_type=jnp.float32)  12.4 us
  transfers between devices with their start and end apart: 2, of which 2 were waited for; matrix products, arithmetic and copies ran while one was open for 3% of the time, Pallas kernels for 0%

profile of v9, /device:TPU:50, one launch (start us, length us, event | category | flops | bytes accessed | tf_op | source)
XLA Modules:
  0.0 427.5 jit_solution(13935767860841936532)
XLA Ops:
  6.5 1.5 fusion.18
  8.1 2.5 fusion.20
  10.7 0.8 copy.34
  12.5 0.7 reduce_sum.73
  13.2 0.7 divide_multiply_fusion
  14.2 0.7 broadcast_in_dim.83
  15.1 0.3 fusion.23
  15.6 0.5 fusion.22
  16.2 1.2 select_reduce_fusion.2
  17.4 0.1 convert_element_type.104
  17.5 0.8 fusion.6
  18.3 0.1 convert_element_type.102
  18.5 0.7 select_reduce_fusion
  19.1 0.1 stack.8
  19.3 0.2 copy.39
  19.5 16.6 %all_gather.6 = f32[16,8,8,10,3]{0,2,4,3,1:T(8,128)S(1)} all-gather(f32[16,1,8,10,3]{0,2,4,3,1:T(8,128)S(1)} %copy.39), channel_id=1, replica_groups=mesh['rep'=16,'exp'=8] {'exp'}, dimensions={1}, use_global_device_ids=true | all-gather | bytes 138240 | tf_op jit(solution)/shard_map/all_gather | solution.py:56
  36.2 0.1 copy.42
  36.4 0.1 broadcast_in_dim.89
  36.6 0.1 copy.43
  36.7 0.1 convert_element_type.110
  36.8 0.1 copy.41
  37.0 0.1 convert_element_type.107
  37.1 1.9 fusion.13
  39.6 24.4 %all-gather.2.cloned.1.call-done = bf16[1024,4096]{1,0:T(8,128)(2,1)} async-done(((bf16[128,4096]{1,0:T(8,128)(2,1)}), bf16[1024,4096]{1,0:T(8,128)(2,1)}) %all-gather.2.cloned.1.call-update) | async-done | bytes 8388624 | tf_op jit(solution)/shard_map/all_gather | solution.py:55
  64.0 15.2 %add_convert_fusion = bf16[1280,4096]{1,0:T(8,128)(2,1)S(1)} fusion(bf16[1024,4096]{1,0:T(8,128)(2,1)} %all-gather.2.cloned.1.call-done, f32[]{:T(128)S(6)} %convert_element_type.113, s32[1280]{0:T(1024)S(1)} %compare_select_fusion), kind=kOutput, calls=%fused_computation | convolution fusion | flops 10749214720 | bytes 18879492 | tf_op jit(solution)/shard_map/dot_general | solution.py:69
  79.2 122.3 %all_to_all.24 = bf16[16,80,4096]{2,1,0:T(8,128)(2,1)S(1)} all-to-all(bf16[16,80,4096]{2,1,0:T(8,128)(2,1)S(1)} %bitcast.52), channel_id=1, replica_groups=mesh['rep'=16,'exp'=8] {'rep'}, dimensions={0} | all-to-all | bytes 20971520 | tf_op jit(solution)/shard_map/all_to_all | solution.py:72
  201.5 12.4 %fusion.4 = f32[1280,768]{1,0:T(8,128)S(1)} fusion(bf16[1280,4096]{1,0:T(8,128)(2,1)S(1)} %bitcast.54, bf16[1,4096,768]{2,1,0:T(8,128)(2,1)} %param.15), kind=kOutput, calls=%fused_computation.7 | convolution fusion | flops 8053063680 | bytes 20709376 | tf_op jit(solution)/shard_map/dot_general | solution.py:8
  214.0 9.0 %fusion.10 = bf16[1280,768]{1,0:T(8,128)(2,1)S(1)} fusion(bf16[1280,4096]{1,0:T(8,128)(2,1)S(1)} %bitcast.55, bf16[1,4096,768]{2,1,0:T(8,128)(2,1)S(1)} %bitcast.60, f32[1280,768]{1,0:T(8,128)S(1)} %fusion.4), kind=kOutput, calls=%fused_computation.18 | convolution fusion | flops 8058961920 | bytes 22675456 | tf_op jit(solution)/shard_map/dot_general | solution.py:9
  223.0 11.7 %fusion = bf16[1280,4096]{1,0:T(8,128)(2,1)S(1)} fusion(bf16[1280,768]{1,0:T(8,128)(2,1)S(1)} %fusion.10, bf16[1,768,4096]{2,1,0:T(8,128)(2,1)} %param.17, bf16[]{:T(256)S(6)} %mul.65), kind=kOutput, calls=%fused_computation.2 | convolution fusion | flops 8063549440 | bytes 18743298 | tf_op jit(solution)/shard_map/dot_general | solution.py:11
  234.7 121.0 %all_to_all.25 = bf16[16,80,4096]{2,1,0:T(8,128)(2,1)S(1)} all-to-all(bf16[16,80,4096]{2,1,0:T(8,128)(2,1)S(1)} %bitcast.56), channel_id=1, replica_groups=mesh['rep'=16,'exp'=8] {'rep'}, dimensions={0} | all-to-all | bytes 20971520 | tf_op jit(solution)/shard_map/all_to_all | solution.py:75
  355.7 13.0 %convolution_convert_fusion.1 = bf16[1024,4096]{1,0:T(8,128)(2,1)} fusion(bf16[1280,4096]{1,0:T(8,128)(2,1)S(1)} %bitcast.53, bf16[1280]{0:T(1024)(128)(2,1)S(1)} %broadcast_in_dim.89, s32[1280]{0:T(1024)S(1)} %convert_element_type.107), kind=kOutput, calls=%fused_computation.3 | convolution fusion | flops 10744233984 | bytes 18882048 | tf_op jit(solution)/shard_map/dot_general | solution.py:76
  368.7 52.0 %reduce-scatter.2.cloned.1.call-done = bf16[128,4096]{1,0:T(8,128)(2,1)} async-done(((bf16[1024,4096]{1,0:T(8,128)(2,1)}), bf16[128,4096]{1,0:T(8,128)(2,1)}) %reduce-scatter.2.cloned.1.call-update) | async-done | bytes 1048592 | tf_op jit(solution)/shard_map/reduce_scatter | solution.py:77
  (36 shorter events, 1.2 us)
Async XLA Ops:
  6.5 57.5 %all-gather.2.cloned.1.call-start = ((), (), s32[]{:S(2)}) async-start(), calls=%async_computation.3 | async-start | bytes 9437184 | tf_op jit(solution)/shard_map/all_gather | solution.py:55
  10.6 410.1 %reduce-scatter.2.cloned.1.call-start = ((), (), s32[]{:S(2)}) async-start(), calls=%async_computation.4 | async-start | bytes 9437184 | tf_op jit(solution)/shard_map/reduce_scatter | solution.py:77
  79.2 134.8 %slice-start = ((s8[6291456]{0:T(1024)(128)(4,1)}), s8[2097152]{0:T(1024)(128)(4,1)S(1)}, s32[]{:S(2)}) async-start(s8[6291456]{0:T(1024)(128)(4,1)} %bitcast.59), calls=%async_computation.5 | async-start | bytes 4194304
  201.5 12.5 %slice-start.1 = ((s8[6291456]{0:T(1024)(128)(4,1)}), s8[4194304]{0:T(1024)(128)(4,1)S(1)}, s32[]{:S(2)}) async-start(s8[6291456]{0:T(1024)(128)(4,1)} %bitcast.59), calls=%async_computation.6 | async-start | bytes 8388608
Sparse Core Ops, SparseCore 0:
  10.7 53.2 all-gather.1
  368.9 51.7 reduce-scatter.1

commit v10 on v9

--- a/solution.py
+++ b/solution.py
@@ -62,6 +62,7 @@
 
     src_key = jnp.where(filled, src_row, -1)
     choose = (src_key[:, None] == jnp.arange(micro, dtype=jnp.int32)[None, :]).astype(jnp.bfloat16)
+    choose = lax.optimization_barrier(choose)
     key = table_col[..., 0].astype(jnp.int32).reshape(-1)
     w_key = table_col[..., 2].reshape(-1)
     pick = jnp.arange(micro, dtype=jnp.int32)[:, None] == key[None, :]

time: 431 us -> 429 us (level)
  no operation moved by 1% of the time
where the time goes in v10:
time: 429 us; the launch traced here: 426 us
  blocking collectives  260 us (61%)
  waiting for transfers between devices  75.8 us (18%)
  matrix products  59.6 us (14%)
  between operations  14.9 us (3%)
  other arithmetic  11.5 us (3%)
    all_to_all x1, blocking collectives, shards(): lax.all_to_all(outgoing, 'rep', split_axis=0, concat_axis=0, tiled=True)  122 us
    all_to_all x1, blocking collectives, shards(): lax.all_to_all(results, 'rep', split_axis=0, concat_axis=0, tiled=True)  121 us
    reduce_scatter x1, waiting for transfers between devices, shards(): lax.psum_scatter(partial.astype(jnp.bfloat16), 'exp', scatter_dimension=0...  51.9 us
    all_gather x1, waiting for transfers between devices, shards(): group = lax.all_gather(normed, 'exp', axis=0, tiled=True)  23.9 us
    all_gather x1, blocking collectives, shards(): lax.all_gather(table.reshape(n_rep, n_exp, cap, 3), 'exp', axis=1, tiled=...  16.6 us
    dot_general x1, matrix products, shards(): jnp.dot(choose, group, preferred_element_type=jnp.float32)  13.4 us
    dot_general x1, matrix products, shards(): partial = jnp.dot(mix, returned, preferred_element_type=jnp.float32)  13 us
    dot_general x1, matrix products, run_expert(): gate_val = jnp.dot(arrived, w_gate[0], preferred_element_type=jnp.float32)  12.4 us
  transfers between devices with their start and end apart: 2, of which 2 were waited for; matrix products, arithmetic and copies ran while one was open for 3% of the time, Pallas kernels for 0%

profile of v10, /device:TPU:50, one launch (start us, length us, event | category | flops | bytes accessed | tf_op | source)
XLA Modules:
  0.0 425.8 jit_solution(10453354141405701714)
XLA Ops:
  6.5 1.5 fusion.18
  8.1 2.5 fusion.20
  10.7 0.8 copy.34
  12.5 0.7 reduce_sum.73
  13.2 0.7 divide_multiply_fusion
  14.2 0.7 broadcast_in_dim.83
  15.1 0.3 fusion.23
  15.6 0.5 fusion.22
  16.2 1.2 select_reduce_fusion.2
  17.4 0.1 convert_element_type.106
  17.5 0.8 fusion.6
  18.3 0.1 convert_element_type.104
  18.5 0.7 select_reduce_fusion
  19.3 0.2 copy.39
  19.5 16.6 %all_gather.6 = f32[16,8,8,10,3]{0,2,4,3,1:T(8,128)S(1)} all-gather(f32[16,1,8,10,3]{0,2,4,3,1:T(8,128)S(1)} %copy.39), channel_id=1, replica_groups=mesh['rep'=16,'exp'=8] {'exp'}, dimensions={1}, use_global_device_ids=true | all-gather | bytes 138240 | tf_op jit(solution)/shard_map/all_gather | solution.py:56
  36.2 0.1 copy.42
  36.4 0.1 broadcast_in_dim.89
  36.6 0.1 copy.41
  36.7 0.1 convert_element_type.109
  36.8 1.9 fusion.14
  39.3 0.1 copy.43
  39.5 0.1 convert_element_type.112
  39.6 0.5 fusion.7
  40.1 23.9 %all-gather.2.cloned.1.call-done = bf16[1024,4096]{1,0:T(8,128)(2,1)} async-done(((bf16[128,4096]{1,0:T(8,128)(2,1)}), bf16[1024,4096]{1,0:T(8,128)(2,1)}) %all-gather.2.cloned.1.call-update) | async-done | bytes 8388624 | tf_op jit(solution)/shard_map/all_gather | solution.py:55
  64.0 13.4 %add_convert_fusion = bf16[1280,4096]{1,0:T(8,128)(2,1)S(1)} fusion(bf16[1280,1024]{1,0:T(8,128)(2,1)S(1)} %fusion.7, bf16[1024,4096]{1,0:T(8,128)(2,1)} %all-gather.2.cloned.1.call-done, f32[]{:T(128)S(6)} %convert_element_type.116), kind=kOutput, calls=%fused_computation | convolution fusion | flops 10747904000 | bytes 21495812 | tf_op jit(solution)/shard_map/dot_general | solution.py:70
  77.5 122.3 %all_to_all.24 = bf16[16,80,4096]{2,1,0:T(8,128)(2,1)S(1)} all-to-all(bf16[16,80,4096]{2,1,0:T(8,128)(2,1)S(1)} %bitcast.53), channel_id=1, replica_groups=mesh['rep'=16,'exp'=8] {'rep'}, dimensions={0} | all-to-all | bytes 20971520 | tf_op jit(solution)/shard_map/all_to_all | solution.py:73
  199.8 12.4 %fusion.4 = f32[1280,768]{1,0:T(8,128)S(1)} fusion(bf16[1280,4096]{1,0:T(8,128)(2,1)S(1)} %bitcast.55, bf16[1,4096,768]{2,1,0:T(8,128)(2,1)} %param.15), kind=kOutput, calls=%fused_computation.7 | convolution fusion | flops 8053063680 | bytes 20709376 | tf_op jit(solution)/shard_map/dot_general | solution.py:8
  212.3 9.0 %fusion.11 = bf16[1280,768]{1,0:T(8,128)(2,1)S(1)} fusion(bf16[1280,4096]{1,0:T(8,128)(2,1)S(1)} %bitcast.56, bf16[1,4096,768]{2,1,0:T(8,128)(2,1)S(1)} %bitcast.61, f32[1280,768]{1,0:T(8,128)S(1)} %fusion.4), kind=kOutput, calls=%fused_computation.19 | convolution fusion | flops 8058961920 | bytes 22675456 | tf_op jit(solution)/shard_map/dot_general | solution.py:9
  221.3 11.7 %fusion = bf16[1280,4096]{1,0:T(8,128)(2,1)S(1)} fusion(bf16[1280,768]{1,0:T(8,128)(2,1)S(1)} %fusion.11, bf16[1,768,4096]{2,1,0:T(8,128)(2,1)} %param.17, bf16[]{:T(256)S(6)} %mul.65), kind=kOutput, calls=%fused_computation.2 | convolution fusion | flops 8063549440 | bytes 18743298 | tf_op jit(solution)/shard_map/dot_general | solution.py:11
  233.0 121.0 %all_to_all.25 = bf16[16,80,4096]{2,1,0:T(8,128)(2,1)S(1)} all-to-all(bf16[16,80,4096]{2,1,0:T(8,128)(2,1)S(1)} %bitcast.57), channel_id=1, replica_groups=mesh['rep'=16,'exp'=8] {'rep'}, dimensions={0} | all-to-all | bytes 20971520 | tf_op jit(solution)/shard_map/all_to_all | solution.py:76
  354.0 13.0 %convolution_convert_fusion.1 = bf16[1024,4096]{1,0:T(8,128)(2,1)} fusion(bf16[1280,4096]{1,0:T(8,128)(2,1)S(1)} %bitcast.54, bf16[1280]{0:T(1024)(128)(2,1)S(1)} %broadcast_in_dim.89, s32[1280]{0:T(1024)S(1)} %convert_element_type.109), kind=kOutput, calls=%fused_computation.3 | convolution fusion | flops 10744233984 | bytes 18882048 | tf_op jit(solution)/shard_map/dot_general | solution.py:77
  367.0 51.9 %reduce-scatter.2.cloned.1.call-done = bf16[128,4096]{1,0:T(8,128)(2,1)} async-done(((bf16[1024,4096]{1,0:T(8,128)(2,1)}), bf16[128,4096]{1,0:T(8,128)(2,1)}) %reduce-scatter.2.cloned.1.call-update) | async-done | bytes 1048592 | tf_op jit(solution)/shard_map/reduce_scatter | solution.py:78
  (37 shorter events, 1.3 us)
Async XLA Ops:
  6.5 57.5 %all-gather.2.cloned.1.call-start = ((), (), s32[]{:S(2)}) async-start(), calls=%async_computation.3 | async-start | bytes 9437184 | tf_op jit(solution)/shard_map/all_gather | solution.py:55
  10.6 408.4 %reduce-scatter.2.cloned.1.call-start = ((), (), s32[]{:S(2)}) async-start(), calls=%async_computation.4 | async-start | bytes 9437184 | tf_op jit(solution)/shard_map/reduce_scatter | solution.py:78
  77.5 134.8 %slice-start = ((s8[6291456]{0:T(1024)(128)(4,1)}), s8[2097152]{0:T(1024)(128)(4,1)S(1)}, s32[]{:S(2)}) async-start(s8[6291456]{0:T(1024)(128)(4,1)} %bitcast.60), calls=%async_computation.5 | async-start | bytes 4194304
  199.8 12.5 %slice-start.1 = ((s8[6291456]{0:T(1024)(128)(4,1)}), s8[4194304]{0:T(1024)(128)(4,1)S(1)}, s32[]{:S(2)}) async-start(s8[6291456]{0:T(1024)(128)(4,1)} %bitcast.60), calls=%async_computation.6 | async-start | bytes 8388608
Sparse Core Ops, SparseCore 0:
  10.7 53.2 all-gather.1
  367.2 51.7 reduce-scatter.1

commit v11 on v10

--- a/solution.py
+++ b/solution.py
@@ -5,8 +5,11 @@
 
 
 def run_expert(arrived, w_gate, w_up, w_down):
-    gate_val = jnp.dot(arrived, w_gate[0], preferred_element_type=jnp.float32)
-    up_val = jnp.dot(arrived, w_up[0], preferred_element_type=jnp.float32)
+    ffw = w_gate.shape[2]
+    both = jnp.concatenate([w_gate[0], w_up[0]], axis=1)
+    joint = jnp.dot(arrived, both, preferred_element_type=jnp.float32)
+    gate_val = joint[:, :ffw]
+    up_val = joint[:, ffw:]
     act = (jax.nn.silu(gate_val) * up_val).astype(jnp.bfloat16)
     return jnp.dot(act, w_down[0], preferred_element_type=jnp.float32).astype(jnp.bfloat16)
 

time: 429 us -> 430 us (level)
    dot_general x2 -> x1, matrix products: 21.4 us -> 21.4 us  [run_expert(): joint = jnp.dot(arrived, both, preferred_element_type=jnp.float32)]
where the time goes in v11:
time: 430 us; the launch traced here: 426 us
  blocking collectives  260 us (60%)
  waiting for transfers between devices  75.8 us (18%)
  matrix products  60.4 us (14%)
  between operations  14.9 us (3%)
  other arithmetic  11.5 us (3%)
    all_to_all x1, blocking collectives, shards(): lax.all_to_all(outgoing, 'rep', split_axis=0, concat_axis=0, tiled=True)  122 us
    all_to_all x1, blocking collectives, shards(): lax.all_to_all(results, 'rep', split_axis=0, concat_axis=0, tiled=True)  121 us
    reduce_scatter x1, waiting for transfers between devices, shards(): lax.psum_scatter(partial.astype(jnp.bfloat16), 'exp', scatter_dimension=0...  51.9 us
    all_gather x1, waiting for transfers between devices, shards(): group = lax.all_gather(normed, 'exp', axis=0, tiled=True)  23.9 us
    dot_general x1, matrix products, run_expert(): joint = jnp.dot(arrived, both, preferred_element_type=jnp.float32)  21.4 us
    all_gather x1, blocking collectives, shards(): lax.all_gather(table.reshape(n_rep, n_exp, cap, 3), 'exp', axis=1, tiled=...  16.6 us
    dot_general x1, matrix products, shards(): jnp.dot(choose, group, preferred_element_type=jnp.float32)  13.4 us
    dot_general x1, matrix products, shards(): partial = jnp.dot(mix, returned, preferred_element_type=jnp.float32)  13 us
  transfers between devices with their start and end apart: 2, of which 2 were waited for; matrix products, arithmetic and copies ran while one was open for 3% of the time, Pallas kernels for 0%

profile of v11, /device:TPU:50, one launch (start us, length us, event | category | flops | bytes accessed | tf_op | source)
XLA Modules:
  0.0 426.2 jit_solution(7225304409996998411)
XLA Ops:
  6.5 1.5 fusion.13
  8.1 2.5 fusion.15
  10.7 0.8 copy.34
  12.5 0.7 reduce_sum.73
  13.2 0.7 divide_multiply_fusion
  14.2 0.7 broadcast_in_dim.83
  15.1 0.3 fusion.20
  15.6 0.5 fusion.19
  16.2 1.2 select_reduce_fusion.2
  17.4 0.1 convert_element_type.106
  17.5 0.8 fusion.6
  18.3 0.1 convert_element_type.104
  18.5 0.7 select_reduce_fusion
  19.1 0.1 stack.8
  19.3 0.2 copy.39
  19.5 16.6 %all_gather.6 = f32[16,8,8,10,3]{0,2,4,3,1:T(8,128)S(1)} all-gather(f32[16,1,8,10,3]{0,2,4,3,1:T(8,128)S(1)} %copy.39), channel_id=1, replica_groups=mesh['rep'=16,'exp'=8] {'exp'}, dimensions={1}, use_global_device_ids=true | all-gather | bytes 138240 | tf_op jit(solution)/shard_map/all_gather | solution.py:59
  36.2 0.1 copy.42
  36.4 0.1 broadcast_in_dim.89
  36.6 0.1 copy.43
  36.7 0.1 convert_element_type.112
  36.8 0.1 copy.41
  37.0 0.1 convert_element_type.109
  37.1 1.9 fusion.9
  39.6 0.5 fusion.7
  40.1 23.9 %all-gather.2.cloned.1.call-done = bf16[1024,4096]{1,0:T(8,128)(2,1)} async-done(((bf16[128,4096]{1,0:T(8,128)(2,1)}), bf16[1024,4096]{1,0:T(8,128)(2,1)}) %all-gather.2.cloned.1.call-update) | async-done | bytes 8388624 | tf_op jit(solution)/shard_map/all_gather | solution.py:58
  64.0 13.4 %add_convert_fusion = bf16[1280,4096]{1,0:T(8,128)(2,1)S(1)} fusion(bf16[1280,1024]{1,0:T(8,128)(2,1)S(1)} %fusion.7, bf16[1024,4096]{1,0:T(8,128)(2,1)} %all-gather.2.cloned.1.call-done, f32[]{:T(128)S(6)} %convert_element_type.116), kind=kOutput, calls=%fused_computation | convolution fusion | flops 10747904000 | bytes 21495812 | tf_op jit(solution)/shard_map/dot_general | solution.py:73
  77.4 122.2 %all_to_all.24 = bf16[16,80,4096]{2,1,0:T(8,128)(2,1)S(1)} all-to-all(bf16[16,80,4096]{2,1,0:T(8,128)(2,1)S(1)} %bitcast.43), channel_id=1, replica_groups=mesh['rep'=16,'exp'=8] {'rep'}, dimensions={0} | all-to-all | bytes 20971520 | tf_op jit(solution)/shard_map/all_to_all | solution.py:76
  199.6 21.4 %fusion = f32[1280,1536]{1,0:T(8,128)} fusion(bf16[1280,4096]{1,0:T(8,128)(2,1)S(1)} %bitcast.46, bf16[4096,768]{1,0:T(8,128)(2,1)} %bitcast.49, bf16[4096,768]{1,0:T(8,128)(2,1)} %bitcast.50), kind=kOutput, calls=%fused_computation.2 | convolution fusion | flops 16131293184 | bytes 30932992 | tf_op jit(solution)/shard_map/dot_general | solution.py:10
  221.0 12.6 %fusion.4 = bf16[1280,4096]{1,0:T(8,128)(2,1)S(1)} fusion(bf16[1,768,4096]{2,1,0:T(8,128)(2,1)} %param.17, bf16[]{:T(256)S(6)} %mul.65, f32[1280,1536]{1,0:T(8,128)} %fusion), kind=kOutput, calls=%fused_computation.6 | convolution fusion | flops 8069447680 | bytes 24641538 | tf_op jit(solution)/shard_map/dot_general | solution.py:14
  233.6 120.8 %all_to_all.25 = bf16[16,80,4096]{2,1,0:T(8,128)(2,1)S(1)} all-to-all(bf16[16,80,4096]{2,1,0:T(8,128)(2,1)S(1)} %bitcast.45), channel_id=1, replica_groups=mesh['rep'=16,'exp'=8] {'rep'}, dimensions={0} | all-to-all | bytes 20971520 | tf_op jit(solution)/shard_map/all_to_all | solution.py:79
  354.4 13.0 %convolution_convert_fusion.1 = bf16[1024,4096]{1,0:T(8,128)(2,1)} fusion(bf16[1280,4096]{1,0:T(8,128)(2,1)S(1)} %bitcast.44, bf16[1280]{0:T(1024)(128)(2,1)S(1)} %broadcast_in_dim.89, s32[1280]{0:T(1024)S(1)} %convert_element_type.109), kind=kOutput, calls=%fused_computation.7 | convolution fusion | flops 10744233984 | bytes 18882048 | tf_op jit(solution)/shard_map/dot_general | solution.py:80
  367.4 51.9 %reduce-scatter.2.cloned.1.call-done = bf16[128,4096]{1,0:T(8,128)(2,1)} async-done(((bf16[1024,4096]{1,0:T(8,128)(2,1)}), bf16[128,4096]{1,0:T(8,128)(2,1)}) %reduce-scatter.2.cloned.1.call-update) | async-done | bytes 1048592 | tf_op jit(solution)/shard_map/reduce_scatter | solution.py:81
  (31 shorter events, 1.2 us)
Async XLA Ops:
  6.5 57.5 %all-gather.2.cloned.1.call-start = ((), (), s32[]{:S(2)}) async-start(), calls=%async_computation.3 | async-start | bytes 9437184 | tf_op jit(solution)/shard_map/all_gather | solution.py:58
  10.6 408.7 %reduce-scatter.2.cloned.1.call-start = ((), (), s32[]{:S(2)}) async-start(), calls=%async_computation.4 | async-start | bytes 9437184 | tf_op jit(solution)/shard_map/reduce_scatter | solution.py:81
Sparse Core Ops, SparseCore 0:
  10.7 53.2 all-gather.1
  367.5 51.7 reduce-scatter.1

commit v12 on v10

--- a/solution.py
+++ b/solution.py
@@ -49,10 +49,10 @@
         axis=1,
     )
 
+    group = lax.all_gather(hidden, "exp", axis=0, tiled=True)
     own = hidden.astype(jnp.float32)
-    own_scale = lax.rsqrt(jnp.mean(own * own, axis=1, keepdims=True) + 1e-06)
-    normed = (own * own_scale * norm_gain).astype(jnp.bfloat16)
-    group = lax.all_gather(normed, "exp", axis=0, tiled=True)
+    own_scale = lax.rsqrt(jnp.mean(own * own, axis=1) + 1e-06)
+    scale_all = lax.all_gather(own_scale, "exp", axis=0, tiled=True)
     table_all = lax.all_gather(table.reshape(n_rep, n_exp, cap, 3), "exp", axis=1, tiled=False)
     table_col = lax.dynamic_index_in_dim(table_all, column, axis=2, keepdims=False)
     row_tbl = table_col[..., 0].astype(jnp.int32)
@@ -67,7 +67,9 @@
     w_key = table_col[..., 2].reshape(-1)
     pick = jnp.arange(micro, dtype=jnp.int32)[:, None] == key[None, :]
     mix = jnp.where(pick, w_key[None, :], 0.0).astype(jnp.bfloat16)
-    outgoing = jnp.dot(choose, group, preferred_element_type=jnp.float32) + jnp.sum(mix) * 0
+    scale_sel = jnp.take(scale_all, jnp.maximum(src_key, 0))
+    picked = jnp.dot(choose, group, preferred_element_type=jnp.float32)
+    outgoing = picked * scale_sel[:, None] * norm_gain + jnp.sum(mix) * 0
     outgoing = outgoing.astype(jnp.bfloat16)
 
     arrived = lax.all_to_all(outgoing, "rep", split_axis=0, concat_axis=0, tiled=True)

time: 429 us -> 427 us (level)
  waiting for transfers between devices: 75.8 us -> 63.8 us
  blocking collectives: 260 us -> 268 us
  local copies, waits for them, and re-layouts: 3.95 us -> 9.18 us
    all_gather x1, waiting for transfers between devices: 23.9 us -> 10.9 us  [shards(): group = lax.all_gather(hidden, 'exp', axis=0, tiled=True)]
    all_gather x0 -> x1, blocking collectives: none -> 8.27 us  [shards(): scale_all = lax.all_gather(own_scale, 'exp', axis=0, tiled=True)]
    gather x0 -> x1, local copies, waits for them, and re-layouts: none -> 4.97 us  [shards(): scale_sel = jnp.take(scale_all, jnp.maximum(src_key, 0))]
  transfers between devices with their start and end apart: 2 -> 2, of which waited for: 2 -> 2; matrix products, arithmetic and copies ran while one was open for 3% -> 4% of each run, Pallas kernels for 0% -> 0%
where the time goes in v12:
time: 427 us; the launch traced here: 424 us
  blocking collectives  268 us (63%)
  waiting for transfers between devices  63.8 us (15%)
  matrix products  60.1 us (14%)
  between operations  15 us (4%)
  local copies, waits for them, and re-layouts  9.18 us (2%)
  other arithmetic  7.8 us (2%)
    all_to_all x1, blocking collectives, shards(): lax.all_to_all(outgoing, 'rep', split_axis=0, concat_axis=0, tiled=True)  122 us
    all_to_all x1, blocking collectives, shards(): lax.all_to_all(results, 'rep', split_axis=0, concat_axis=0, tiled=True)  121 us
    reduce_scatter x1, waiting for transfers between devices, shards(): lax.psum_scatter(partial.astype(jnp.bfloat16), 'exp', scatter_dimension=0...  52.2 us
    all_gather x1, blocking collectives, shards(): lax.all_gather(table.reshape(n_rep, n_exp, cap, 3), 'exp', axis=1, tiled=...  16.4 us
    dot_general x1, matrix products, shards(): picked = jnp.dot(choose, group, preferred_element_type=jnp.float32)  13.7 us
    dot_general x1, matrix products, shards(): partial = jnp.dot(mix, returned, preferred_element_type=jnp.float32)  13 us
    dot_general x1, matrix products, run_expert(): gate_val = jnp.dot(arrived, w_gate[0], preferred_element_type=jnp.float32)  12.5 us
    dot_general x1, matrix products, run_expert(): jnp.dot(act, w_down[0], preferred_element_type=jnp.float32)  11 us
  transfers between devices with their start and end apart: 2, of which 2 were waited for; matrix products, arithmetic and copies ran while one was open for 4% of the time, Pallas kernels for 0%

profile of v12, /device:TPU:50, one launch (start us, length us, event | category | flops | bytes accessed | tf_op | source)
XLA Modules:
  0.0 423.9 jit_solution(2725431339173172228)
XLA Ops:
  6.5 0.7 all-gather.3.cloned.1.call-update
  7.3 0.8 copy.36
  9.1 0.7 reduce_sum.73
  9.8 0.7 divide_multiply_fusion
  10.8 0.7 broadcast_in_dim.91
  11.7 0.3 fusion.20
  12.3 0.5 fusion.19
  12.8 1.2 select_reduce_fusion.2
  14.2 0.8 fusion.6
  15.1 0.7 select_reduce_fusion
  15.9 0.2 copy.41
  16.1 16.4 %all_gather.9 = f32[16,8,8,10,3]{0,2,4,3,1:T(8,128)S(1)} all-gather(f32[16,1,8,10,3]{0,2,4,3,1:T(8,128)S(1)} %copy.41), channel_id=1, replica_groups=mesh['rep'=16,'exp'=8] {'exp'}, dimensions={1}, use_global_device_ids=true | all-gather | bytes 138240 | tf_op jit(solution)/shard_map/all_gather | solution.py:56
  32.7 0.1 copy.44
  32.8 0.1 broadcast_in_dim.97
  33.0 0.1 copy.43
  33.1 0.1 convert_element_type.130
  33.3 1.9 fusion.14
  36.0 0.1 reshape.196
  36.3 0.1 convert_element_type.133
  36.4 0.3 multiply_reduce_fusion
  36.7 8.3 %all-gather = f32[8,1,128]{2,1,0:T(1,128)S(1)} all-gather(f32[1,1,128]{2,1,0:T(1,128)S(1)} %rsqrt_bitcast_fusion), channel_id=1, replica_groups=mesh['rep'=16,'exp'=8] {'exp'}, dimensions={0}, use_global_device_ids=true | all-gather | bytes 4608 | tf_op jit(solution)/shard_map/all_gather | solution.py:55
  45.0 5.0 %gather_fusion = f32[1280]{0:T(1024)S(1)} fusion(f32[1024]{0:T(1024)S(1)} %bitcast.60, s32[2048]{0:T(1024)S(1)} %pad_clamp_fusion), kind=kCustom, calls=%fused_computation | custom fusion | bytes 15360 | tf_op jit(solution)/shard_map/jit(_take)/gather | solution.py:70
  50.0 0.5 fusion.7
  50.5 10.9 %all-gather.3.cloned.1.call-done = bf16[1024,4096]{1,0:T(8,128)(2,1)} async-done(((bf16[128,4096]{1,0:T(8,128)(2,1)}), bf16[1024,4096]{1,0:T(8,128)(2,1)}) %all-gather.3.cloned.1.call-update) | async-done | bytes 8388624 | tf_op jit(solution)/shard_map/all_gather | solution.py:52
  61.4 13.7 %add_convert_fusion = bf16[1280,4096]{1,0:T(8,128)(2,1)S(1)} fusion(bf16[1280,1024]{1,0:T(8,128)(2,1)S(1)} %fusion.7, bf16[1024,4096]{1,0:T(8,128)(2,1)} %all-gather.3.cloned.1.call-done, f32[]{:T(128)S(6)} %convert_element_type.136, f32[4096]{0:T(1024)S(1)} %copy-done.1, f32[1280]{0:T(1024)S(1)} %get-tuple-element.7), kind=kOutput, calls=%fused_computation.1 | convolution fusion | flops 10758389760 | bytes 21517316 | tf_op jit(solution)/shard_map/dot_general | solution.py:71
  75.2 122.5 %all_to_all.24 = bf16[16,80,4096]{2,1,0:T(8,128)(2,1)S(1)} all-to-all(bf16[16,80,4096]{2,1,0:T(8,128)(2,1)S(1)} %bitcast.61), channel_id=1, replica_groups=mesh['rep'=16,'exp'=8] {'rep'}, dimensions={0} | all-to-all | bytes 20971520 | tf_op jit(solution)/shard_map/all_to_all | solution.py:75
  197.6 12.5 %fusion.4 = f32[1280,768]{1,0:T(8,128)S(1)} fusion(bf16[1280,4096]{1,0:T(8,128)(2,1)S(1)} %bitcast.63, bf16[1,4096,768]{2,1,0:T(8,128)(2,1)} %param.15), kind=kOutput, calls=%fused_computation.8 | convolution fusion | flops 8053063680 | bytes 20709376 | tf_op jit(solution)/shard_map/dot_general | solution.py:8
  210.2 9.8 %fusion.11 = bf16[1280,768]{1,0:T(8,128)(2,1)} fusion(bf16[1280,4096]{1,0:T(8,128)(2,1)S(1)} %bitcast.64, bf16[1,4096,768]{2,1,0:T(8,128)(2,1)S(1)} %bitcast.70, f32[1280,768]{1,0:T(8,128)S(1)} %fusion.4), kind=kOutput, calls=%fused_computation.20 | convolution fusion | flops 8058961920 | bytes 22675456 | tf_op jit(solution)/shard_map/dot_general | solution.py:9
  220.0 11.0 %fusion = bf16[1280,4096]{1,0:T(8,128)(2,1)S(1)} fusion(bf16[1280,768]{1,0:T(8,128)(2,1)} %fusion.11, bf16[1,768,4096]{2,1,0:T(8,128)(2,1)} %param.17, bf16[]{:T(256)S(6)} %mul.65), kind=kOutput, calls=%fused_computation.3 | convolution fusion | flops 8063549440 | bytes 18743298 | tf_op jit(solution)/shard_map/dot_general | solution.py:11
  231.1 120.8 %all_to_all.25 = bf16[16,80,4096]{2,1,0:T(8,128)(2,1)S(1)} all-to-all(bf16[16,80,4096]{2,1,0:T(8,128)(2,1)S(1)} %bitcast.65), channel_id=1, replica_groups=mesh['rep'=16,'exp'=8] {'rep'}, dimensions={0} | all-to-all | bytes 20971520 | tf_op jit(solution)/shard_map/all_to_all | solution.py:78
  351.8 13.0 %convolution_convert_fusion.1 = bf16[1024,4096]{1,0:T(8,128)(2,1)} fusion(bf16[1280,4096]{1,0:T(8,128)(2,1)S(1)} %bitcast.62, bf16[1280]{0:T(1024)(128)(2,1)S(1)} %broadcast_in_dim.97, s32[1280]{0:T(1024)S(1)} %convert_element_type.130), kind=kOutput, calls=%fused_computation.4 | convolution fusion | flops 10744233984 | bytes 18882048 | tf_op jit(solution)/shard_map/dot_general | solution.py:79
  364.9 52.2 %reduce-scatter.2.cloned.1.call-done = bf16[128,4096]{1,0:T(8,128)(2,1)} async-done(((bf16[1024,4096]{1,0:T(8,128)(2,1)}), bf16[128,4096]{1,0:T(8,128)(2,1)}) %reduce-scatter.2.cloned.1.call-update) | async-done | bytes 1048592 | tf_op jit(solution)/shard_map/reduce_scatter | solution.py:80
  (46 shorter events, 1.9 us)
Async XLA Ops:
  6.5 29.9 %copy-start = (bf16[128,4096]{1,0:T(8,128)(2,1)S(1)}, bf16[128,4096]{1,0:T(8,128)(2,1)}, u32[]{:S(2)}) copy-start(bf16[128,4096]{1,0:T(8,128)(2,1)} %param.9) | copy-start | bytes 3145732
  6.5 54.9 %all-gather.3.cloned.1.call-start = ((), (), s32[]{:S(2)}) async-start(), calls=%async_computation.3 | async-start | bytes 9437184 | tf_op jit(solution)/shard_map/all_gather | solution.py:52
  7.3 409.8 %reduce-scatter.2.cloned.1.call-start = ((), (), s32[]{:S(2)}) async-start(), calls=%async_computation.4 | async-start | bytes 9437184 | tf_op jit(solution)/shard_map/reduce_scatter | solution.py:80
  45.0 16.4 %copy-start.1 = (f32[4096]{0:T(1024)S(1)}, f32[4096]{0:T(1024)}, u32[]{:S(2)}) copy-start(f32[4096]{0:T(1024)} %param.14) | copy-start | bytes 49156
  75.1 135.0 %slice-start = ((s8[6291456]{0:T(1024)(128)(4,1)}), s8[4194304]{0:T(1024)(128)(4,1)S(1)}, s32[]{:S(2)}) async-start(s8[6291456]{0:T(1024)(128)(4,1)} %bitcast.69), calls=%async_computation.5 | async-start | bytes 8388608
  197.6 12.5 %slice-start.1 = ((s8[6291456]{0:T(1024)(128)(4,1)}), s8[2097152]{0:T(1024)(128)(4,1)S(1)}, s32[]{:S(2)}) async-start(s8[6291456]{0:T(1024)(128)(4,1)} %bitcast.69), calls=%async_computation.6 | async-start | bytes 4194304
Sparse Core Ops, SparseCore 0:
  9.1 52.2 all-gather.2
  365.0 52.0 reduce-scatter.1

commit v13 on v12

--- a/solution.py
+++ b/solution.py
@@ -40,20 +40,20 @@
     row_here = jnp.sum(jnp.where(match, slot_row[:, None], 0), axis=0)
     parent_here = jnp.sum(jnp.where(match, jnp.repeat(parents, top)[:, None], 0), axis=0)
     w_here = jnp.sum(jnp.where(match, weights.reshape(-1)[:, None], 0.0), axis=0)
+    group = lax.all_gather(hidden, "exp", axis=0, tiled=True)
+    own = hidden.astype(jnp.float32)
+    own_scale = lax.rsqrt(jnp.mean(own * own, axis=1) + 1e-06)
     table = jnp.stack(
         [
             jnp.where(filled_here, column * rows + row_here, -1).astype(jnp.float32),
             parent_here.astype(jnp.float32),
             w_here,
+            jnp.pad(own_scale, (0, n_dev * cap - rows)),
         ],
         axis=1,
     )
-
-    group = lax.all_gather(hidden, "exp", axis=0, tiled=True)
-    own = hidden.astype(jnp.float32)
-    own_scale = lax.rsqrt(jnp.mean(own * own, axis=1) + 1e-06)
-    scale_all = lax.all_gather(own_scale, "exp", axis=0, tiled=True)
-    table_all = lax.all_gather(table.reshape(n_rep, n_exp, cap, 3), "exp", axis=1, tiled=False)
+    table_all = lax.all_gather(table.reshape(n_rep, n_exp, cap, 4), "exp", axis=1, tiled=False)
+    scale_all = jnp.transpose(table_all[..., 3], (1, 0, 2, 3)).reshape(n_exp, -1)[:, :rows].reshape(-1)
     table_col = lax.dynamic_index_in_dim(table_all, column, axis=2, keepdims=False)
     row_tbl = table_col[..., 0].astype(jnp.int32)
     src_row = table_col[..., 1].astype(jnp.int32).reshape(-1)

time: 427 us -> 429 us (level)
  waiting for transfers between devices: 63.8 us -> 69.9 us
  blocking collectives: 268 us -> 262 us
    all_gather x2 -> x1, blocking collectives: 24.7 us -> 18.2 us  [shards(): lax.all_gather(table.reshape(n_rep, n_exp, cap, 4), 'exp', axis=1, tiled=...]
    all_gather x1, waiting for transfers between devices: 10.9 us -> 17.3 us  [shards(): group = lax.all_gather(hidden, 'exp', axis=0, tiled=True)]
  transfers between devices with their start and end apart: 2 -> 2, of which waited for: 2 -> 2; matrix products, arithmetic and copies ran while one was open for 4% -> 5% of each run, Pallas kernels for 0% -> 0%
where the time goes in v13:
time: 429 us; the launch traced here: 426 us
  blocking collectives  262 us (61%)
  waiting for transfers between devices  69.9 us (16%)
  matrix products  59.9 us (14%)
  between operations  15.1 us (4%)
  local copies, waits for them, and re-layouts  10.3 us (2%)
  other arithmetic  9.04 us (2%)
    all_to_all x1, blocking collectives, shards(): lax.all_to_all(outgoing, 'rep', split_axis=0, concat_axis=0, tiled=True)  122 us
    all_to_all x1, blocking collectives, shards(): lax.all_to_all(results, 'rep', split_axis=0, concat_axis=0, tiled=True)  121 us
    reduce_scatter x1, waiting for transfers between devices, shards(): lax.psum_scatter(partial.astype(jnp.bfloat16), 'exp', scatter_dimension=0...  51.9 us
    all_gather x1, blocking collectives, shards(): lax.all_gather(table.reshape(n_rep, n_exp, cap, 4), 'exp', axis=1, tiled=...  18.2 us
    all_gather x1, waiting for transfers between devices, shards(): group = lax.all_gather(hidden, 'exp', axis=0, tiled=True)  17.3 us
    dot_general x1, matrix products, shards(): picked = jnp.dot(choose, group, preferred_element_type=jnp.float32)  13.8 us
    dot_general x1, matrix products, shards(): partial = jnp.dot(mix, returned, preferred_element_type=jnp.float32)  13 us
    dot_general x1, matrix products, run_expert(): gate_val = jnp.dot(arrived, w_gate[0], preferred_element_type=jnp.float32)  12.4 us
  transfers between devices with their start and end apart: 2, of which 2 were waited for; matrix products, arithmetic and copies ran while one was open for 5% of the time, Pallas kernels for 0%

profile of v13, /device:TPU:50, one launch (start us, length us, event | category | flops | bytes accessed | tf_op | source)
XLA Modules:
  0.0 425.8 jit_solution(6997573053714149328)
XLA Ops:
  6.5 0.7 all-gather.2.cloned.1.call-update
  7.3 0.8 copy.41
  8.9 0.7 reduce_sum.73
  9.6 1.5 multiply_reduce_fusion
  11.5 0.7 divide_multiply_fusion
  12.5 0.7 broadcast_in_dim.91
  13.4 0.3 fusion.20
  13.9 0.5 fusion.19
  14.5 1.2 select_reduce_fusion.2
  15.9 0.8 fusion.6
  16.8 0.7 select_reduce_fusion
  17.6 0.3 copy.46
  17.9 18.2 %all_gather.6 = f32[16,8,8,10,4]{0,2,4,3,1:T(8,128)S(1)} all-gather(f32[16,1,8,10,4]{0,2,4,3,1:T(8,128)S(1)} %copy.46), channel_id=1, replica_groups=mesh['rep'=16,'exp'=8] {'exp'}, dimensions={1}, use_global_device_ids=true | all-gather | bytes 184320 | tf_op jit(solution)/shard_map/all_gather | solution.py:55
  36.1 0.1 constant_dynamic-slice_fusion
  36.3 0.1 copy.49
  36.4 0.1 broadcast_in_dim.97
  36.7 0.1 convert_element_type.133
  36.9 1.9 fusion.14
  39.6 0.1 reshape.206
  40.1 0.5 copy.51
  40.6 0.3 reshape.202
  40.9 5.0 %gather_fusion = f32[1280]{0:T(1024)S(1)} fusion(f32[1024]{0:T(1024)S(1)} %slice_bitcast_fusion.1, s32[2048]{0:T(1024)S(1)} %pad_clamp_fusion), kind=kCustom, calls=%fused_computation | custom fusion | bytes 15360 | tf_op jit(solution)/shard_map/jit(_take)/gather | solution.py:70
  45.9 0.5 fusion.7
  46.4 17.3 %all-gather.2.cloned.1.call-done = bf16[1024,4096]{1,0:T(8,128)(2,1)} async-done(((bf16[128,4096]{1,0:T(8,128)(2,1)}), bf16[1024,4096]{1,0:T(8,128)(2,1)}) %all-gather.2.cloned.1.call-update) | async-done | bytes 8388624 | tf_op jit(solution)/shard_map/all_gather | solution.py:43
  63.7 13.8 %add_convert_fusion = bf16[1280,4096]{1,0:T(8,128)(2,1)S(1)} fusion(bf16[1280,1024]{1,0:T(8,128)(2,1)S(1)} %fusion.7, bf16[1024,4096]{1,0:T(8,128)(2,1)} %all-gather.2.cloned.1.call-done, f32[]{:T(128)S(6)} %convert_element_type.138, f32[4096]{0:T(1024)S(1)} %copy-done, f32[1280]{0:T(1024)S(1)} %get-tuple-element.7), kind=kOutput, calls=%fused_computation.1 | convolution fusion | flops 10758389760 | bytes 21517316 | tf_op jit(solution)/shard_map/dot_general | solution.py:71
  77.4 122.3 %all_to_all.24 = bf16[16,80,4096]{2,1,0:T(8,128)(2,1)S(1)} all-to-all(bf16[16,80,4096]{2,1,0:T(8,128)(2,1)S(1)} %bitcast.65), channel_id=1, replica_groups=mesh['rep'=16,'exp'=8] {'rep'}, dimensions={0} | all-to-all | bytes 20971520 | tf_op jit(solution)/shard_map/all_to_all | solution.py:75
  199.8 12.4 %fusion.4 = f32[1280,768]{1,0:T(8,128)S(1)} fusion(bf16[1280,4096]{1,0:T(8,128)(2,1)S(1)} %bitcast.67, bf16[1,4096,768]{2,1,0:T(8,128)(2,1)} %param.15), kind=kOutput, calls=%fused_computation.8 | convolution fusion | flops 8053063680 | bytes 20709376 | tf_op jit(solution)/shard_map/dot_general | solution.py:8
  212.3 9.0 %fusion.11 = bf16[1280,768]{1,0:T(8,128)(2,1)S(1)} fusion(bf16[1280,4096]{1,0:T(8,128)(2,1)S(1)} %bitcast.68, bf16[1,4096,768]{2,1,0:T(8,128)(2,1)S(1)} %bitcast.74, f32[1280,768]{1,0:T(8,128)S(1)} %fusion.4), kind=kOutput, calls=%fused_computation.20 | convolution fusion | flops 8058961920 | bytes 22675456 | tf_op jit(solution)/shard_map/dot_general | solution.py:9
  221.3 11.7 %fusion = bf16[1280,4096]{1,0:T(8,128)(2,1)S(1)} fusion(bf16[1280,768]{1,0:T(8,128)(2,1)S(1)} %fusion.11, bf16[1,768,4096]{2,1,0:T(8,128)(2,1)} %param.17, bf16[]{:T(256)S(6)} %mul.65), kind=kOutput, calls=%fused_computation.3 | convolution fusion | flops 8063549440 | bytes 18743298 | tf_op jit(solution)/shard_map/dot_general | solution.py:11
  233.0 121.0 %all_to_all.25 = bf16[16,80,4096]{2,1,0:T(8,128)(2,1)S(1)} all-to-all(bf16[16,80,4096]{2,1,0:T(8,128)(2,1)S(1)} %bitcast.69), channel_id=1, replica_groups=mesh['rep'=16,'exp'=8] {'rep'}, dimensions={0} | all-to-all | bytes 20971520 | tf_op jit(solution)/shard_map/all_to_all | solution.py:78
  354.0 13.0 %convolution_convert_fusion.1 = bf16[1024,4096]{1,0:T(8,128)(2,1)} fusion(bf16[1280,4096]{1,0:T(8,128)(2,1)S(1)} %bitcast.66, bf16[1280]{0:T(1024)(128)(2,1)S(1)} %broadcast_in_dim.97, s32[1280]{0:T(1024)S(1)} %convert_element_type.133), kind=kOutput, calls=%fused_computation.4 | convolution fusion | flops 10744233984 | bytes 18882048 | tf_op jit(solution)/shard_map/dot_general | solution.py:79
  367.1 51.9 %reduce-scatter.2.cloned.1.call-done = bf16[128,4096]{1,0:T(8,128)(2,1)} async-done(((bf16[1024,4096]{1,0:T(8,128)(2,1)}), bf16[128,4096]{1,0:T(8,128)(2,1)}) %reduce-scatter.2.cloned.1.call-update) | async-done | bytes 1048592 | tf_op jit(solution)/shard_map/reduce_scatter | solution.py:80
  (49 shorter events, 2.3 us)
Async XLA Ops:
  6.5 57.1 %all-gather.2.cloned.1.call-start = ((), (), s32[]{:S(2)}) async-start(), calls=%async_computation.3 | async-start | bytes 9437184 | tf_op jit(solution)/shard_map/all_gather | solution.py:43
  7.3 411.7 %reduce-scatter.2.cloned.1.call-start = ((), (), s32[]{:S(2)}) async-start(), calls=%async_computation.4 | async-start | bytes 9437184 | tf_op jit(solution)/shard_map/reduce_scatter | solution.py:80
  40.9 22.8 %copy-start = (f32[4096]{0:T(1024)S(1)}, f32[4096]{0:T(1024)}, u32[]{:S(2)}) copy-start(f32[4096]{0:T(1024)} %param.14) | copy-start | bytes 49156
  77.4 134.8 %slice-start = ((s8[6291456]{0:T(1024)(128)(4,1)}), s8[2097152]{0:T(1024)(128)(4,1)S(1)}, s32[]{:S(2)}) async-start(s8[6291456]{0:T(1024)(128)(4,1)} %bitcast.73), calls=%async_computation.5 | async-start | bytes 4194304
  199.8 12.5 %slice-start.1 = ((s8[6291456]{0:T(1024)(128)(4,1)}), s8[4194304]{0:T(1024)(128)(4,1)S(1)}, s32[]{:S(2)}) async-start(s8[6291456]{0:T(1024)(128)(4,1)} %bitcast.73), calls=%async_computation.6 | async-start | bytes 8388608
Sparse Core Ops, SparseCore 0:
  9.1 54.5 all-gather.1
  367.2 51.7 reduce-scatter.1
